TPU v7x, 32 devices: a whole 2x2x4 slice. The times are simulated.
32 devices in a mesh: expert: 8 (over z, core), hid: 4 (over y, x).
Axes of the slice: x: 2, y: 2, z: 4, core: 2. Of those that a mesh axis runs over, the one named last changes fastest.
Arguments:
- tokens: bfloat16 [64, 3584], P('expert', 'hid'), may hold values from -6 to 6
- cotangent: bfloat16 [64, 3584], P('expert', 'hid'), may hold values from -6 to 6
- gate_prob: float32 [64, 8], P('expert'), may hold values from 0.1 to 1
- routes: int32 [64, 8], P('expert'), may hold values from 0 to 7, as said below
- slots: int32 [64, 8], P('expert'), may hold values from 0 to 8, as said below
- drop_seed: int32 [1], replicated, may hold values from 0 to 16777215
- layer_id: int32 [1], replicated, may hold values from 0 to 63
- w_gate: bfloat16 [8, 2560, 3584], P('expert', 'hid'), may hold values from -0.09375 to 0.09375
- w_up: bfloat16 [8, 2560, 3584], P('expert', 'hid'), may hold values from -0.09375 to 0.09375
- w_down: bfloat16 [8, 2560, 3584], P('expert', 'hid'), may hold values from -0.125 to 0.125
Outputs:
- grad_tokens: bfloat16 [64, 3584], P('expert', 'hid')
- grad_gate: bfloat16 [8, 2560, 3584], P('expert', 'hid')
- grad_up: bfloat16 [8, 2560, 3584], P('expert', 'hid')
- grad_down: bfloat16 [8, 2560, 3584], P('expert', 'hid')
Inputs may be any that keep to these rules, and one draw needn't show every extreme that they name: `routes`: each row names 8 different experts; one expert, drawn from the seed, is named by every token. Within one token group, the choices of each expert, taken in a priority order drawn from the seed, get slots 0, 1, 2 and so on, each slot at most once; those past 8 - 1 get the drop marker 8.
All inputs are finite; a program needn't handle non-finite values.
Results may differ from a plain program's by a relative error of at most 0.012.
Values may be sent and summed in bfloat16 or wider, within the bound.
No kernel may reach another device: no remote copies, remote signals or barrier semaphores. Data moves between devices by JAX's collectives and lax.ppermute only.
A program may use at most 64 MiB of HBM per device.

v0:
```python
import jax
import jax.numpy as jnp
from jax import lax
from jax.sharding import PartitionSpec as P

FF = 2560
CAP_SRC = 8


KEEP_FACTOR = 1024.0 / 922.0


def logical_shift(values, amount):
    return jnp.right_shift(values, amount) & (1 << 32 - amount) - 1


def keep_mask(counter, seed_value, layer_value):
    mixed = counter * -1640531535 + seed_value * 40503 + layer_value * 97
    mixed = mixed ^ logical_shift(mixed, 15)
    mixed = mixed * -2048144789
    mixed = mixed ^ logical_shift(mixed, 13)
    mixed = mixed * -1028477387
    mixed = mixed ^ logical_shift(mixed, 16)
    levels = logical_shift(mixed, 8) & 1023
    return jnp.where(levels >= 102, KEEP_FACTOR, 0.0).astype(jnp.float32)


def contract_rows(left, right):
    return lax.dot_general(
        left, right, (((0,), (0,)), ((), ())), preferred_element_type=jnp.float32
    )


def contract_cols(left, right):
    return lax.dot_general(
        left, right, (((1,), (1,)), ((), ())), preferred_element_type=jnp.float32
    )


def on_device(
    tokens, cotangent, gate_prob, routes, slots, drop_seed, layer_id, w_gate, w_up, w_down
):
    experts = lax.axis_size("expert")
    part_width = tokens.shape[1]
    capacity = experts * CAP_SRC
    local_units = w_gate.shape[1]
    target = jnp.where(slots < CAP_SRC, routes * CAP_SRC + slots, -1)
    slot_ids = jnp.arange(experts * CAP_SRC, dtype=jnp.int32)
    matches = target[None, :, :] == slot_ids[:, None, None]
    placed = jnp.any(matches, axis=2).astype(jnp.bfloat16)
    slot_gate = jnp.sum(jnp.where(matches, gate_prob[None, :, :], 0.0), axis=(1, 2))
    sent_x = jnp.dot(placed, tokens, preferred_element_type=jnp.float32).astype(jnp.bfloat16)
    plain_dy = jnp.dot(placed, cotangent, preferred_element_type=jnp.float32)
    sent_dy = (slot_gate[:, None] * plain_dy).astype(jnp.bfloat16)
    send_shape = (experts, CAP_SRC * part_width)
    recv_x, recv_dy = (
        lax.all_to_all(
            sent_x.reshape(send_shape), "expert", split_axis=0, concat_axis=0, tiled=True
        ),
        lax.all_to_all(
            sent_dy.reshape(send_shape), "expert", split_axis=0, concat_axis=0, tiled=True
        ),
    )
    rows_x, rows_dy = (
        lax.all_gather(recv_x.reshape(capacity, part_width), "hid", axis=1, tiled=True),
        lax.all_gather(recv_dy.reshape(capacity, part_width), "hid", axis=1, tiled=True),
    )
    gate_w = w_gate[0]
    up_w = w_up[0]
    down_w = w_down[0]
    gate_pre = contract_cols(rows_x, gate_w)
    up_pre = contract_cols(rows_x, up_w)
    expert_id = lax.axis_index("expert")
    unit_ids = lax.axis_index("hid") * local_units + jnp.arange(local_units, dtype=jnp.int32)
    row_ids = jnp.arange(capacity, dtype=jnp.int32)
    counter = (expert_id * capacity + row_ids[:, None]) * FF + unit_ids[None, :]
    keep_mul = keep_mask(counter, drop_seed[0], layer_id[0])
    logistic = jax.nn.sigmoid(gate_pre)
    swish = gate_pre * logistic
    hidden = (swish * up_pre * keep_mul).astype(jnp.bfloat16)
    grad_hidden = contract_cols(rows_dy, down_w) * keep_mul
    grad_upre = (grad_hidden * swish).astype(jnp.bfloat16)
    grad_gpre = (grad_hidden * up_pre * logistic * (1.0 + gate_pre * (1.0 - logistic))).astype(
        jnp.bfloat16
    )
    grad_down = contract_rows(hidden, rows_dy).astype(jnp.bfloat16)
    grad_gate = contract_rows(grad_gpre, rows_x).astype(jnp.bfloat16)
    grad_up = contract_rows(grad_upre, rows_x).astype(jnp.bfloat16)
    partial_sum = jnp.dot(grad_gpre, gate_w, preferred_element_type=jnp.float32) + jnp.dot(
        grad_upre, up_w, preferred_element_type=jnp.float32
    )
    summed = lax.psum(partial_sum.astype(jnp.bfloat16), "hid").astype(jnp.float32)
    own_cols = lax.dynamic_slice_in_dim(summed, lax.axis_index("hid") * part_width, part_width, 1)
    back_rows = lax.all_to_all(
        own_cols.astype(jnp.bfloat16).reshape(send_shape),
        "expert",
        split_axis=0,
        concat_axis=0,
        tiled=True,
    )
    grad_tokens = contract_rows(placed, back_rows.reshape(experts * CAP_SRC, part_width)).astype(
        jnp.bfloat16
    )
    return (grad_tokens, grad_gate[None], grad_up[None], grad_down[None])


def solution(mesh):
    in_specs = (
        P("expert", "hid"),
        P("expert", "hid"),
        P("expert", None),
        P("expert", None),
        P("expert", None),
        P(),
        P(),
        P("expert", "hid", None),
        P("expert", "hid", None),
        P("expert", "hid", None),
    )
    out_specs = (
        P("expert", "hid"),
        P("expert", "hid", None),
        P("expert", "hid", None),
        P("expert", "hid", None),
    )
    return jax.shard_map(
        on_device, mesh=mesh, in_specs=in_specs, out_specs=out_specs, check_vma=False
    )
```

profile of v0, /device:TPU:0, one launch (start us, length us, event | category | flops | bytes accessed | tf_op | source)
XLA Modules:
  0.0 131.3 jit_solution(13579242598336714023)
XLA Ops:
  7.2 0.7 add_select_fusion
  8.0 0.8 select_reduce_fusion
  9.6 1.3 reduce.4
  11.6 6.3 %all-to-all-start = ((bf16[8,2,3584]{2,1,0:T(2,128)(2,1)}), bf16[8,2,3584]{2,1,0:T(2,128)(2,1)S(1)}, u32[]{:S(2)}, u32[]{:S(2)}) async-start(bf16[8,2,3584]{2,1,0:T(2,128)(2,1)} %reshape.58), calls=%async_computation | async-start | bytes 229376 | tf_op jit(solution)/shard_map/all_to_all | solution.py:60
  19.2 0.9 convolution_convert_fusion.3
  20.2 1.3 %reduce.3 = bf16[8,7168]{1,0:T(8,128)(2,1)S(1)} reduce(bf16[8,1,7168]{2,1,0:T(2,128)(2,1)S(1)} %all_to_all.25, bf16[]{:T(256)} %broadcast.36), dimensions={1}, to_apply=%all_to_all.25.reduce_sub_computation | reduce | bytes 229378 | tf_op jit(solution)/shard_map/all_to_all | solution.py:57
  22.3 2.2 %all-to-all-done = bf16[8,2,3584]{2,1,0:T(2,128)(2,1)S(1)} async-done(((bf16[8,2,3584]{2,1,0:T(2,128)(2,1)}), bf16[8,2,3584]{2,1,0:T(2,128)(2,1)S(1)}, u32[]{:S(2)}, u32[]{:S(2)}) %all-to-all-start) | async-done | bytes 114720 | tf_op jit(solution)/shard_map/all_to_all | solution.py:60
  24.5 3.4 %all-to-all-start.1 = ((bf16[8,2,3584]{2,1,0:T(2,128)(2,1)}), bf16[8,2,3584]{2,1,0:T(2,128)(2,1)S(1)}, u32[]{:S(2)}, u32[]{:S(2)}) async-start(bf16[8,2,3584]{2,1,0:T(2,128)(2,1)} %reshape.56), calls=%async_computation.1 | async-start | bytes 229376 | tf_op jit(solution)/shard_map/all_to_all | solution.py:57
  28.8 5.6 %all-to-all-done.1 = bf16[8,2,3584]{2,1,0:T(2,128)(2,1)S(1)} async-done(((bf16[8,2,3584]{2,1,0:T(2,128)(2,1)}), bf16[8,2,3584]{2,1,0:T(2,128)(2,1)S(1)}, u32[]{:S(2)}, u32[]{:S(2)}) %all-to-all-start.1) | async-done | bytes 114720 | tf_op jit(solution)/shard_map/all_to_all | solution.py:57
  35.2 10.3 %all_gather.7 = bf16[64,3584]{1,0:T(8,128)(2,1)S(1)} all-gather(bf16[64,896]{1,0:T(8,128)(2,1)S(1)} %reshape.51), channel_id=1, replica_groups=mesh['expert'=8,'hid'=4] {'hid'}, dimensions={1}, use_global_device_ids=true | all-gather | bytes 573440 | tf_op jit(solution)/shard_map/all_gather | solution.py:65
  45.5 3.9 %fusion.6 = f32[64,640]{1,0:T(8,128)S(1)} fusion(bf16[64,3584]{1,0:T(8,128)(2,1)S(1)} %all_gather.7, bf16[1,640,3584]{2,1,0:T(8,128)(2,1)} %param.17), kind=kOutput, calls=%fused_computation.10 | convolution fusion | flops 293601280 | bytes 5210112 | tf_op jit(solution)/shard_map/dot_general | solution.py:35
  49.5 1.5 %fusion.9 = f32[64,640]{1,0:T(8,128)S(1)} fusion(bf16[64,3584]{1,0:T(8,128)(2,1)S(1)} %all_gather.7, bf16[1,640,3584]{2,1,0:T(8,128)(2,1)S(1)} %copy-done.1), kind=kOutput, calls=%fused_computation.13 | convolution fusion | flops 293601280 | bytes 5210112 | tf_op jit(solution)/shard_map/dot_general | solution.py:35
  51.0 10.2 %all_gather.6 = bf16[64,3584]{1,0:T(8,128)(2,1)S(1)} all-gather(bf16[64,896]{1,0:T(8,128)(2,1)S(1)} %reshape.50), channel_id=1, replica_groups=mesh['expert'=8,'hid'=4] {'hid'}, dimensions={1}, use_global_device_ids=true | all-gather | bytes 573440 | tf_op jit(solution)/shard_map/all_gather | solution.py:66
  61.2 1.5 %multiply_convert_fusion = (bf16[64,640]{1,0:T(8,128)(2,1)S(1)}, bf16[64,640]{1,0:T(8,128)(2,1)S(1)}) fusion(f32[64,640]{1,0:T(8,128)S(1)} %fusion.6, f32[64,640]{1,0:T(8,128)S(1)} %fusion.9, s32[]{:T(128)} %bitcast.2, s32[]{:T(128)} %bitcast.1, s32[640]{0:T(1024)S(1)} %iota_add_fusion, s32[64]{0:T(128)S(1)} %add_multiply_fusion, ...), kind=kOutput, calls=%fused_computation.25 | convolution fusion | flops 294993920 | bytes 5540616 | tf_op jit(solution)/shard_map/dot_general | solution.py:35
  62.8 0.9 fusion.4
  63.7 1.7 %fusion.3 = bf16[64,3584]{1,0:T(8,128)(2,1)} fusion(f32[64,3584]{1,0:T(8,128)S(1)} %fusion.4, bf16[64,640]{1,0:T(8,128)(2,1)S(1)} %get-tuple-element.4, bf16[1,640,3584]{2,1,0:T(8,128)(2,1)S(1)} %copy-done.1), kind=kOutput, calls=%fused_computation.7 | convolution fusion | flops 294060032 | bytes 6045696 | tf_op jit(solution)/shard_map/dot_general | solution.py:89
  65.4 3.5 %fusion.1 = bf16[1,640,3584]{2,1,0:T(8,128)(2,1)} fusion(bf16[64,640]{1,0:T(8,128)(2,1)S(1)} %get-tuple-element.4, bf16[64,3584]{1,0:T(8,128)(2,1)S(1)} %all_gather.7), kind=kOutput, calls=%fused_computation.4 | convolution fusion | flops 295895040 | bytes 5128192 | tf_op jit(solution)/shard_map/dot_general | solution.py:29
  69.0 39.2 %all-reduce.2.cloned.1.call-done = bf16[64,3584]{1,0:T(8,128)(2,1)} async-done(((bf16[64,3584]{1,0:T(8,128)(2,1)}), bf16[64,3584]{1,0:T(8,128)(2,1)}) %all-reduce.2.cloned.1.call-update) | async-done | bytes 458768 | tf_op jit(solution)/shard_map/psum | solution.py:92
  108.2 0.9 convert_convert_fusion
  109.1 1.3 %reduce.5 = bf16[8,7168]{1,0:T(8,128)(2,1)S(1)} reduce(bf16[8,1,7168]{2,1,0:T(2,128)(2,1)S(1)} %all_to_all.26, bf16[]{:T(256)} %broadcast.36), dimensions={1}, to_apply=%all_to_all.26.reduce_sub_computation | reduce | bytes 229378 | tf_op jit(solution)/shard_map/all_to_all | solution.py:94
  111.2 4.6 %all-to-all-start.2 = ((bf16[8,2,3584]{2,1,0:T(2,128)(2,1)}), bf16[8,2,3584]{2,1,0:T(2,128)(2,1)S(1)}, u32[]{:S(2)}, u32[]{:S(2)}) async-start(bf16[8,2,3584]{2,1,0:T(2,128)(2,1)} %reshape.60), calls=%async_computation.2 | async-start | bytes 229376 | tf_op jit(solution)/shard_map/all_to_all | solution.py:94
  115.8 3.5 %fusion = bf16[1,640,3584]{2,1,0:T(8,128)(2,1)} fusion(bf16[64,640]{1,0:T(8,128)(2,1)S(1)} %get-tuple-element.5, bf16[64,3584]{1,0:T(8,128)(2,1)S(1)} %all_gather.7), kind=kOutput, calls=%fused_computation.3 | convolution fusion | flops 295895040 | bytes 5128192 | tf_op jit(solution)/shard_map/dot_general | solution.py:29
  119.3 3.6 %fusion.2 = bf16[1,640,3584]{2,1,0:T(8,128)(2,1)} fusion(bf16[64,3584]{1,0:T(8,128)(2,1)S(1)} %all_gather.6, f32[64,640]{1,0:T(8,128)S(1)} %fusion.9, s32[]{:T(128)} %bitcast.2, s32[]{:T(128)} %bitcast.1, s32[640]{0:T(1024)S(1)} %iota_add_fusion, s32[64]{0:T(128)S(1)} %add_multiply_fusion, f32[64,640]{1,0:T(8,128)S(1)} %fusion.6), kind=kOutput, calls=%fused_computation.5 | convolution fusion | flops 297000960 | bytes 5376776 | tf_op jit(solution)/shard_map/dot_general | solution.py:29
  123.7 0.7 convolution_convert_fusion.4
  (34 shorter events, 5.6 us)
Async XLA Ops:
  7.2 1.6 %copy-start = (bf16[8,896]{1,0:T(8,128)(2,1)S(1)}, bf16[8,896]{1,0:T(8,128)(2,1)}, u32[]{:S(2)}) copy-start(bf16[8,896]{1,0:T(8,128)(2,1)} %param.11) | copy-start | bytes 43012
  11.6 12.9 %all-to-all-start = ((bf16[8,2,3584]{2,1,0:T(2,128)(2,1)}), bf16[8,2,3584]{2,1,0:T(2,128)(2,1)S(1)}, u32[]{:S(2)}, u32[]{:S(2)}) async-start(bf16[8,2,3584]{2,1,0:T(2,128)(2,1)} %reshape.58), calls=%async_computation | async-start | bytes 229376 | tf_op jit(solution)/shard_map/all_to_all | solution.py:60
  24.5 9.9 %all-to-all-start.1 = ((bf16[8,2,3584]{2,1,0:T(2,128)(2,1)}), bf16[8,2,3584]{2,1,0:T(2,128)(2,1)S(1)}, u32[]{:S(2)}, u32[]{:S(2)}) async-start(bf16[8,2,3584]{2,1,0:T(2,128)(2,1)} %reshape.56), calls=%async_computation.1 | async-start | bytes 229376 | tf_op jit(solution)/shard_map/all_to_all | solution.py:57
  27.9 80.3 %all-reduce.2.cloned.1.call-start = ((), (), s32[]{:S(2)}) async-start(), calls=%async_computation.3 | async-start | bytes 917504 | tf_op jit(solution)/shard_map/psum | solution.py:92
  35.2 14.3 %copy-start.1 = (bf16[1,640,3584]{2,1,0:T(8,128)(2,1)S(1)}, bf16[1,640,3584]{2,1,0:T(8,128)(2,1)}, u32[]{:S(2)}) copy-start(bf16[1,640,3584]{2,1,0:T(8,128)(2,1)} %param.18) | copy-start | bytes 13762564
  35.2 26.0 %copy-start.2 = (bf16[1,640,3584]{2,1,0:T(8,128)(2,1)S(1)}, bf16[1,640,3584]{2,1,0:T(8,128)(2,1)}, u32[]{:S(2)}) copy-start(bf16[1,640,3584]{2,1,0:T(8,128)(2,1)} %param.19) | copy-start | bytes 13762564
  45.5 17.2 %slice-start = ((s8[4587520]{0:T(1024)(128)(4,1)}), s8[4194304]{0:T(1024)(128)(4,1)S(1)}, s32[]{:S(2)}) async-start(s8[4587520]{0:T(1024)(128)(4,1)} %bitcast.41), calls=%async_computation.4 | async-start | bytes 8388608
  49.5 13.3 %slice-start.1 = ((s8[4587520]{0:T(1024)(128)(4,1)}), s8[393216]{0:T(1024)(128)(4,1)S(1)}, s32[]{:S(2)}) async-start(s8[4587520]{0:T(1024)(128)(4,1)} %bitcast.41), calls=%async_computation.5 | async-start | bytes 786432
  111.2 11.8 %all-to-all-start.2 = ((bf16[8,2,3584]{2,1,0:T(2,128)(2,1)}), bf16[8,2,3584]{2,1,0:T(2,128)(2,1)S(1)}, u32[]{:S(2)}, u32[]{:S(2)}) async-start(bf16[8,2,3584]{2,1,0:T(2,128)(2,1)} %reshape.60), calls=%async_computation.2 | async-start | bytes 229376 | tf_op jit(solution)/shard_map/all_to_all | solution.py:94
Sparse Core Ops, SparseCore 0:
  65.6 42.5 all-reduce.1
where the time goes:
time: 132 us; the launch traced here: 131 us
  waiting for transfers between devices  47 us (36%)
  matrix products  22.2 us (17%)
  blocking collectives  20.5 us (16%)
  between operations  15.5 us (12%)
  starting transfers between devices  14.3 us (11%)
  other arithmetic  8.46 us (6%)
  local copies, waits for them, and re-layouts  3.23 us (2%)
    psum x1, waiting for transfers between devices, on_device(): lax.psum(partial_sum.astype(jnp.bfloat16), 'hid').astype(jnp.float32)  39.2 us
    dot_general x4, matrix products, contract_rows(): lax.dot_general(left, right, (((0,), (0,)), ((), ())), preferred_element_...  11.4 us
    all_gather x1, blocking collectives, on_device(): lax.all_gather(recv_x.reshape(capacity, part_width), 'hid', axis=1, tiled...  10.3 us
    all_gather x1, blocking collectives, on_device(): lax.all_gather(recv_dy.reshape(capacity, part_width), 'hid', axis=1, tile...  10.2 us
    dot_general x3, matrix products, contract_cols(): lax.dot_general(left, right, (((1,), (1,)), ((), ())), preferred_element_...  6.96 us
    all_to_all x1, starting transfers between devices, on_device(): lax.all_to_all(sent_dy.reshape(send_shape), 'expert', split_axis=0, conca...  6.32 us
    all_to_all x1, waiting for transfers between devices, on_device(): lax.all_to_all(sent_x.reshape(send_shape), 'expert', split_axis=0, concat...  5.57 us
    all_to_all x1, starting transfers between devices, on_device(): lax.all_to_all(own_cols.astype(jnp.bfloat16).reshape(send_shape), 'expert...  4.61 us
  transfers between devices with their start and end apart: 4, of which 3 were waited for; matrix products, arithmetic and copies ran while one was open for 11% of the time, Pallas kernels for 0%

commit v1 on v0

--- a/solution.py
+++ b/solution.py
@@ -1,6 +1,8 @@
 import jax
 import jax.numpy as jnp
 from jax import lax
+from jax.experimental import pallas as pl
+from jax.experimental.pallas import tpu as pltpu
 from jax.sharding import PartitionSpec as P
 
 FF = 2560
@@ -37,7 +39,7 @@
     )
 
 
-def on_device(
+def general_device(
     tokens, cotangent, gate_prob, routes, slots, drop_seed, layer_id, w_gate, w_up, w_down
 ):
     experts = lax.axis_size("expert")
@@ -104,6 +106,231 @@
     return (grad_tokens, grad_gate[None], grad_up[None], grad_down[None])
 
 
+BF16 = jnp.bfloat16
+F32 = jnp.float32
+AXES = ("expert", "hid")
+
+
+def relative_order(size):
+    order = [0]
+    bits = [1 << b for b in range(1, size.bit_length() - 1)][::-1] + [1]
+    for bit in bits:
+        order = order + [o ^ bit for o in order]
+    return order
+
+
+def swap(value, distance, size):
+    return lax.ppermute(value, AXES, [(i, i ^ distance) for i in range(size)])
+
+
+def logical(values, amount):
+    return lax.shift_right_logical(values, jnp.full(values.shape, amount, jnp.int32))
+
+
+def contract_last(left, right):
+    return lax.dot_general(
+        left, right, (((1,), (1,)), ((), ())), preferred_element_type=F32
+    )
+
+
+def hidden_kernel(
+    place_ref, x_ref, c_ref, gate_ref, base_ref, wg_hbm, wu_hbm, wd_hbm,
+    piece_ref, dy_ref, hid_t_ref, gpre_t_ref, upre_t_ref,
+    wg, wu, wd, sems,
+):
+    parts, rows, width = x_ref.shape
+    units = wg.shape[0]
+    me = place_ref[0]
+
+    def copies(j):
+        cols = pl.ds(pl.multiple_of((me ^ j) * width, 128), width)
+        return [
+            pltpu.make_async_copy(src.at[:, cols], dst.at[:, cols], sems.at[j, k])
+            for k, (src, dst) in enumerate(((wg_hbm, wg), (wu_hbm, wu), (wd_hbm, wd)))
+        ]
+
+    for j in range(parts):
+        for copy in copies(j):
+            copy.start()
+    gate = gate_ref[...]
+    unit_ids = me * units + lax.broadcasted_iota(jnp.int32, (rows, units), 1)
+    mixed = base_ref[...] + unit_ids * -1640531535
+    mixed = mixed ^ logical(mixed, 15)
+    mixed = mixed * -2048144789
+    mixed = mixed ^ logical(mixed, 13)
+    mixed = mixed * -1028477387
+    mixed = mixed ^ logical(mixed, 16)
+    levels = logical(mixed, 8) & 1023
+    keep_mul = jnp.where(levels >= 102, KEEP_FACTOR, 0.0).astype(F32)
+    gate_pre = up_pre = grad_hidden = None
+    for j in range(parts):
+        cols = pl.ds(pl.multiple_of((me ^ j) * width, 128), width)
+        x = x_ref[j]
+        dy = (gate * c_ref[j].astype(F32)).astype(BF16)
+        dy_ref[j] = dy
+        for copy in copies(j):
+            copy.wait()
+        terms = (
+            contract_last(x, wg[:, cols]),
+            contract_last(x, wu[:, cols]),
+            contract_last(dy, wd[:, cols]),
+        )
+        if j == 0:
+            gate_pre, up_pre, grad_hidden = terms
+        else:
+            gate_pre, up_pre, grad_hidden = (
+                gate_pre + terms[0], up_pre + terms[1], grad_hidden + terms[2]
+            )
+    grad_hidden = grad_hidden * keep_mul
+    logistic = jax.nn.sigmoid(gate_pre)
+    swish = gate_pre * logistic
+    hidden = swish * up_pre * keep_mul
+    upre = grad_hidden * swish
+    gpre = grad_hidden * up_pre * logistic * (1.0 + gate_pre * (1.0 - logistic))
+    hid_t_ref[...] = hidden.T.astype(BF16)
+    gpre_t_ref[...] = gpre.T.astype(BF16)
+    upre_t_ref[...] = upre.T.astype(BF16)
+    gpre = gpre.astype(BF16)
+    upre = upre.astype(BF16)
+    for j in range(parts):
+        cols = pl.ds(pl.multiple_of((me ^ j) * width, 128), width)
+        piece_ref[j] = (
+            jnp.dot(gpre, wg[:, cols], preferred_element_type=F32)
+            + jnp.dot(upre, wu[:, cols], preferred_element_type=F32)
+        ).astype(BF16)
+
+
+def weight_kernel(place_ref, left_ref, right_ref, out_ref):
+    out_ref[...] = jnp.dot(
+        left_ref[...], right_ref[0], preferred_element_type=F32
+    ).astype(BF16)
+
+
+def weight_grad(place, left, right):
+    parts, rows, width = right.shape
+    units = left.shape[0]
+    return pl.pallas_call(
+        weight_kernel,
+        grid_spec=pltpu.PrefetchScalarGridSpec(
+            num_scalar_prefetch=1,
+            grid=(parts,),
+            in_specs=[
+                pl.BlockSpec((units, rows), lambda j, place: (0, 0)),
+                pl.BlockSpec((1, rows, width), lambda j, place: (j, 0, 0)),
+            ],
+            out_specs=pl.BlockSpec((units, width), lambda j, place: (0, place[0] ^ j)),
+        ),
+        out_shape=jax.ShapeDtypeStruct((units, parts * width), BF16),
+        cost_estimate=pl.CostEstimate(
+            flops=2 * units * rows * parts * width,
+            bytes_accessed=2 * units * parts * width,
+            transcendentals=0,
+        ),
+    )(place, left, right)
+
+
+def token_device(
+    tokens, cotangent, gate_prob, routes, slots, drop_seed, layer_id, w_gate, w_up, w_down
+):
+    experts = lax.axis_size("expert")
+    parts = lax.axis_size("hid")
+    size = experts * parts
+    group, width = tokens.shape
+    units = w_gate.shape[1]
+    rows = experts * group
+    expert_id = lax.axis_index("expert")
+    hid_id = lax.axis_index("hid")
+    top = gate_prob.shape[1]
+    high = gate_prob.astype(BF16)
+    rest = gate_prob - high.astype(F32)
+    middle = rest.astype(BF16)
+    low = (rest - middle.astype(F32)).astype(BF16)
+    notes = jnp.concatenate(
+        [routes.astype(BF16), slots.astype(BF16), high, middle, low,
+         jnp.zeros((group, 128 - 5 * top), BF16)], axis=1)
+    data = jnp.concatenate(
+        [jnp.concatenate([tokens, notes], axis=1),
+         jnp.concatenate([cotangent, jnp.zeros((group, 128), BF16)], axis=1)], axis=0)[None]
+    distance = experts // 2
+    while distance > 1:
+        data = jnp.concatenate([data, swap(data, distance * parts, size)], axis=0)
+        distance //= 2
+    notes = data[:, :group, width:]
+    data = data[:, :, :width]
+    notes = jnp.concatenate([notes, swap(notes, parts, size)], axis=0).reshape(rows, 128)
+    data = jnp.stack([data] + [swap(data, j, size) for j in range(1, parts)], axis=0)
+    data = jnp.concatenate([data, swap(data, parts, size)], axis=1)
+    x = data[:, :, :group].reshape(parts, rows, width)
+    c = data[:, :, group:].reshape(parts, rows, width)
+    order = jnp.array(relative_order(experts), jnp.int32)
+    group_ids = jnp.repeat(order ^ expert_id, group)[:, None]
+    notes = notes.astype(F32)
+    route, slot, high, middle, low = (notes[:, i * top:(i + 1) * top] for i in range(5))
+    chosen = (route == expert_id.astype(F32)) & (slot < CAP_SRC)
+    gate = jnp.sum(jnp.where(chosen, high + middle + low, 0.0), axis=1, keepdims=True)
+    slot = jnp.sum(jnp.where(chosen, slot, 0.0), axis=1, keepdims=True).astype(jnp.int32)
+    row_ids = expert_id * (experts * CAP_SRC) + group_ids * CAP_SRC + slot
+    base = row_ids * FF * -1640531535 + drop_seed[0] * 40503 + layer_id[0] * 97
+    place = hid_id.astype(jnp.int32)[None]
+    any_spec = pl.BlockSpec(memory_space=pl.ANY)
+    vmem_spec = pl.BlockSpec(memory_space=pltpu.VMEM)
+    turned = jax.ShapeDtypeStruct((units, rows), BF16)
+    spread = jax.ShapeDtypeStruct((parts, rows, width), BF16)
+    piece, dy, hid_t, gpre_t, upre_t = pl.pallas_call(
+        hidden_kernel,
+        in_specs=[pl.BlockSpec(memory_space=pltpu.SMEM)] + [vmem_spec] * 4 + [any_spec] * 3,
+        out_specs=[vmem_spec] * 5,
+        out_shape=[spread, spread, turned, turned, turned],
+        scratch_shapes=[pltpu.VMEM((units, parts * width), BF16)] * 3
+        + [pltpu.SemaphoreType.DMA((parts, 3))],
+        compiler_params=pltpu.CompilerParams(vmem_limit_bytes=32 * 1024 * 1024),
+        cost_estimate=pl.CostEstimate(
+            flops=10 * units * rows * parts * width,
+            bytes_accessed=6 * units * parts * width,
+            transcendentals=rows * units,
+        ),
+    )(place, x, c, gate, base, w_gate[0], w_up[0], w_down[0])
+    part = piece.reshape(parts, experts, group, width)
+    half = experts // 2
+
+    def add(kept, came):
+        return (kept.astype(F32) + came.astype(F32)).astype(BF16)
+
+    part = add(part[:, :half], swap(part[:, half:], parts, size))
+    distance = parts // 2
+    while distance:
+        count = part.shape[0] // 2
+        part = add(part[:count], swap(part[count:], distance, size))
+        distance //= 2
+    part = part[0]
+    distance = 2
+    while distance < experts:
+        count = part.shape[0] // 2
+        part = add(part[:count], swap(part[count:], distance * parts, size))
+        distance *= 2
+    grad_tokens = part[0]
+    grad_down = weight_grad(place, hid_t, dy)
+    grad_gate = weight_grad(place, gpre_t, x)
+    grad_up = weight_grad(place, upre_t, x)
+    return (grad_tokens, grad_gate[None], grad_up[None], grad_down[None])
+
+
+def power_of_two(number):
+    return number & (number - 1) == 0
+
+
+def on_device(*args):
+    tokens, gate_prob = args[0], args[2]
+    experts = lax.axis_size("expert")
+    parts = lax.axis_size("hid")
+    small = tokens.shape[0] <= CAP_SRC and 5 * gate_prob.shape[1] <= 128
+    even = power_of_two(experts) and power_of_two(parts) and experts > 1
+    tiled = tokens.shape[1] % 128 == 0 and args[7].shape[1] % 128 == 0
+    if small and even and tiled and tokens.shape[0] % 8 == 0 and experts <= 256:
+        return token_device(*args)
+    return general_device(*args)
+
+
 def solution(mesh):
     in_specs = (
         P("expert", "hid"),

time: 132 us -> 72.4 us (0.55)
  waiting for transfers between devices: 47 us -> 19.3 us
  matrix products: 22.2 us -> 0 us
  Pallas kernels: 0 us -> 22.2 us
  blocking collectives: 20.5 us -> 0 us
  between operations: 15.5 us -> 2.14 us
  local copies, waits for them, and re-layouts: 3.23 us -> 8.37 us
  other arithmetic: 8.46 us -> 4.69 us
    psum x1 -> x0, waiting for transfers between devices: 39.2 us -> none  [on_device(): lax.psum(partial_sum.astype(jnp.bfloat16), 'hid').astype(jnp.float32)]
    pallas_call x0 -> x4, Pallas kernels: none -> 22.2 us  [the longest x3 14.3 us: weight_grad(): pl.pallas_call(weight_kernel, grid_spec=pltpu.PrefetchScalarGridSpec(num_...]
    dot_general x11 -> x0, matrix products: 22.2 us -> none  [the longest x4 11.4 us: contract_rows(): lax.dot_general(left, right, (((0,), (0,)), ((), ())), preferred_element_...]
    all_gather x2 -> x0, blocking collectives: 20.5 us -> none  [the longest x1 10.3 us: on_device(): lax.all_gather(recv_x.reshape(capacity, part_width), 'hid', axis=1, tiled...]
    ppermute x0 -> x12, waiting for transfers between devices: none -> 19.3 us  [swap(): return lax.ppermute(value, AXES, [(i, i ^ distance) for i in range(size)])]
    ppermute x0 -> x12, starting transfers between devices: none -> 15 us  [swap(): return lax.ppermute(value, AXES, [(i, i ^ distance) for i in range(size)])]
    all_to_all x3 -> x0, starting transfers between devices: 14.3 us -> none  [the longest x1 6.32 us: on_device(): lax.all_to_all(sent_dy.reshape(send_shape), 'expert', split_axis=0, conca...]
    all_to_all x3 -> x0, waiting for transfers between devices: 7.8 us -> none  [the longest x1 5.57 us: on_device(): lax.all_to_all(sent_x.reshape(send_shape), 'expert', split_axis=0, concat...]
  transfers between devices with their start and end apart: 4 -> 12, of which waited for: 3 -> 9; matrix products, arithmetic and copies ran while one was open for 11% -> 2% of each run, Pallas kernels for 0% -> 20%
where the time goes in v1:
time: 72.4 us; the launch traced here: 71.7 us
  Pallas kernels  22.2 us (31%)
  waiting for transfers between devices  19.3 us (27%)
  starting transfers between devices  15 us (21%)
  local copies, waits for them, and re-layouts  8.37 us (12%)
  other arithmetic  4.69 us (6%)
  between operations  2.14 us (3%)
    ppermute x12, waiting for transfers between devices, swap(): return lax.ppermute(value, AXES, [(i, i ^ distance) for i in range(size)])  19.3 us
    ppermute x12, starting transfers between devices, swap(): return lax.ppermute(value, AXES, [(i, i ^ distance) for i in range(size)])  15 us
    pallas_call x3, Pallas kernels, weight_grad(): pl.pallas_call(weight_kernel, grid_spec=pltpu.PrefetchScalarGridSpec(num_...  14.3 us
    pallas_call x1, Pallas kernels, token_device(): pl.pallas_call(hidden_kernel, in_specs=[pl.BlockSpec(memory_space=pltpu.S...  7.99 us
    unnamed x16, local copies, waits for them, and re-layouts  7.08 us
  transfers between devices with their start and end apart: 12, of which 9 were waited for; matrix products, arithmetic and copies ran while one was open for 2% of the time, Pallas kernels for 20%

profile of v1, /device:TPU:0, one launch (start us, length us, event | category | flops | bytes accessed | tf_op | source)
XLA Modules:
  0.0 71.7 jit_solution(12343552986516622923)
XLA Ops:
  0.6 0.7 convert_element_type.92
  2.0 0.8 %subtract_convert_fusion = (bf16[8,8]{1,0:T(8,128)(2,1)S(1)}, bf16[8,8]{1,0:T(8,128)(2,1)S(1)}, bf16[8,8]{1,0:T(8,128)(2,1)S(1)}) fusion(f32[8,8]{1,0:T(8,128)} %param.13), kind=kLoop, calls=%fused_computation.30 | loop fusion | flops 448 | bytes 640 | tf_op jit(solution)/shard_map/convert_element_type | solution.py:247
  2.8 0.8 %concatenate.22 = bf16[8,1024]{1,0:T(8,128)(2,1)S(1)} concatenate(bf16[8,896]{1,0:T(8,128)(2,1)} %param.11, bf16[8,8]{1,0:T(8,128)(2,1)S(1)} %convert_element_type.92, bf16[8,8]{1,0:T(8,128)(2,1)S(1)} %convert_element_type.93, bf16[8,8]{1,0:T(8,128)(2,1)S(1)} %get-tuple-element.22, bf16[8,8]{1,0:T(8,128)(2,1)S(1)} %get-tuple-element.21, bf16[8,8]{1,0:T(8,128)(2,1)S(1)} %get-tuple-element.20, ...), dimensions={1} | concatenate | bytes 32768 | tf_op jit(solution)/shard_map/concatenate | solution.py:252
  3.6 0.7 fusion.3
  4.3 4.0 %collective-permute-start = (bf16[1,16,1024]{2,1,0:T(8,128)(2,1)S(1)}, bf16[1,16,1024]{2,1,0:T(8,128)(2,1)S(1)}, u32[]{:S(2)}, u32[]{:S(2)}) collective-permute-start(bf16[1,16,1024]{2,1,0:T(8,128)(2,1)S(1)} %fusion.3), channel_id=1, source_target_pairs={{0,16},{1,17},{2,18},{3,19},{4,20},{5,21},{6,22},{7,23},{8,24},{9,... | collective-permute-start | bytes 98312 | tf_op jit(solution)/shard_map/ppermute | solution.py:123
  8.3 2.2 %collective-permute-done = bf16[1,16,1024]{2,1,0:T(8,128)(2,1)S(1)} collective-permute-done((bf16[1,16,1024]{2,1,0:T(8,128)(2,1)S(1)}, bf16[1,16,1024]{2,1,0:T(8,128)(2,1)S(1)}, u32[]{:S(2)}, u32[]{:S(2)}) %collective-permute-start) | collective-permute-done | bytes 32800 | tf_op jit(solution)/shard_map/ppermute | solution.py:123
  10.6 1.6 %collective-permute-start.1 = (bf16[2,16,1024]{2,1,0:T(8,128)(2,1)S(1)}, bf16[2,16,1024]{2,1,0:T(8,128)(2,1)S(1)}, u32[]{:S(2)}, u32[]{:S(2)}) collective-permute-start(bf16[2,16,1024]{2,1,0:T(8,128)(2,1)S(1)} %pad_maximum_fusion.3), channel_id=1, source_target_pairs={{0,8},{1,9},{2,10},{3,11},{4,12},{5,13},{6,14},{7,15},{8,0},{9,1},... | collective-permute-start | bytes 196616 | tf_op jit(solution)/shard_map/ppermute | solution.py:123
  12.2 2.7 %collective-permute-done.1 = bf16[2,16,1024]{2,1,0:T(8,128)(2,1)S(1)} collective-permute-done((bf16[2,16,1024]{2,1,0:T(8,128)(2,1)S(1)}, bf16[2,16,1024]{2,1,0:T(8,128)(2,1)S(1)}, u32[]{:S(2)}, u32[]{:S(2)}) %collective-permute-start.1) | collective-permute-done | bytes 65568 | tf_op jit(solution)/shard_map/ppermute | solution.py:123
  15.0 1.8 %collective-permute-start.3 = (bf16[4,16,896]{2,1,0:T(8,128)(2,1)S(1)}, bf16[4,16,896]{2,1,0:T(8,128)(2,1)S(1)}, u32[]{:S(2)}, u32[]{:S(2)}) collective-permute-start(bf16[4,16,896]{2,1,0:T(8,128)(2,1)S(1)} %get-tuple-element.19), channel_id=1, source_target_pairs={{0,2},{1,3},{2,0},{3,1},{4,6},{5,7},{6,4},{7,5},{8,10},{9,11},{10,... | collective-permute-start | bytes 344072 | tf_op jit(solution)/shard_map/ppermute | solution.py:123
  16.8 1.5 %collective-permute-start.2 = (bf16[4,16,896]{2,1,0:T(8,128)(2,1)S(1)}, bf16[4,16,896]{2,1,0:T(8,128)(2,1)S(1)}, u32[]{:S(2)}, u32[]{:S(2)}) collective-permute-start(bf16[4,16,896]{2,1,0:T(8,128)(2,1)S(1)} %get-tuple-element.19), channel_id=1, source_target_pairs={{0,1},{1,0},{2,3},{3,2},{4,5},{5,4},{6,7},{7,6},{8,9},{9,8},{10,11... | collective-permute-start | bytes 344072 | tf_op jit(solution)/shard_map/ppermute | solution.py:123
  21.5 2.4 %collective-permute-done.4 = bf16[4,16,896]{2,1,0:T(8,128)(2,1)S(1)} collective-permute-done((bf16[4,16,896]{2,1,0:T(8,128)(2,1)S(1)}, bf16[4,16,896]{2,1,0:T(8,128)(2,1)S(1)}, u32[]{:S(2)}, u32[]{:S(2)}) %collective-permute-start.4) | collective-permute-done | bytes 114720 | tf_op jit(solution)/shard_map/ppermute | solution.py:123
  24.5 1.4 %collective-permute-done.5 = bf16[4,4,16,896]{3,2,1,0:T(8,128)(2,1)S(1)} collective-permute-done((bf16[4,4,16,896]{3,2,1,0:T(8,128)(2,1)S(1)}, bf16[4,4,16,896]{3,2,1,0:T(8,128)(2,1)S(1)}, u32[]{:S(2)}, u32[]{:S(2)}) %collective-permute-start.5) | collective-permute-done | bytes 458784 | tf_op jit(solution)/shard_map/ppermute | solution.py:123
  26.1 2.5 %copy-done.1 = bf16[1,640,3584]{2,1,0:T(8,128)(2,1)S(1)} copy-done((bf16[1,640,3584]{2,1,0:T(8,128)(2,1)S(1)}, bf16[1,640,3584]{2,1,0:T(8,128)(2,1)}, u32[]{:S(2)}) %copy-start.1) | copy-done | bytes 4587544
  28.6 2.3 %copy-done.2 = bf16[1,640,3584]{2,1,0:T(8,128)(2,1)S(1)} copy-done((bf16[1,640,3584]{2,1,0:T(8,128)(2,1)S(1)}, bf16[1,640,3584]{2,1,0:T(8,128)(2,1)}, u32[]{:S(2)}) %copy-start.2) | copy-done | bytes 4587544
  30.9 2.3 %copy-done.3 = bf16[1,640,3584]{2,1,0:T(8,128)(2,1)S(1)} copy-done((bf16[1,640,3584]{2,1,0:T(8,128)(2,1)S(1)}, bf16[1,640,3584]{2,1,0:T(8,128)(2,1)}, u32[]{:S(2)}) %copy-start.3) | copy-done | bytes 4587544
  33.2 8.0 %shard_map.138 = (bf16[4,64,896]{2,1,0:T(8,128)(2,1)S(1)}, bf16[4,64,896]{2,1,0:T(8,128)(2,1)S(1)}, bf16[640,64]{1,0:T(8,128)(2,1)S(1)}, bf16[640,64]{1,0:T(8,128)(2,1)S(1)}, bf16[640,64]{1,0:T(8,128)(2,1)S(1)}) custom-call(s32[1]{0:T(128)} %bitcast.place_ref, bf16[4,64,896]{2,1,0:T(8,128)(2,1)S(1)} %get-tuple-element.17.x_ref.right_ref, ...), custom_call_target="tpu_custom_call" | custom-call | flops 1468006400 | bytes 13762560 | tf_op jit(solution)/shard_map/pallas_call | solution.py:279
  41.5 1.4 %collective-permute-done.7 = bf16[4,4,8,896]{3,2,1,0:T(8,128)(2,1)S(1)} collective-permute-done((bf16[4,4,8,896]{3,2,1,0:T(8,128)(2,1)S(1)}, bf16[4,4,8,896]{3,2,1,0:T(8,128)(2,1)S(1)}, u32[]{:S(2)}, u32[]{:S(2)}) %collective-permute-start.7) | collective-permute-done | bytes 229408 | tf_op jit(solution)/shard_map/ppermute | solution.py:123
  43.5 4.7 %collective-permute-done.8 = bf16[2,4,8,896]{3,2,1,0:T(8,128)(2,1)S(1)} collective-permute-done((bf16[2,4,8,896]{3,2,1,0:T(8,128)(2,1)S(1)}, bf16[2,4,8,896]{3,2,1,0:T(8,128)(2,1)S(1)}, u32[]{:S(2)}, u32[]{:S(2)}) %collective-permute-start.8) | collective-permute-done | bytes 114720 | tf_op jit(solution)/shard_map/ppermute | solution.py:123
  48.8 3.6 %collective-permute-done.9 = bf16[1,4,8,896]{3,2,1,0:T(8,128)(2,1)S(1)} collective-permute-done((bf16[1,4,8,896]{3,2,1,0:T(8,128)(2,1)S(1)}, bf16[1,4,8,896]{3,2,1,0:T(8,128)(2,1)S(1)}, u32[]{:S(2)}, u32[]{:S(2)}) %collective-permute-start.9) | collective-permute-done | bytes 57376 | tf_op jit(solution)/shard_map/ppermute | solution.py:123
  52.5 1.4 %collective-permute-start.10 = (bf16[2,8,896]{2,1,0:T(8,128)(2,1)S(1)}, bf16[2,8,896]{2,1,0:T(8,128)(2,1)S(1)}, u32[]{:S(2)}, u32[]{:S(2)}) collective-permute-start(bf16[2,8,896]{2,1,0:T(8,128)(2,1)S(1)} %slice_bitcast_fusion.2), channel_id=1, source_target_pairs={{0,8},{1,9},{2,10},{3,11},{4,12},{5,13},{6,14},{7,15},{8,0},{9,1},... | collective-permute-start | bytes 86024 | tf_op jit(solution)/shard_map/ppermute | solution.py:123
  53.9 4.7 %shard_map.139 = bf16[640,3584]{1,0:T(8,128)(2,1)} custom-call(s32[1]{0:T(128)} %bitcast.place_ref, bf16[640,64]{1,0:T(8,128)(2,1)} %copy-done.7, bf16[4,64,896]{2,1,0:T(8,128)(2,1)} %copy-done), custom_call_target="tpu_custom_call" | custom-call | flops 293601280 | bytes 4587520 | tf_op jit(solution)/shard_map/pallas_call | solution.py:212
  58.7 4.8 %shard_map.140 = bf16[640,3584]{1,0:T(8,128)(2,1)} custom-call(s32[1]{0:T(128)} %bitcast.place_ref, bf16[640,64]{1,0:T(8,128)(2,1)} %copy-done.6, bf16[4,64,896]{2,1,0:T(8,128)(2,1)} %copy-done), custom_call_target="tpu_custom_call" | custom-call | flops 293601280 | bytes 4587520 | tf_op jit(solution)/shard_map/pallas_call | solution.py:212
  63.5 2.9 %collective-permute-start.11 = (bf16[1,8,896]{2,1,0:T(8,128)(2,1)S(1)}, bf16[1,8,896]{2,1,0:T(8,128)(2,1)S(1)}, u32[]{:S(2)}, u32[]{:S(2)}) collective-permute-start(bf16[1,8,896]{2,1,0:T(8,128)(2,1)S(1)} %slice.98), channel_id=1, source_target_pairs={{0,16},{1,17},{2,18},{3,19},{4,20},{5,21},{6,22},{7,23},{8,24},{9,... | collective-permute-start | bytes 43016 | tf_op jit(solution)/shard_map/ppermute | solution.py:123
  66.3 4.8 %shard_map.141 = bf16[640,3584]{1,0:T(8,128)(2,1)} custom-call(s32[1]{0:T(128)} %bitcast.place_ref, bf16[640,64]{1,0:T(8,128)(2,1)} %copy-done.5, bf16[4,64,896]{2,1,0:T(8,128)(2,1)} %copy-done.4), custom_call_target="tpu_custom_call" | custom-call | flops 293601280 | bytes 4587520 | tf_op jit(solution)/shard_map/pallas_call | solution.py:212
  (52 shorter events, 5.7 us)
Async XLA Ops:
  4.3 6.3 %collective-permute-start = (bf16[1,16,1024]{2,1,0:T(8,128)(2,1)S(1)}, bf16[1,16,1024]{2,1,0:T(8,128)(2,1)S(1)}, u32[]{:S(2)}, u32[]{:S(2)}) collective-permute-start(bf16[1,16,1024]{2,1,0:T(8,128)(2,1)S(1)} %fusion.3), channel_id=1, source_target_pairs={{0,16},{1,17},{2,18},{3,19},{4,20},{5,21},{6,22},{7,23},{8,24},{9,... | collective-permute-start | bytes 98312 | tf_op jit(solution)/shard_map/ppermute | solution.py:123
  10.6 4.3 %collective-permute-start.1 = (bf16[2,16,1024]{2,1,0:T(8,128)(2,1)S(1)}, bf16[2,16,1024]{2,1,0:T(8,128)(2,1)S(1)}, u32[]{:S(2)}, u32[]{:S(2)}) collective-permute-start(bf16[2,16,1024]{2,1,0:T(8,128)(2,1)S(1)} %pad_maximum_fusion.3), channel_id=1, source_target_pairs={{0,8},{1,9},{2,10},{3,11},{4,12},{5,13},{6,14},{7,15},{8,0},{9,1},... | collective-permute-start | bytes 196616 | tf_op jit(solution)/shard_map/ppermute | solution.py:123
  15.0 6.0 %collective-permute-start.3 = (bf16[4,16,896]{2,1,0:T(8,128)(2,1)S(1)}, bf16[4,16,896]{2,1,0:T(8,128)(2,1)S(1)}, u32[]{:S(2)}, u32[]{:S(2)}) collective-permute-start(bf16[4,16,896]{2,1,0:T(8,128)(2,1)S(1)} %get-tuple-element.19), channel_id=1, source_target_pairs={{0,2},{1,3},{2,0},{3,1},{4,6},{5,7},{6,4},{7,5},{8,10},{9,11},{10,... | collective-permute-start | bytes 344072 | tf_op jit(solution)/shard_map/ppermute | solution.py:123
  16.8 4.8 %collective-permute-start.2 = (bf16[4,16,896]{2,1,0:T(8,128)(2,1)S(1)}, bf16[4,16,896]{2,1,0:T(8,128)(2,1)S(1)}, u32[]{:S(2)}, u32[]{:S(2)}) collective-permute-start(bf16[4,16,896]{2,1,0:T(8,128)(2,1)S(1)} %get-tuple-element.19), channel_id=1, source_target_pairs={{0,1},{1,0},{2,3},{3,2},{4,5},{5,4},{6,7},{7,6},{8,9},{9,8},{10,11... | collective-permute-start | bytes 344072 | tf_op jit(solution)/shard_map/ppermute | solution.py:123
  18.2 5.7 %collective-permute-start.4 = (bf16[4,16,896]{2,1,0:T(8,128)(2,1)S(1)}, bf16[4,16,896]{2,1,0:T(8,128)(2,1)S(1)}, u32[]{:S(2)}, u32[]{:S(2)}) collective-permute-start(bf16[4,16,896]{2,1,0:T(8,128)(2,1)S(1)} %get-tuple-element.19), channel_id=1, source_target_pairs={{0,3},{1,2},{2,1},{3,0},{4,7},{5,6},{6,5},{7,4},{8,11},{9,10},{10,... | collective-permute-start | bytes 344072 | tf_op jit(solution)/shard_map/ppermute | solution.py:123
  18.5 2.1 %collective-permute-start.6 = (bf16[4,8,128]{2,1,0:T(8,128)(2,1)S(1)}, bf16[4,8,128]{2,1,0:T(8,128)(2,1)S(1)}, u32[]{:S(2)}, u32[]{:S(2)}) collective-permute-start(bf16[4,8,128]{2,1,0:T(8,128)(2,1)S(1)} %pad_maximum_fusion.4), channel_id=1, source_target_pairs={{0,4},{1,5},{2,6},{3,7},{4,0},{5,1},{6,2},{7,3},{8,12},{9,13},{10,... | collective-permute-start | bytes 24584 | tf_op jit(solution)/shard_map/ppermute | solution.py:123
  24.0 1.9 %collective-permute-start.5 = (bf16[4,4,16,896]{3,2,1,0:T(8,128)(2,1)S(1)}, bf16[4,4,16,896]{3,2,1,0:T(8,128)(2,1)S(1)}, u32[]{:S(2)}, u32[]{:S(2)}) collective-permute-start(bf16[4,4,16,896]{3,2,1,0:T(8,128)(2,1)S(1)} %pad_maximum_fusion.1), channel_id=1, source_target_pairs={{0,4},{1,5},{2,6},{3,7},{4,0},{5,1},{6,2},{7,3},{8,12},{9,13},{10,... | collective-permute-start | bytes 1376264 | tf_op jit(solution)/shard_map/ppermute | solution.py:123
  26.1 15.1 %copy-start = (bf16[4,64,896]{2,1,0:T(8,128)(2,1)}, bf16[4,64,896]{2,1,0:T(8,128)(2,1)S(1)}, u32[]{:S(2)}) copy-start(bf16[4,64,896]{2,1,0:T(8,128)(2,1)S(1)} %get-tuple-element.17.x_ref.right_ref) | copy-start | bytes 1376260
  26.1 2.5 %copy-start.1 = (bf16[1,640,3584]{2,1,0:T(8,128)(2,1)S(1)}, bf16[1,640,3584]{2,1,0:T(8,128)(2,1)}, u32[]{:S(2)}) copy-start(bf16[1,640,3584]{2,1,0:T(8,128)(2,1)} %param.18) | copy-start | bytes 13762564
  28.6 2.3 %copy-start.2 = (bf16[1,640,3584]{2,1,0:T(8,128)(2,1)S(1)}, bf16[1,640,3584]{2,1,0:T(8,128)(2,1)}, u32[]{:S(2)}) copy-start(bf16[1,640,3584]{2,1,0:T(8,128)(2,1)} %param.19) | copy-start | bytes 13762564
  30.9 2.3 %copy-start.3 = (bf16[1,640,3584]{2,1,0:T(8,128)(2,1)S(1)}, bf16[1,640,3584]{2,1,0:T(8,128)(2,1)}, u32[]{:S(2)}) copy-start(bf16[1,640,3584]{2,1,0:T(8,128)(2,1)} %param.20) | copy-start | bytes 13762564
  41.2 1.7 %copy-start.4 = (bf16[4,64,896]{2,1,0:T(8,128)(2,1)}, bf16[4,64,896]{2,1,0:T(8,128)(2,1)S(1)}, u32[]{:S(2)}) copy-start(bf16[4,64,896]{2,1,0:T(8,128)(2,1)S(1)} %get-tuple-element.13.right_ref) | copy-start | bytes 1376260
  41.2 1.7 %copy-start.5 = (bf16[640,64]{1,0:T(8,128)(2,1)}, bf16[640,64]{1,0:T(8,128)(2,1)S(1)}, u32[]{:S(2)}) copy-start(bf16[640,64]{1,0:T(8,128)(2,1)S(1)} %get-tuple-element.12.left_ref) | copy-start | bytes 245764
  41.2 2.3 %copy-start.6 = (bf16[640,64]{1,0:T(8,128)(2,1)}, bf16[640,64]{1,0:T(8,128)(2,1)S(1)}, u32[]{:S(2)}) copy-start(bf16[640,64]{1,0:T(8,128)(2,1)S(1)} %get-tuple-element.11.left_ref) | copy-start | bytes 245764
  41.2 6.9 %copy-start.7 = (bf16[640,64]{1,0:T(8,128)(2,1)}, bf16[640,64]{1,0:T(8,128)(2,1)S(1)}, u32[]{:S(2)}) copy-start(bf16[640,64]{1,0:T(8,128)(2,1)S(1)} %get-tuple-element.10.left_ref) | copy-start | bytes 245764
  41.3 1.6 %collective-permute-start.7 = (bf16[4,4,8,896]{3,2,1,0:T(8,128)(2,1)S(1)}, bf16[4,4,8,896]{3,2,1,0:T(8,128)(2,1)S(1)}, u32[]{:S(2)}, u32[]{:S(2)}) collective-permute-start(bf16[4,4,8,896]{3,2,1,0:T(8,128)(2,1)S(1)} %slice.90), channel_id=1, source_target_pairs={{0,4},{1,5},{2,6},{3,7},{4,0},{5,1},{6,2},{7,3},{8,12},{9,13},{10,... | collective-permute-start | bytes 688136 | tf_op jit(solution)/shard_map/ppermute | solution.py:123
  42.9 5.3 %collective-permute-start.8 = (bf16[2,4,8,896]{3,2,1,0:T(8,128)(2,1)S(1)}, bf16[2,4,8,896]{3,2,1,0:T(8,128)(2,1)S(1)}, u32[]{:S(2)}, u32[]{:S(2)}) collective-permute-start(bf16[2,4,8,896]{3,2,1,0:T(8,128)(2,1)S(1)} %slice.92), channel_id=1, source_target_pairs={{0,2},{1,3},{2,0},{3,1},{4,6},{5,7},{6,4},{7,5},{8,10},{9,11},{10,... | collective-permute-start | bytes 344072 | tf_op jit(solution)/shard_map/ppermute | solution.py:123
  48.2 4.2 %collective-permute-start.9 = (bf16[1,4,8,896]{3,2,1,0:T(8,128)(2,1)S(1)}, bf16[1,4,8,896]{3,2,1,0:T(8,128)(2,1)S(1)}, u32[]{:S(2)}, u32[]{:S(2)}) collective-permute-start(bf16[1,4,8,896]{3,2,1,0:T(8,128)(2,1)S(1)} %slice.94), channel_id=1, source_target_pairs={{0,1},{1,0},{2,3},{3,2},{4,5},{5,4},{6,7},{7,6},{8,9},{9,8},{10,11... | collective-permute-start | bytes 172040 | tf_op jit(solution)/shard_map/ppermute | solution.py:123
  52.5 10.9 %collective-permute-start.10 = (bf16[2,8,896]{2,1,0:T(8,128)(2,1)S(1)}, bf16[2,8,896]{2,1,0:T(8,128)(2,1)S(1)}, u32[]{:S(2)}, u32[]{:S(2)}) collective-permute-start(bf16[2,8,896]{2,1,0:T(8,128)(2,1)S(1)} %slice_bitcast_fusion.2), channel_id=1, source_target_pairs={{0,8},{1,9},{2,10},{3,11},{4,12},{5,13},{6,14},{7,15},{8,0},{9,1},... | collective-permute-start | bytes 86024 | tf_op jit(solution)/shard_map/ppermute | solution.py:123
  63.5 7.6 %collective-permute-start.11 = (bf16[1,8,896]{2,1,0:T(8,128)(2,1)S(1)}, bf16[1,8,896]{2,1,0:T(8,128)(2,1)S(1)}, u32[]{:S(2)}, u32[]{:S(2)}) collective-permute-start(bf16[1,8,896]{2,1,0:T(8,128)(2,1)S(1)} %slice.98), channel_id=1, source_target_pairs={{0,16},{1,17},{2,18},{3,19},{4,20},{5,21},{6,22},{7,23},{8,24},{9,... | collective-permute-start | bytes 43016 | tf_op jit(solution)/shard_map/ppermute | solution.py:123

commit v2 on v0

--- a/solution.py
+++ b/solution.py
@@ -1,6 +1,8 @@
 import jax
 import jax.numpy as jnp
 from jax import lax
+from jax.experimental import pallas as pl
+from jax.experimental.pallas import tpu as pltpu
 from jax.sharding import PartitionSpec as P
 
 FF = 2560
@@ -37,7 +39,7 @@
     )
 
 
-def on_device(
+def general_device(
     tokens, cotangent, gate_prob, routes, slots, drop_seed, layer_id, w_gate, w_up, w_down
 ):
     experts = lax.axis_size("expert")
@@ -104,6 +106,346 @@
     return (grad_tokens, grad_gate[None], grad_up[None], grad_down[None])
 
 
+BF16 = jnp.bfloat16
+F32 = jnp.float32
+I32 = jnp.int32
+AXES = ("expert", "hid")
+LANES = 128
+HBM = pl.BlockSpec(memory_space=pltpu.HBM)
+VMEM = pl.BlockSpec(memory_space=pltpu.VMEM)
+SMEM = pl.BlockSpec(memory_space=pltpu.SMEM)
+
+
+def shape(dims, dtype=BF16):
+    return jax.ShapeDtypeStruct(dims, dtype)
+
+
+def call(kernel, ins, outs, out_shape, scratch=(), flops=0, moved=0, vmem=8):
+    return pl.pallas_call(
+        kernel,
+        in_specs=ins,
+        out_specs=outs,
+        out_shape=out_shape,
+        scratch_shapes=list(scratch),
+        compiler_params=pltpu.CompilerParams(vmem_limit_bytes=vmem * 1024 * 1024),
+        cost_estimate=pl.CostEstimate(flops=flops, bytes_accessed=moved, transcendentals=0),
+    )
+
+
+def swap(value, distance, size):
+    return lax.ppermute(value, AXES, [(i, i ^ distance) for i in range(size)])
+
+
+def logical(values, amount):
+    return lax.shift_right_logical(values, jnp.full(values.shape, amount, I32))
+
+
+def contract_last(left, right):
+    return lax.dot_general(
+        left, right, (((1,), (1,)), ((), ())), preferred_element_type=F32
+    )
+
+
+def columns(me, part, parts, width):
+    return pl.ds(pl.multiple_of(((me % parts) ^ part) * width, LANES), width)
+
+
+def pack(tokens, cotangent, gate_prob, routes, slots):
+    group, width = tokens.shape
+    top = gate_prob.shape[1]
+
+    def put(value, row, start):
+        stop = width + LANES - start - value.shape[1]
+        zero = jnp.zeros((), value.dtype)
+        return lax.pad(value[None], zero, ((row, 1 - row, 0), (0, 0, 0), (start, stop, 0)))
+
+    def rounded(value):
+        return lax.reduce_precision(value, 8, 7)
+
+    high, middle, low = (put(gate_prob, 0, width + i * top) for i in (2, 3, 4))
+    rest = low - rounded(low)
+    return (
+        put(tokens, 0, 0).astype(F32)
+        + put(cotangent, 1, 0).astype(F32)
+        + put(routes, 0, width).astype(F32)
+        + put(slots, 0, width + top).astype(F32)
+        + rounded(high)
+        + rounded(middle - rounded(middle))
+        + (rest - rounded(rest))
+    ).astype(BF16)
+
+
+def load_kernel(count, *refs):
+    sems = refs[-1]
+    copies = [
+        pltpu.make_async_copy(refs[i], refs[count + 1 + i], sems.at[i]) for i in range(count)
+    ]
+    for copy in copies:
+        copy.start()
+    for copy in copies:
+        copy.wait()
+
+
+def load(weights, after, vmem):
+    count = len(weights)
+    return call(
+        lambda *refs: load_kernel(count, *refs), [HBM] * count + [VMEM], [VMEM] * count,
+        [shape(w.shape) for w in weights], [pltpu.SemaphoreType.DMA((count,))],
+        moved=2 * count * weights[0].size, vmem=vmem,
+    )(*weights, after)
+
+
+def plan_kernel(bits, parts, top, place_ref, seed_ref, layer_ref, own_ref, other_ref, *refs):
+    gate_ref, base_ref = refs[-2:]
+    notes = jnp.concatenate([own_ref[...], other_ref[...]], axis=0).astype(F32)
+    rows = notes.shape[0]
+    group = rows >> bits
+    expert = place_ref[0] // parts
+    lane = lax.broadcasted_iota(I32, (rows, LANES), 1)
+
+    def field(i):
+        return pltpu.roll(notes, LANES - i * top, 1) if i else notes
+
+    slots = field(1)
+    chosen = (
+        (lane < top)
+        & (field(0) == jnp.full((rows, LANES), expert, I32).astype(F32))
+        & (slots < CAP_SRC)
+    )
+    gate = jnp.where(chosen, field(2) + field(3) + field(4), 0.0)
+    gate_ref[...] = jnp.sum(gate, axis=1, keepdims=True)
+    slot = jnp.sum(jnp.where(chosen, slots, 0.0), axis=1, keepdims=True).astype(I32)
+    position = lax.broadcasted_iota(I32, (rows, 1), 0) // group
+    offset = jnp.zeros((rows, 1), I32)
+    for b in range(bits):
+        offset = offset + (((position >> b) & 1) << (bits - 1 - b))
+    row_ids = (expert << bits) * CAP_SRC + (offset ^ expert) * CAP_SRC + slot
+    base_ref[...] = row_ids * FF * -1640531535 + seed_ref[0] * 40503 + layer_ref[0] * 97
+
+
+def pre_kernel(part, first, *refs):
+    place_ref, own_ref, other_ref, gate_ref, wg, wu, wd = refs[:7]
+    x_ref, dy_ref, acc_ref = refs[-3:]
+    width = own_ref.shape[2]
+    cols = columns(place_ref[0], part, wg.shape[1] // width, width)
+    x = jnp.concatenate([own_ref[0], other_ref[0]], axis=0)
+    c = jnp.concatenate([own_ref[1], other_ref[1]], axis=0)
+    dy = (gate_ref[...] * c.astype(F32)).astype(BF16)
+    x_ref[...] = x
+    dy_ref[...] = dy
+    for i, (left, weight) in enumerate(((x, wg), (x, wu), (dy, wd))):
+        term = contract_last(left, weight[:, cols])
+        acc_ref[i] = term if first else refs[7][i] + term
+
+
+def pieces(me, part_ids, g, u, wg, wu, keep_ref, send_ref):
+    _, half, width = keep_ref.shape
+    for i, part in enumerate(part_ids):
+        cols = columns(me, part, wg.shape[1] // width, width)
+        piece = (
+            jnp.dot(g, wg[:, cols], preferred_element_type=F32)
+            + jnp.dot(u, wu[:, cols], preferred_element_type=F32)
+        ).astype(BF16)
+        keep_ref[i] = piece[:half]
+        send_ref[i] = piece[half:]
+
+
+def hidden_kernel(
+    part_ids, place_ref, base_ref, acc_ref, wg, wu,
+    keep_ref, send_ref, g_ref, u_ref, hid_t_ref, g_t_ref, u_t_ref,
+):
+    me = place_ref[0]
+    _, rows, units = acc_ref.shape
+    width = keep_ref.shape[2]
+    unit_ids = (me % (wg.shape[1] // width)) * units + lax.broadcasted_iota(I32, (rows, units), 1)
+    mixed = base_ref[...] + unit_ids * -1640531535
+    mixed = mixed ^ logical(mixed, 15)
+    mixed = mixed * -2048144789
+    mixed = mixed ^ logical(mixed, 13)
+    mixed = mixed * -1028477387
+    mixed = mixed ^ logical(mixed, 16)
+    levels = logical(mixed, 8) & 1023
+    keep_mul = jnp.where(levels >= 102, KEEP_FACTOR, 0.0).astype(F32)
+    gate_pre = acc_ref[0]
+    up_pre = acc_ref[1]
+    grad_hidden = acc_ref[2] * keep_mul
+    logistic = jax.nn.sigmoid(gate_pre)
+    swish = gate_pre * logistic
+    upre = grad_hidden * swish
+    gpre = grad_hidden * up_pre * logistic * (1.0 + gate_pre * (1.0 - logistic))
+    g = gpre.astype(BF16)
+    u = upre.astype(BF16)
+    g_ref[...] = g
+    u_ref[...] = u
+    pieces(me, part_ids, g, u, wg, wu, keep_ref, send_ref)
+    hid_t_ref[...] = (swish * up_pre * keep_mul).T.astype(BF16)
+    g_t_ref[...] = gpre.T.astype(BF16)
+    u_t_ref[...] = upre.T.astype(BF16)
+
+
+def piece_kernel(part_ids, place_ref, g_ref, u_ref, wg, wu, keep_ref, send_ref):
+    pieces(place_ref[0], part_ids, g_ref[...], u_ref[...], wg, wu, keep_ref, send_ref)
+
+
+def weight_kernel(place_ref, left_ref, *refs):
+    rights, out_ref, held, sems = refs[:-3], refs[-3], refs[-2], refs[-1]
+    width = rights[0].shape[1]
+    copies = []
+    for j, right in enumerate(rights):
+        held[j] = jnp.dot(
+            left_ref[...], right[...], preferred_element_type=F32
+        ).astype(BF16)
+        copies.append(
+            pltpu.make_async_copy(
+                held.at[j], out_ref.at[:, columns(place_ref[0], j, len(rights), width)], sems.at[j]
+            )
+        )
+        copies[-1].start()
+    for copy in copies:
+        copy.wait()
+
+
+def weight_grad(place, left, rights):
+    parts = len(rights)
+    rows, width = rights[0].shape
+    units = left.shape[0]
+    return call(
+        weight_kernel, [SMEM, VMEM] + [VMEM] * parts, HBM, shape((units, parts * width)),
+        [pltpu.VMEM((parts, units, width), BF16), pltpu.SemaphoreType.DMA((parts,))],
+        flops=2 * units * rows * parts * width, moved=2 * units * parts * width, vmem=12,
+    )(place, left, *rights)
+
+
+def add(kept, came):
+    return (kept.astype(F32) + came.astype(F32)).astype(BF16)
+
+
+def token_device(
+    tokens, cotangent, gate_prob, routes, slots, drop_seed, layer_id, w_gate, w_up, w_down
+):
+    experts = lax.axis_size("expert")
+    parts = lax.axis_size("hid")
+    size = experts * parts
+    group, width = tokens.shape
+    top = gate_prob.shape[1]
+    units = w_gate.shape[1]
+    rows = experts * group
+    half = rows // 2
+    bits = experts.bit_length() - 1
+    place = lax.axis_index(AXES).astype(I32)[None]
+    wg, wu, wd = w_gate[0], w_up[0], w_down[0]
+    data = pack(tokens, cotangent, gate_prob, routes, slots)
+    data, place = lax.optimization_barrier((data, place))
+    distance = experts // 2
+    loads, loaded = [([wg], 48), ([wu, wd], 40)], []
+    while distance > 1:
+        came = swap(data, distance * parts, size)
+        if loads:
+            held = load(loads[0][0], data, loads[0][1])
+            came, *held = lax.optimization_barrier((came, *held))
+            loads, loaded = loads[1:], loaded + held
+        data = jnp.concatenate([data, came], axis=1)
+        distance //= 2
+    wg, wu, wd = loaded + [w for pair in loads for w in pair[0]]
+    notes = data[0, :, width:]
+    own = [data[:, :, :width]]
+    own += [swap(own[0], j, size) for j in range(1, parts)]
+    other_notes = swap(notes, parts, size)
+    gate, base = call(
+        lambda *refs: plan_kernel(bits, parts, top, *refs),
+        [SMEM] * 3 + [VMEM] * 2, [VMEM] * 2,
+        [shape((rows, 1), F32), shape((rows, 1), I32)],
+    )(place, drop_seed, layer_id, notes, other_notes)
+    xs, dys, acc = [None] * parts, [None] * parts, None
+    order = [0] + list(range(1, parts))[::-1]
+    order = order[:2] + order[2:][::-1]
+    others = [swap(own[0], parts, size)] + [None] * (parts - 1)
+    for n, j in enumerate(order):
+        held = [] if acc is None else [acc]
+        other = others[j]
+        xs[j], dys[j], acc = call(
+            lambda *refs, j=j, n=n: pre_kernel(j, n == 0, *refs),
+            [SMEM] + [VMEM] * (6 + len(held)), [VMEM] * 3,
+            [shape((rows, width)), shape((rows, width)), shape((3, rows, units), F32)],
+            flops=6 * rows * units * width, moved=6 * units * width,
+        )(place, own[j], other, gate, wg, wu, wd, *held)
+        if n == 0:
+            came = lax.optimization_barrier((acc, own[order[1]]))
+            acc, own[order[1]] = came
+            others[order[1]] = swap(own[order[1]], parts, size)
+        if n + 2 < parts:
+            i, k = order[n + 1], order[n + 2]
+            others[k] = swap(own[k], parts, size)
+            others[i], others[k] = others[i], others[k]
+    high = list(range(parts // 2, parts))
+    low = list(range(parts // 2))
+    block = shape((parts // 2, half, width))
+    turned = shape((units, rows))
+    straight = shape((rows, units))
+    flops = 4 * rows * units * width * (parts // 2)
+    keep, send, g, u, hid_t, g_t, u_t = call(
+        lambda *refs: hidden_kernel(high, *refs), [SMEM] + [VMEM] * 4, [VMEM] * 7,
+        [block, block, straight, straight, turned, turned, turned],
+        flops=flops, moved=2 * units * width * parts,
+    )(place, base, acc, wg, wu)
+    upper = add(keep, swap(send, parts, size))
+    keep, send = call(
+        lambda *refs: piece_kernel(low, *refs), [SMEM] + [VMEM] * 4, [VMEM] * 2,
+        [block, block], flops=flops, moved=2 * units * width * parts,
+    )(place, g, u, wg, wu)
+    lower = add(keep, swap(send, parts, size))
+    lefts, rights, grads = [hid_t, g_t, u_t], [dys, xs, xs], []
+
+    def exchange(kept, sent, distance):
+        if len(grads) == len(lefts):
+            return add(kept, swap(sent, distance, size))
+        i = len(grads)
+        sent, left = lax.optimization_barrier((sent, lefts[i]))
+        came = swap(sent, distance, size)
+        grad = weight_grad(place, left, rights[i])
+        came, grad = lax.optimization_barrier((came, grad))
+        grads.append(grad)
+        return add(kept, came)
+
+    part = exchange(lower, upper, parts // 2)
+    distance = parts // 4
+    while distance:
+        count = part.shape[0] // 2
+        part = exchange(part[:count], part[count:], distance)
+        distance //= 2
+    part = part[0].reshape(experts // 2, group, width)
+    distance = 2
+    while distance < experts:
+        count = part.shape[0] // 2
+        part = exchange(part[:count], part[count:], distance * parts)
+        distance *= 2
+    for i in range(len(grads), len(lefts)):
+        grads.append(weight_grad(place, lefts[i], rights[i]))
+    grad_down, grad_gate, grad_up = grads
+    return (part[0], grad_gate[None], grad_up[None], grad_down[None])
+
+
+def power_of_two(number):
+    return number & (number - 1) == 0
+
+
+def on_device(*args):
+    tokens, gate_prob, w_gate = args[0], args[2], args[7]
+    experts = lax.axis_size("expert")
+    parts = lax.axis_size("hid")
+    few = tokens.shape[0] <= CAP_SRC and experts <= 256
+    noted = 5 * gate_prob.shape[1] <= LANES
+    even = power_of_two(experts) and power_of_two(parts) and experts > 1 and parts > 1
+    tiled = (
+        tokens.shape[0] % 8 == 0
+        and tokens.shape[1] % LANES == 0
+        and w_gate.shape[1] % LANES == 0
+    )
+    if few and noted and even and tiled:
+        return token_device(*args)
+    return general_device(*args)
+
+
 def solution(mesh):
     in_specs = (
         P("expert", "hid"),

time: 132 us -> 47.2 us (0.36)
  waiting for transfers between devices: 47 us -> 5.38 us
  matrix products: 22.2 us -> 0 us
  blocking collectives: 20.5 us -> 0 us
  Pallas kernels: 0 us -> 20 us
  between operations: 15.5 us -> 2.19 us
  other arithmetic: 8.46 us -> 1.61 us
  starting transfers between devices: 14.3 us -> 17.7 us
  local copies, waits for them, and re-layouts: 3.23 us -> 0.06 us
    psum x1 -> x0, waiting for transfers between devices: 39.2 us -> none  [on_device(): lax.psum(partial_sum.astype(jnp.bfloat16), 'hid').astype(jnp.float32)]
    dot_general x11 -> x0, matrix products: 22.2 us -> none  [the longest x4 11.4 us: contract_rows(): lax.dot_general(left, right, (((0,), (0,)), ((), ())), preferred_element_...]
    all_gather x2 -> x0, blocking collectives: 20.5 us -> none  [the longest x1 10.3 us: on_device(): lax.all_gather(recv_x.reshape(capacity, part_width), 'hid', axis=1, tiled...]
    pallas_call x0 -> x12, Pallas kernels: none -> 20 us  [the longest x3 7.93 us: weight_grad(): call(weight_kernel, [SMEM, VMEM] + [VMEM] * parts, HBM, shape((units, par...]
    ppermute x0 -> x16, starting transfers between devices: none -> 17.7 us  [swap(): return lax.ppermute(value, AXES, [(i, i ^ distance) for i in range(size)])]
    all_to_all x3 -> x0, starting transfers between devices: 14.3 us -> none  [the longest x1 6.32 us: on_device(): lax.all_to_all(sent_dy.reshape(send_shape), 'expert', split_axis=0, conca...]
    all_to_all x3 -> x0, waiting for transfers between devices: 7.8 us -> none  [the longest x1 5.57 us: on_device(): lax.all_to_all(sent_x.reshape(send_shape), 'expert', split_axis=0, concat...]
    all_to_all x6 -> x0, other arithmetic: 5.95 us -> none  [the longest x2 2.01 us: on_device(): lax.all_to_all(sent_x.reshape(send_shape), 'expert', split_axis=0, concat...]
  transfers between devices with their start and end apart: 4 -> 16, of which waited for: 3 -> 5; matrix products, arithmetic and copies ran while one was open for 11% -> 0% of each run, Pallas kernels for 0% -> 38%
where the time goes in v2:
time: 47.2 us; the launch traced here: 47 us
  Pallas kernels  20 us (42%)
  starting transfers between devices  17.7 us (38%)
  waiting for transfers between devices  5.38 us (11%)
  between operations  2.19 us (5%)
  other arithmetic  1.61 us (3%)
    ppermute x16, starting transfers between devices, swap(): return lax.ppermute(value, AXES, [(i, i ^ distance) for i in range(size)])  17.7 us
    pallas_call x3, Pallas kernels, weight_grad(): call(weight_kernel, [SMEM, VMEM] + [VMEM] * parts, HBM, shape((units, par...  7.93 us
    ppermute x16, waiting for transfers between devices, swap(): return lax.ppermute(value, AXES, [(i, i ^ distance) for i in range(size)])  5.38 us
    pallas_call x2, Pallas kernels, load(): call(lambda *refs: load_kernel(count, *refs), [HBM] * count + [VMEM], [VM...  5.25 us
    pallas_call x4, Pallas kernels, token_device(): call(lambda *refs, j=j, n=n: pre_kernel(j, n == 0, *refs), [SMEM] + [VMEM...  4.83 us
    pallas_call x1, Pallas kernels, token_device(): call(lambda *refs: hidden_kernel(high, *refs), [SMEM] + [VMEM] * 4, [VMEM...  1 us
  transfers between devices with their start and end apart: 16, of which 5 were waited for; matrix products, arithmetic and copies ran while one was open for 0% of the time, Pallas kernels for 38%

profile of v2, /device:TPU:0, one launch (start us, length us, event | category | flops | bytes accessed | tf_op | source)
XLA Modules:
  0.0 47.0 jit_solution(17634544535798667691)
XLA Ops:
  0.6 0.9 %fusion.3.refs_1_ = bf16[2,8,1024]{2,1,0:T(8,128)(2,1)S(1)} fusion(f32[1,8,8]{2,1,0:T(8,128)} %bitcast.33, s32[1,8,8]{2,1,0:T(8,128)} %bitcast.34, s32[1,8,8]{2,1,0:T(8,128)} %bitcast.35, bf16[1,8,896]{2,1,0:T(8,128)(2,1)} %bitcast.31, bf16[1,8,896]{2,1,0:T(8,128)(2,1)} %bitcast.32), kind=kLoop, calls=%fused_computation.10 | loop fusion | flops 311296 | bytes 62208 | tf_op jit(solution)/shard_map/convert_element_type | solution.py:175
  1.5 4.0 %collective-permute-start = (bf16[2,8,1024]{2,1,0:T(8,128)(2,1)S(1)}, bf16[2,8,1024]{2,1,0:T(8,128)(2,1)S(1)}, u32[]{:S(2)}, u32[]{:S(2)}) collective-permute-start(bf16[2,8,1024]{2,1,0:T(8,128)(2,1)S(1)} %fusion.3.refs_1_), channel_id=1, source_target_pairs={{0,16},{1,17},{2,18},{3,19},{4,20},{5,21},{6,22},{7,23},{8,24},{9,... | collective-permute-start | bytes 98312 | tf_op jit(solution)/shard_map/ppermute | solution.py:136
  5.6 2.5 %shard_map.129.refs_4_.refs_3_ = bf16[640,3584]{1,0:T(8,128)(2,1)S(1)} custom-call(bf16[640,3584]{1,0:T(8,128)(2,1)} %bitcast.26, bf16[2,8,1024]{2,1,0:T(8,128)(2,1)S(1)} %fusion.3.refs_1_), custom_call_target="tpu_custom_call" | custom-call | bytes 4587520 | tf_op jit(solution)/shard_map/pallas_call | solution.py:191
  8.1 1.6 %collective-permute-start.1 = (bf16[2,16,1024]{2,1,0:T(8,128)(2,1)S(1)}, bf16[2,16,1024]{2,1,0:T(8,128)(2,1)S(1)}, u32[]{:S(2)}, u32[]{:S(2)}) collective-permute-start(bf16[2,16,1024]{2,1,0:T(8,128)(2,1)S(1)} %get-tuple-element.96.refs_2_), channel_id=1, source_target_pairs={{0,8},{1,9},{2,10},{3,11},{4,12},{5,13},{6,14},{7,15},{8,0},{9,1},... | collective-permute-start | bytes 196616 | tf_op jit(solution)/shard_map/ppermute | solution.py:136
  9.7 2.8 %shard_map.130 = (bf16[640,3584]{1,0:T(8,128)(2,1)S(1)}, bf16[640,3584]{1,0:T(8,128)(2,1)S(1)}) custom-call(bf16[640,3584]{1,0:T(8,128)(2,1)S(1)} %bitcast.25, bf16[640,3584]{1,0:T(8,128)(2,1)} %bitcast.27, bf16[2,16,1024]{2,1,0:T(8,128)(2,1)S(1)} %get-tuple-element.96.refs_2_), custom_call_target="tpu_custom_call" | custom-call | bytes 9175040 | tf_op jit(solution)/shard_map/pallas_call | solution.py:191
  12.6 2.5 %collective-permute-start.8 = (bf16[2,32,896]{2,1,0:T(8,128)(2,1)S(1)}, bf16[2,32,896]{2,1,0:T(8,128)(2,1)S(1)}, u32[]{:S(2)}, u32[]{:S(2)}) collective-permute-start(bf16[2,32,896]{2,1,0:T(8,128)(2,1)S(1)} %slice.38.refs_1_), channel_id=1, source_target_pairs={{0,3},{1,2},{2,1},{3,0},{4,7},{5,6},{6,5},{7,4},{8,11},{9,10},{10,... | collective-permute-start | bytes 344072 | tf_op jit(solution)/shard_map/ppermute | solution.py:136
  17.6 1.2 %shard_map.132 = (bf16[64,896]{1,0:T(8,128)(2,1)S(1)}, bf16[64,896]{1,0:T(8,128)(2,1)S(1)}, f32[3,64,640]{2,1,0:T(8,128)S(1)}) custom-call(s32[1]{0:T(128)} %bitcast.5.refs_0_.place_ref, bf16[2,32,896]{2,1,0:T(8,128)(2,1)S(1)} %slice.38.refs_1_, bf16[2,32,896]{2,1,0:T(8,128)(2,1)S(1)} %collective-permute-done.7.refs_2_, ...), custom_call_target="tpu_custom_call" | custom-call | flops 220200960 | bytes 3440640 | tf_op jit(solution)/shard_map/pallas_call | solution.py:366
  18.9 0.6 %collective-permute-start.9 = (bf16[2,32,896]{2,1,0:T(8,128)(2,1)S(1)}, bf16[2,32,896]{2,1,0:T(8,128)(2,1)S(1)}, u32[]{:S(2)}, u32[]{:S(2)}) collective-permute-start(bf16[2,32,896]{2,1,0:T(8,128)(2,1)S(1)} %collective-permute-done.8.refs_1_), channel_id=1, source_target_pairs={{0,4},{1,5},{2,6},{3,7},{4,0},{5,1},{6,2},{7,3},{8,12},{9,13},{10,... | collective-permute-start | bytes 344072 | tf_op jit(solution)/shard_map/ppermute | solution.py:136
  19.4 1.4 %collective-permute-done.5.refs_1_ = bf16[2,32,896]{2,1,0:T(8,128)(2,1)S(1)} collective-permute-done((bf16[2,32,896]{2,1,0:T(8,128)(2,1)S(1)}, bf16[2,32,896]{2,1,0:T(8,128)(2,1)S(1)}, u32[]{:S(2)}, u32[]{:S(2)}) %collective-permute-start.5) | collective-permute-done | bytes 114720 | tf_op jit(solution)/shard_map/ppermute | solution.py:136
  21.4 1.2 %shard_map.133 = (bf16[64,896]{1,0:T(8,128)(2,1)S(1)}, bf16[64,896]{1,0:T(8,128)(2,1)S(1)}, f32[3,64,640]{2,1,0:T(8,128)S(1)}) custom-call(s32[1]{0:T(128)} %bitcast.5.refs_0_.place_ref, bf16[2,32,896]{2,1,0:T(8,128)(2,1)S(1)} %collective-permute-done.8.refs_1_, bf16[2,32,896]{2,1,0:T(8,128)(2,1)S(1)} %collective-permute-done.9.refs_2_, ...), custom_call_target="tpu_custom_call" | custom-call | flops 220200960 | bytes 3440640 | tf_op jit(solution)/shard_map/pallas_call | solution.py:366
  22.6 1.2 %shard_map.134 = (bf16[64,896]{1,0:T(8,128)(2,1)S(1)}, bf16[64,896]{1,0:T(8,128)(2,1)S(1)}, f32[3,64,640]{2,1,0:T(8,128)S(1)}) custom-call(s32[1]{0:T(128)} %bitcast.5.refs_0_.place_ref, bf16[2,32,896]{2,1,0:T(8,128)(2,1)S(1)} %collective-permute-done.5.refs_1_, bf16[2,32,896]{2,1,0:T(8,128)(2,1)S(1)} %collective-permute-done.6.refs_2_, ...), custom_call_target="tpu_custom_call" | custom-call | flops 220200960 | bytes 3440640 | tf_op jit(solution)/shard_map/pallas_call | solution.py:366
  23.8 1.2 %shard_map.135 = (bf16[64,896]{1,0:T(8,128)(2,1)S(1)}, bf16[64,896]{1,0:T(8,128)(2,1)S(1)}, f32[3,64,640]{2,1,0:T(8,128)S(1)}) custom-call(s32[1]{0:T(128)} %bitcast.5.refs_0_.place_ref, bf16[2,32,896]{2,1,0:T(8,128)(2,1)S(1)} %collective-permute-done.3.refs_1_, bf16[2,32,896]{2,1,0:T(8,128)(2,1)S(1)} %collective-permute-done.4.refs_2_, ...), custom_call_target="tpu_custom_call" | custom-call | flops 220200960 | bytes 3440640 | tf_op jit(solution)/shard_map/pallas_call | solution.py:366
  25.0 1.0 %shard_map.136 = (bf16[2,32,896]{2,1,0:T(8,128)(2,1)S(1)}, bf16[2,32,896]{2,1,0:T(8,128)(2,1)S(1)}, bf16[64,640]{1,0:T(8,128)(2,1)S(1)}, bf16[64,640]{1,0:T(8,12...) custom-call(s32[1]{0:T(128)} %bitcast.5.refs_0_.place_ref, ...), custom_call_target="tpu_custom_call" | custom-call | flops 293601280 | bytes 4587520 | tf_op jit(solution)/shard_map/pallas_call | solution.py:386
  26.2 1.2 %collective-permute-done.11 = bf16[2,32,896]{2,1,0:T(8,128)(2,1)S(1)} collective-permute-done((bf16[2,32,896]{2,1,0:T(8,128)(2,1)S(1)}, bf16[2,32,896]{2,1,0:T(8,128)(2,1)S(1)}, u32[]{:S(2)}, u32[]{:S(2)}) %collective-permute-start.11) | collective-permute-done | bytes 114720 | tf_op jit(solution)/shard_map/ppermute | solution.py:136
  27.5 1.2 %collective-permute-start.12 = (bf16[2,32,896]{2,1,0:T(8,128)(2,1)S(1)}, bf16[2,32,896]{2,1,0:T(8,128)(2,1)S(1)}, u32[]{:S(2)}, u32[]{:S(2)}) collective-permute-start(bf16[2,32,896]{2,1,0:T(8,128)(2,1)S(1)} %add_convert_fusion.1), channel_id=1, source_target_pairs={{0,2},{1,3},{2,0},{3,1},{4,6},{5,7},{6,4},{7,5},{8,10},{9,11},{10,... | collective-permute-start | bytes 344072 | tf_op jit(solution)/shard_map/ppermute | solution.py:136
  28.6 0.8 %shard_map.137 = (bf16[2,32,896]{2,1,0:T(8,128)(2,1)S(1)}, bf16[2,32,896]{2,1,0:T(8,128)(2,1)S(1)}) custom-call(s32[1]{0:T(128)} %bitcast.5.refs_0_.place_ref, bf16[64,640]{1,0:T(8,128)(2,1)S(1)} %get-tuple-element.67.refs_1_, bf16[64,640]{1,0:T(8,128)(2,1)S(1)} %get-tuple-element.68.refs_2_, bf16[640,3584]{1,0:T(8,128)(2,1)S(1)} %shard_map.129.refs_4_.refs_3_, ...), custom_call_target="tpu_custom_call" | custom-call | flops 293601280 | bytes 4587520 | tf_op jit(solution)/shard_map/pallas_call | solution.py:392
  29.6 2.6 %shard_map.138 = bf16[640,3584]{1,0:T(8,128)(2,1)} custom-call(s32[1]{0:T(128)} %bitcast.5.refs_0_.place_ref, bf16[640,64]{1,0:T(8,128)(2,1)S(1)} %get-tuple-element.75.left_ref, bf16[64,896]{1,0:T(8,128)(2,1)S(1)} %get-tuple-element.76.refs_0_, bf16[64,896]{1,0:T(8,128)(2,1)S(1)} %get-tuple-element.77.refs_1_, ...), custom_call_target="tpu_custom_call" | custom-call | flops 293601280 | bytes 4587520 | tf_op jit(solution)/shard_map/pallas_call | solution.py:312
  32.8 2.0 %collective-permute-start.13 = (bf16[1,32,896]{2,1,0:T(8,128)(2,1)S(1)}, bf16[1,32,896]{2,1,0:T(8,128)(2,1)S(1)}, u32[]{:S(2)}, u32[]{:S(2)}) collective-permute-start(bf16[1,32,896]{2,1,0:T(8,128)(2,1)S(1)} %slice.40), channel_id=1, source_target_pairs={{0,1},{1,0},{2,3},{3,2},{4,5},{5,4},{6,7},{7,6},{8,9},{9,8},{10,11... | collective-permute-start | bytes 172040 | tf_op jit(solution)/shard_map/ppermute | solution.py:136
  34.8 2.6 %shard_map.139 = bf16[640,3584]{1,0:T(8,128)(2,1)} custom-call(s32[1]{0:T(128)} %bitcast.5.refs_0_.place_ref, bf16[640,64]{1,0:T(8,128)(2,1)S(1)} %get-tuple-element.83.left_ref, bf16[64,896]{1,0:T(8,128)(2,1)S(1)} %get-tuple-element.84.refs_0_, bf16[64,896]{1,0:T(8,128)(2,1)S(1)} %get-tuple-element.85.refs_1_, ...), custom_call_target="tpu_custom_call" | custom-call | flops 293601280 | bytes 4587520 | tf_op jit(solution)/shard_map/pallas_call | solution.py:312
  37.5 1.5 %collective-permute-start.14 = (bf16[2,8,896]{2,1,0:T(8,128)(2,1)S(1)}, bf16[2,8,896]{2,1,0:T(8,128)(2,1)S(1)}, u32[]{:S(2)}, u32[]{:S(2)}) collective-permute-start(bf16[2,8,896]{2,1,0:T(8,128)(2,1)S(1)} %slice_bitcast_fusion), channel_id=1, source_target_pairs={{0,8},{1,9},{2,10},{3,11},{4,12},{5,13},{6,14},{7,15},{8,0},{9,1},... | collective-permute-start | bytes 86024 | tf_op jit(solution)/shard_map/ppermute | solution.py:136
  39.0 2.6 %shard_map.140 = bf16[640,3584]{1,0:T(8,128)(2,1)} custom-call(s32[1]{0:T(128)} %bitcast.5.refs_0_.place_ref, bf16[640,64]{1,0:T(8,128)(2,1)S(1)} %get-tuple-element.91.left_ref, bf16[64,896]{1,0:T(8,128)(2,1)S(1)} %get-tuple-element.84.refs_0_, bf16[64,896]{1,0:T(8,128)(2,1)S(1)} %get-tuple-element.85.refs_1_, ...), custom_call_target="tpu_custom_call" | custom-call | flops 293601280 | bytes 4587520 | tf_op jit(solution)/shard_map/pallas_call | solution.py:312
  41.7 2.5 %collective-permute-start.15 = (bf16[1,8,896]{2,1,0:T(8,128)(2,1)S(1)}, bf16[1,8,896]{2,1,0:T(8,128)(2,1)S(1)}, u32[]{:S(2)}, u32[]{:S(2)}) collective-permute-start(bf16[1,8,896]{2,1,0:T(8,128)(2,1)S(1)} %slice.44), channel_id=1, source_target_pairs={{0,16},{1,17},{2,18},{3,19},{4,20},{5,21},{6,22},{7,23},{8,24},{9,... | collective-permute-start | bytes 43016 | tf_op jit(solution)/shard_map/ppermute | solution.py:136
  44.2 2.1 %collective-permute-done.15 = bf16[1,8,896]{2,1,0:T(8,128)(2,1)S(1)} collective-permute-done((bf16[1,8,896]{2,1,0:T(8,128)(2,1)S(1)}, bf16[1,8,896]{2,1,0:T(8,128)(2,1)S(1)}, u32[]{:S(2)}, u32[]{:S(2)}) %collective-permute-start.15) | collective-permute-done | bytes 14368 | tf_op jit(solution)/shard_map/ppermute | solution.py:136
  46.4 0.6 %fusion.5 = bf16[8,896]{1,0:T(8,128)(2,1)} fusion(bf16[1,8,896]{2,1,0:T(8,128)(2,1)S(1)} %collective-permute-done.15, bf16[2,8,896]{2,1,0:T(8,128)(2,1)S(1)} %fusion.4), kind=kLoop, calls=%fused_computation.16 | loop fusion | flops 28672 | bytes 43008 | tf_op jit(solution)/shard_map/squeeze | solution.py:425
  (39 shorter events, 2.7 us)
Async XLA Ops:
  1.5 6.5 %collective-permute-start = (bf16[2,8,1024]{2,1,0:T(8,128)(2,1)S(1)}, bf16[2,8,1024]{2,1,0:T(8,128)(2,1)S(1)}, u32[]{:S(2)}, u32[]{:S(2)}) collective-permute-start(bf16[2,8,1024]{2,1,0:T(8,128)(2,1)S(1)} %fusion.3.refs_1_), channel_id=1, source_target_pairs={{0,16},{1,17},{2,18},{3,19},{4,20},{5,21},{6,22},{7,23},{8,24},{9,... | collective-permute-start | bytes 98312 | tf_op jit(solution)/shard_map/ppermute | solution.py:136
  5.6 4.2 %slice-start = ((s8[4587520]{0:T(1024)(128)(4,1)}), s8[4194304]{0:T(1024)(128)(4,1)S(1)}, s32[]{:S(2)}) async-start(s8[4587520]{0:T(1024)(128)(4,1)} %bitcast.23), calls=%async_computation | async-start | bytes 8388608
  5.6 4.2 %slice-start.1 = ((s8[4587520]{0:T(1024)(128)(4,1)}), s8[393216]{0:T(1024)(128)(4,1)S(1)}, s32[]{:S(2)}) async-start(s8[4587520]{0:T(1024)(128)(4,1)} %bitcast.23), calls=%async_computation.1 | async-start | bytes 786432
  8.1 4.4 %collective-permute-start.1 = (bf16[2,16,1024]{2,1,0:T(8,128)(2,1)S(1)}, bf16[2,16,1024]{2,1,0:T(8,128)(2,1)S(1)}, u32[]{:S(2)}, u32[]{:S(2)}) collective-permute-start(bf16[2,16,1024]{2,1,0:T(8,128)(2,1)S(1)} %get-tuple-element.96.refs_2_), channel_id=1, source_target_pairs={{0,8},{1,9},{2,10},{3,11},{4,12},{5,13},{6,14},{7,15},{8,0},{9,1},... | collective-permute-start | bytes 196616 | tf_op jit(solution)/shard_map/ppermute | solution.py:136
  12.6 6.3 %collective-permute-start.8 = (bf16[2,32,896]{2,1,0:T(8,128)(2,1)S(1)}, bf16[2,32,896]{2,1,0:T(8,128)(2,1)S(1)}, u32[]{:S(2)}, u32[]{:S(2)}) collective-permute-start(bf16[2,32,896]{2,1,0:T(8,128)(2,1)S(1)} %slice.38.refs_1_), channel_id=1, source_target_pairs={{0,3},{1,2},{2,1},{3,0},{4,7},{5,6},{6,5},{7,4},{8,11},{9,10},{10,... | collective-permute-start | bytes 344072 | tf_op jit(solution)/shard_map/ppermute | solution.py:136
  15.1 2.5 %collective-permute-start.7 = (bf16[2,32,896]{2,1,0:T(8,128)(2,1)S(1)}, bf16[2,32,896]{2,1,0:T(8,128)(2,1)S(1)}, u32[]{:S(2)}, u32[]{:S(2)}) collective-permute-start(bf16[2,32,896]{2,1,0:T(8,128)(2,1)S(1)} %slice.38.refs_1_), channel_id=1, source_target_pairs={{0,4},{1,5},{2,6},{3,7},{4,0},{5,1},{6,2},{7,3},{8,12},{9,13},{10,... | collective-permute-start | bytes 344072 | tf_op jit(solution)/shard_map/ppermute | solution.py:136
  15.1 5.8 %collective-permute-start.5 = (bf16[2,32,896]{2,1,0:T(8,128)(2,1)S(1)}, bf16[2,32,896]{2,1,0:T(8,128)(2,1)S(1)}, u32[]{:S(2)}, u32[]{:S(2)}) collective-permute-start(bf16[2,32,896]{2,1,0:T(8,128)(2,1)S(1)} %slice.38.refs_1_), channel_id=1, source_target_pairs={{0,1},{1,0},{2,3},{3,2},{4,5},{5,4},{6,7},{7,6},{8,9},{9,8},{10,11... | collective-permute-start | bytes 344072 | tf_op jit(solution)/shard_map/ppermute | solution.py:136
  15.6 5.3 %collective-permute-start.3 = (bf16[2,32,896]{2,1,0:T(8,128)(2,1)S(1)}, bf16[2,32,896]{2,1,0:T(8,128)(2,1)S(1)}, u32[]{:S(2)}, u32[]{:S(2)}) collective-permute-start(bf16[2,32,896]{2,1,0:T(8,128)(2,1)S(1)} %slice.38.refs_1_), channel_id=1, source_target_pairs={{0,2},{1,3},{2,0},{3,1},{4,6},{5,7},{6,4},{7,5},{8,10},{9,11},{10,... | collective-permute-start | bytes 344072 | tf_op jit(solution)/shard_map/ppermute | solution.py:136
  16.1 1.3 %collective-permute-start.2 = (bf16[32,128]{1,0:T(8,128)(2,1)S(1)}, bf16[32,128]{1,0:T(8,128)(2,1)S(1)}, u32[]{:S(2)}, u32[]{:S(2)}) collective-permute-start(bf16[32,128]{1,0:T(8,128)(2,1)S(1)} %slice_bitcast_fusion.2.refs_3_), channel_id=1, source_target_pairs={{0,4},{1,5},{2,6},{3,7},{4,0},{5,1},{6,2},{7,3},{8,12},{9,13},{10,... | collective-permute-start | bytes 24584 | tf_op jit(solution)/shard_map/ppermute | solution.py:136
  18.9 2.5 %collective-permute-start.9 = (bf16[2,32,896]{2,1,0:T(8,128)(2,1)S(1)}, bf16[2,32,896]{2,1,0:T(8,128)(2,1)S(1)}, u32[]{:S(2)}, u32[]{:S(2)}) collective-permute-start(bf16[2,32,896]{2,1,0:T(8,128)(2,1)S(1)} %collective-permute-done.8.refs_1_), channel_id=1, source_target_pairs={{0,4},{1,5},{2,6},{3,7},{4,0},{5,1},{6,2},{7,3},{8,12},{9,13},{10,... | collective-permute-start | bytes 344072 | tf_op jit(solution)/shard_map/ppermute | solution.py:136
  20.9 1.7 %collective-permute-start.6 = (bf16[2,32,896]{2,1,0:T(8,128)(2,1)S(1)}, bf16[2,32,896]{2,1,0:T(8,128)(2,1)S(1)}, u32[]{:S(2)}, u32[]{:S(2)}) collective-permute-start(bf16[2,32,896]{2,1,0:T(8,128)(2,1)S(1)} %collective-permute-done.5.refs_1_), channel_id=1, source_target_pairs={{0,4},{1,5},{2,6},{3,7},{4,0},{5,1},{6,2},{7,3},{8,12},{9,13},{10,... | collective-permute-start | bytes 344072 | tf_op jit(solution)/shard_map/ppermute | solution.py:136
  20.9 2.9 %collective-permute-start.4 = (bf16[2,32,896]{2,1,0:T(8,128)(2,1)S(1)}, bf16[2,32,896]{2,1,0:T(8,128)(2,1)S(1)}, u32[]{:S(2)}, u32[]{:S(2)}) collective-permute-start(bf16[2,32,896]{2,1,0:T(8,128)(2,1)S(1)} %collective-permute-done.3.refs_1_), channel_id=1, source_target_pairs={{0,4},{1,5},{2,6},{3,7},{4,0},{5,1},{6,2},{7,3},{8,12},{9,13},{10,... | collective-permute-start | bytes 344072 | tf_op jit(solution)/shard_map/ppermute | solution.py:136
  26.0 1.4 %collective-permute-start.11 = (bf16[2,32,896]{2,1,0:T(8,128)(2,1)S(1)}, bf16[2,32,896]{2,1,0:T(8,128)(2,1)S(1)}, u32[]{:S(2)}, u32[]{:S(2)}) collective-permute-start(bf16[2,32,896]{2,1,0:T(8,128)(2,1)S(1)} %get-tuple-element.72), channel_id=1, source_target_pairs={{0,4},{1,5},{2,6},{3,7},{4,0},{5,1},{6,2},{7,3},{8,12},{9,13},{10,... | collective-permute-start | bytes 344072 | tf_op jit(solution)/shard_map/ppermute | solution.py:136
  27.5 5.3 %collective-permute-start.12 = (bf16[2,32,896]{2,1,0:T(8,128)(2,1)S(1)}, bf16[2,32,896]{2,1,0:T(8,128)(2,1)S(1)}, u32[]{:S(2)}, u32[]{:S(2)}) collective-permute-start(bf16[2,32,896]{2,1,0:T(8,128)(2,1)S(1)} %add_convert_fusion.1), channel_id=1, source_target_pairs={{0,2},{1,3},{2,0},{3,1},{4,6},{5,7},{6,4},{7,5},{8,10},{9,11},{10,... | collective-permute-start | bytes 344072 | tf_op jit(solution)/shard_map/ppermute | solution.py:136
  29.5 3.3 %collective-permute-start.10 = (bf16[2,32,896]{2,1,0:T(8,128)(2,1)S(1)}, bf16[2,32,896]{2,1,0:T(8,128)(2,1)S(1)}, u32[]{:S(2)}, u32[]{:S(2)}) collective-permute-start(bf16[2,32,896]{2,1,0:T(8,128)(2,1)S(1)} %get-tuple-element.70), channel_id=1, source_target_pairs={{0,4},{1,5},{2,6},{3,7},{4,0},{5,1},{6,2},{7,3},{8,12},{9,13},{10,... | collective-permute-start | bytes 344072 | tf_op jit(solution)/shard_map/ppermute | solution.py:136
  32.8 4.6 %collective-permute-start.13 = (bf16[1,32,896]{2,1,0:T(8,128)(2,1)S(1)}, bf16[1,32,896]{2,1,0:T(8,128)(2,1)S(1)}, u32[]{:S(2)}, u32[]{:S(2)}) collective-permute-start(bf16[1,32,896]{2,1,0:T(8,128)(2,1)S(1)} %slice.40), channel_id=1, source_target_pairs={{0,1},{1,0},{2,3},{3,2},{4,5},{5,4},{6,7},{7,6},{8,9},{9,8},{10,11... | collective-permute-start | bytes 172040 | tf_op jit(solution)/shard_map/ppermute | solution.py:136
  37.5 4.2 %collective-permute-start.14 = (bf16[2,8,896]{2,1,0:T(8,128)(2,1)S(1)}, bf16[2,8,896]{2,1,0:T(8,128)(2,1)S(1)}, u32[]{:S(2)}, u32[]{:S(2)}) collective-permute-start(bf16[2,8,896]{2,1,0:T(8,128)(2,1)S(1)} %slice_bitcast_fusion), channel_id=1, source_target_pairs={{0,8},{1,9},{2,10},{3,11},{4,12},{5,13},{6,14},{7,15},{8,0},{9,1},... | collective-permute-start | bytes 86024 | tf_op jit(solution)/shard_map/ppermute | solution.py:136
  41.7 4.7 %collective-permute-start.15 = (bf16[1,8,896]{2,1,0:T(8,128)(2,1)S(1)}, bf16[1,8,896]{2,1,0:T(8,128)(2,1)S(1)}, u32[]{:S(2)}, u32[]{:S(2)}) collective-permute-start(bf16[1,8,896]{2,1,0:T(8,128)(2,1)S(1)} %slice.44), channel_id=1, source_target_pairs={{0,16},{1,17},{2,18},{3,19},{4,20},{5,21},{6,22},{7,23},{8,24},{9,... | collective-permute-start | bytes 43016 | tf_op jit(solution)/shard_map/ppermute | solution.py:136

commit v3 on v2

--- a/solution.py
+++ b/solution.py
@@ -287,37 +287,69 @@
     pieces(place_ref[0], part_ids, g_ref[...], u_ref[...], wg, wu, keep_ref, send_ref)
 
 
-def weight_kernel(place_ref, left_ref, *refs):
-    rights, out_ref, held, sems = refs[:-3], refs[-3], refs[-2], refs[-1]
-    width = rights[0].shape[1]
-    copies = []
-    for j, right in enumerate(rights):
-        held[j] = jnp.dot(
-            left_ref[...], right[...], preferred_element_type=F32
-        ).astype(BF16)
-        copies.append(
-            pltpu.make_async_copy(
-                held.at[j], out_ref.at[:, columns(place_ref[0], j, len(rights), width)], sems.at[j]
-            )
-        )
-        copies[-1].start()
+def weight_kernel(jobs, parts, cuts, place_ref, *refs):
+    outs, held, sems = refs[-len(jobs) - 2:-2], refs[-2], refs[-1]
+    units, width = held.shape[1:]
+    copies, n, at = [], 0, 0
+    for out, ids in zip(outs, jobs):
+        left = refs[at]
+        for k, j in enumerate(ids):
+            cols = columns(place_ref[0], j, parts, width)
+            step = units // (cuts if n == 0 else 1)
+            for r in range(0, units, step):
+                rows = slice(r, r + step)
+                held[n, rows] = jnp.dot(
+                    left[rows], refs[at + 1 + k][...], preferred_element_type=F32
+                ).astype(BF16)
+                copies.append(
+                    pltpu.make_async_copy(
+                        held.at[n, rows], out.at[rows, cols], sems.at[len(copies)]
+                    )
+                )
+                copies[-1].start()
+            n += 1
+        at += 1 + len(ids)
     for copy in copies:
         copy.wait()
 
 
-def weight_grad(place, left, rights):
-    parts = len(rights)
-    rows, width = rights[0].shape
-    units = left.shape[0]
-    return call(
-        weight_kernel, [SMEM, VMEM] + [VMEM] * parts, HBM, shape((units, parts * width)),
-        [pltpu.VMEM((parts, units, width), BF16), pltpu.SemaphoreType.DMA((parts,))],
-        flops=2 * units * rows * parts * width, moved=2 * units * parts * width, vmem=12,
-    )(place, left, *rights)
-
-
-def add(kept, came):
-    return (kept.astype(F32) + came.astype(F32)).astype(BF16)
+def weight_grads(place, jobs):
+    parts = len(jobs[0][1])
+    rows, width = jobs[0][1][0].shape
+    units = jobs[0][0].shape[0]
+    cuts = 4 if units % 64 == 0 else 1
+    ids = [job[2] for job in jobs]
+    count = sum(len(i) for i in ids)
+    flat = [x for left, right, i, _ in jobs for x in [left] + [right[j] for j in i]]
+    begun = [job[3] for job in jobs if job[3] is not None]
+    aliases, at = {}, 1 + len(flat)
+    for n, job in enumerate(jobs):
+        if job[3] is not None:
+            aliases[at] = n
+            at += 1
+    return pl.pallas_call(
+        lambda *refs: weight_kernel(ids, parts, cuts, *refs),
+        in_specs=[SMEM] + [VMEM] * len(flat) + [HBM] * len(begun),
+        out_specs=[HBM] * len(jobs),
+        out_shape=[shape((units, parts * width))] * len(jobs),
+        scratch_shapes=[
+            pltpu.VMEM((count, units, width), BF16), pltpu.SemaphoreType.DMA((count + cuts - 1,))
+        ],
+        input_output_aliases=aliases,
+        compiler_params=pltpu.CompilerParams(vmem_limit_bytes=20 * 1024 * 1024),
+        cost_estimate=pl.CostEstimate(
+            flops=2 * count * units * rows * width,
+            bytes_accessed=2 * count * units * width,
+            transcendentals=0,
+        ),
+    )(place, *flat, *begun)
+
+
+def add(kept, *came):
+    total = kept.astype(F32)
+    for block in came:
+        total = total + block.astype(F32)
+    return total.astype(BF16)
 
 
 def token_device(
@@ -377,9 +409,9 @@
             i, k = order[n + 1], order[n + 2]
             others[k] = swap(own[k], parts, size)
             others[i], others[k] = others[i], others[k]
-    high = list(range(parts // 2, parts))
-    low = list(range(parts // 2))
-    block = shape((parts // 2, half, width))
+    high = [parts - 1]
+    low = list(range(parts - 1))
+    block, blocks = (shape((len(ids), half, width)) for ids in (high, low))
     turned = shape((units, rows))
     straight = shape((rows, units))
     flops = 4 * rows * units * width * (parts // 2)
@@ -388,40 +420,47 @@
         [block, block, straight, straight, turned, turned, turned],
         flops=flops, moved=2 * units * width * parts,
     )(place, base, acc, wg, wu)
-    upper = add(keep, swap(send, parts, size))
+    upper_keep, upper_came = keep, swap(send, parts, size)
     keep, send = call(
         lambda *refs: piece_kernel(low, *refs), [SMEM] + [VMEM] * 4, [VMEM] * 2,
-        [block, block], flops=flops, moved=2 * units * width * parts,
+        [blocks, blocks], flops=flops, moved=2 * units * width * parts,
     )(place, g, u, wg, wu)
+    upper_came, keep, send = lax.optimization_barrier((upper_came, keep, send))
+    upper = add(upper_keep, upper_came)
     lower = add(keep, swap(send, parts, size))
-    lefts, rights, grads = [hid_t, g_t, u_t], [dys, xs, xs], []
-
-    def exchange(kept, sent, distance):
-        if len(grads) == len(lefts):
-            return add(kept, swap(sent, distance, size))
-        i = len(grads)
-        sent, left = lax.optimization_barrier((sent, lefts[i]))
-        came = swap(sent, distance, size)
-        grad = weight_grad(place, left, rights[i])
-        came, grad = lax.optimization_barrier((came, grad))
-        grads.append(grad)
-        return add(kept, came)
-
-    part = exchange(lower, upper, parts // 2)
-    distance = parts // 4
-    while distance:
-        count = part.shape[0] // 2
-        part = exchange(part[:count], part[count:], distance)
+    every, front, back = list(range(parts)), list(range(parts // 2)), list(range(parts // 2, parts))
+
+    def rounds(kept, sends, after, jobs):
+        came = [swap(block, distance, size) for block, distance in sends]
+        made = []
+        if jobs:
+            lefts = lax.optimization_barrier((tuple(job[0] for job in jobs), after))[0]
+            made = weight_grads(place, [(left, *job[1:]) for left, job in zip(lefts, jobs)])
+            *came, made = lax.optimization_barrier((*came, made))
+        return add(kept, *came), made
+
+    sends = [(upper[i], part) for i, part in enumerate(high)][::-1]
+    sends += [(lower[i], part) for i, part in enumerate(low)][:0:-1]
+    waiting, _ = lax.optimization_barrier((tuple(block for block, _ in sends[1:]), lower))
+    sends[1:] = [(block, send[1]) for block, send in zip(waiting, sends[1:])]
+    part, (grad_down, grad_gate) = rounds(
+        lower[0], sends, lower, [(hid_t, dys, every, None), (g_t, xs, front, None)]
+    )
+    part = part.reshape(experts // 2, group, width)
+    distance, grad_up = experts // 2, None
+    jobs = [(g_t, xs, back, grad_gate)]
+    while distance > 1:
+        kept, away = part[0::2], part[1::2]
+        part, made = rounds(kept, [(away, distance * parts)], away, jobs)
+        if distance == experts // 2:
+            (grad_gate,), jobs = made, [(u_t, xs, every, None)]
+        elif jobs:
+            (grad_up,), jobs = made, []
         distance //= 2
-    part = part[0].reshape(experts // 2, group, width)
-    distance = 2
-    while distance < experts:
-        count = part.shape[0] // 2
-        part = exchange(part[:count], part[count:], distance * parts)
-        distance *= 2
-    for i in range(len(grads), len(lefts)):
-        grads.append(weight_grad(place, lefts[i], rights[i]))
-    grad_down, grad_gate, grad_up = grads
+    if experts == 2:
+        (grad_gate,) = weight_grads(place, jobs)
+    if grad_up is None:
+        (grad_up,) = weight_grads(place, [(u_t, xs, every, None)])
     return (part[0], grad_gate[None], grad_up[None], grad_down[None])
 
 

time: 47.2 us -> 44.9 us (0.951)
  waiting for transfers between devices: 5.38 us -> 2.06 us
  starting transfers between devices: 17.7 us -> 19 us
    ppermute x16 -> x17, waiting for transfers between devices: 5.38 us -> 2.06 us  [swap(): return lax.ppermute(value, AXES, [(i, i ^ distance) for i in range(size)])]
    ppermute x16 -> x17, starting transfers between devices: 17.7 us -> 19 us  [swap(): return lax.ppermute(value, AXES, [(i, i ^ distance) for i in range(size)])]
  transfers between devices with their start and end apart: 16 -> 17, of which waited for: 5 -> 3; matrix products, arithmetic and copies ran while one was open for 0% -> 0% of each run, Pallas kernels for 38% -> 40%
where the time goes in v3:
time: 44.9 us; the launch traced here: 44.6 us
  Pallas kernels  19.8 us (44%)
  starting transfers between devices  19 us (42%)
  between operations  2.19 us (5%)
  waiting for transfers between devices  2.06 us (5%)
  other arithmetic  1.61 us (4%)
    ppermute x17, starting transfers between devices, swap(): return lax.ppermute(value, AXES, [(i, i ^ distance) for i in range(size)])  19 us
    pallas_call x3, Pallas kernels, weight_grads(): pl.pallas_call(lambda *refs: weight_kernel(ids, parts, cuts, *refs), in_s...  7.65 us
    pallas_call x2, Pallas kernels, load(): call(lambda *refs: load_kernel(count, *refs), [HBM] * count + [VMEM], [VM...  5.25 us
    pallas_call x4, Pallas kernels, token_device(): call(lambda *refs, j=j, n=n: pre_kernel(j, n == 0, *refs), [SMEM] + [VMEM...  4.83 us
    ppermute x17, waiting for transfers between devices, swap(): return lax.ppermute(value, AXES, [(i, i ^ distance) for i in range(size)])  2.06 us
    pallas_call x1, Pallas kernels, token_device(): call(lambda *refs: piece_kernel(low, *refs), [SMEM] + [VMEM] * 4, [VMEM]...  1.22 us
  transfers between devices with their start and end apart: 17, of which 3 were waited for; matrix products, arithmetic and copies ran while one was open for 0% of the time, Pallas kernels for 40%

profile of v3, /device:TPU:0, one launch (start us, length us, event | category | flops | bytes accessed | tf_op | source)
XLA Modules:
  0.0 44.6 jit_solution(2814653193638944060)
XLA Ops:
  0.6 0.9 %fusion.6.refs_1_ = bf16[2,8,1024]{2,1,0:T(8,128)(2,1)S(1)} fusion(f32[1,8,8]{2,1,0:T(8,128)} %bitcast.38, s32[1,8,8]{2,1,0:T(8,128)} %bitcast.39, s32[1,8,8]{2,1,0:T(8,128)} %bitcast.40, bf16[1,8,896]{2,1,0:T(8,128)(2,1)} %bitcast.36, bf16[1,8,896]{2,1,0:T(8,128)(2,1)} %bitcast.37), kind=kLoop, calls=%fused_computation.12 | loop fusion | flops 311296 | bytes 62208 | tf_op jit(solution)/shard_map/convert_element_type | solution.py:175
  1.5 4.0 %collective-permute-start = (bf16[2,8,1024]{2,1,0:T(8,128)(2,1)S(1)}, bf16[2,8,1024]{2,1,0:T(8,128)(2,1)S(1)}, u32[]{:S(2)}, u32[]{:S(2)}) collective-permute-start(bf16[2,8,1024]{2,1,0:T(8,128)(2,1)S(1)} %fusion.6.refs_1_), channel_id=1, source_target_pairs={{0,16},{1,17},{2,18},{3,19},{4,20},{5,21},{6,22},{7,23},{8,24},{9,... | collective-permute-start | bytes 98312 | tf_op jit(solution)/shard_map/ppermute | solution.py:136
  5.6 2.5 %shard_map.129.refs_4_.refs_3_ = bf16[640,3584]{1,0:T(8,128)(2,1)S(1)} custom-call(bf16[640,3584]{1,0:T(8,128)(2,1)} %bitcast.32, bf16[2,8,1024]{2,1,0:T(8,128)(2,1)S(1)} %fusion.6.refs_1_), custom_call_target="tpu_custom_call" | custom-call | bytes 4587520 | tf_op jit(solution)/shard_map/pallas_call | solution.py:191
  8.1 1.6 %collective-permute-start.1 = (bf16[2,16,1024]{2,1,0:T(8,128)(2,1)S(1)}, bf16[2,16,1024]{2,1,0:T(8,128)(2,1)S(1)}, u32[]{:S(2)}, u32[]{:S(2)}) collective-permute-start(bf16[2,16,1024]{2,1,0:T(8,128)(2,1)S(1)} %get-tuple-element.114.refs_2_), channel_id=1, source_target_pairs={{0,8},{1,9},{2,10},{3,11},{4,12},{5,13},{6,14},{7,15},{8,0},{9,1},... | collective-permute-start | bytes 196616 | tf_op jit(solution)/shard_map/ppermute | solution.py:136
  9.7 2.8 %shard_map.130 = (bf16[640,3584]{1,0:T(8,128)(2,1)S(1)}, bf16[640,3584]{1,0:T(8,128)(2,1)S(1)}) custom-call(bf16[640,3584]{1,0:T(8,128)(2,1)S(1)} %bitcast.31, bf16[640,3584]{1,0:T(8,128)(2,1)} %bitcast.33, bf16[2,16,1024]{2,1,0:T(8,128)(2,1)S(1)} %get-tuple-element.114.refs_2_), custom_call_target="tpu_custom_call" | custom-call | bytes 9175040 | tf_op jit(solution)/shard_map/pallas_call | solution.py:191
  12.6 2.5 %collective-permute-start.8 = (bf16[2,32,896]{2,1,0:T(8,128)(2,1)S(1)}, bf16[2,32,896]{2,1,0:T(8,128)(2,1)S(1)}, u32[]{:S(2)}, u32[]{:S(2)}) collective-permute-start(bf16[2,32,896]{2,1,0:T(8,128)(2,1)S(1)} %slice.39.refs_1_), channel_id=1, source_target_pairs={{0,3},{1,2},{2,1},{3,0},{4,7},{5,6},{6,5},{7,4},{8,11},{9,10},{10,... | collective-permute-start | bytes 344072 | tf_op jit(solution)/shard_map/ppermute | solution.py:136
  15.1 0.5 %collective-permute-start.5 = (bf16[2,32,896]{2,1,0:T(8,128)(2,1)S(1)}, bf16[2,32,896]{2,1,0:T(8,128)(2,1)S(1)}, u32[]{:S(2)}, u32[]{:S(2)}) collective-permute-start(bf16[2,32,896]{2,1,0:T(8,128)(2,1)S(1)} %slice.39.refs_1_), channel_id=1, source_target_pairs={{0,1},{1,0},{2,3},{3,2},{4,5},{5,4},{6,7},{7,6},{8,9},{9,8},{10,11... | collective-permute-start | bytes 344072 | tf_op jit(solution)/shard_map/ppermute | solution.py:136
  17.6 1.2 %shard_map.132 = (bf16[64,896]{1,0:T(8,128)(2,1)S(1)}, bf16[64,896]{1,0:T(8,128)(2,1)S(1)}, f32[3,64,640]{2,1,0:T(8,128)S(1)}) custom-call(s32[1]{0:T(128)} %bitcast.5.refs_0_, bf16[2,32,896]{2,1,0:T(8,128)(2,1)S(1)} %slice.39.refs_1_, bf16[2,32,896]{2,1,0:T(8,128)(2,1)S(1)} %collective-permute-done.7.refs_2_, f32[64,1]{1,0:T(8,128)S(1)} %get-tuple-element.65.refs_3_, ...), custom_call_target="tpu_custom_call" | custom-call | flops 220200960 | bytes 3440640 | tf_op jit(solution)/shard_map/pallas_call | solution.py:398
  18.9 0.6 %collective-permute-start.9 = (bf16[2,32,896]{2,1,0:T(8,128)(2,1)S(1)}, bf16[2,32,896]{2,1,0:T(8,128)(2,1)S(1)}, u32[]{:S(2)}, u32[]{:S(2)}) collective-permute-start(bf16[2,32,896]{2,1,0:T(8,128)(2,1)S(1)} %collective-permute-done.8.refs_1_), channel_id=1, source_target_pairs={{0,4},{1,5},{2,6},{3,7},{4,0},{5,1},{6,2},{7,3},{8,12},{9,13},{10,... | collective-permute-start | bytes 344072 | tf_op jit(solution)/shard_map/ppermute | solution.py:136
  19.4 1.4 %collective-permute-done.5.refs_1_ = bf16[2,32,896]{2,1,0:T(8,128)(2,1)S(1)} collective-permute-done((bf16[2,32,896]{2,1,0:T(8,128)(2,1)S(1)}, bf16[2,32,896]{2,1,0:T(8,128)(2,1)S(1)}, u32[]{:S(2)}, u32[]{:S(2)}) %collective-permute-start.5) | collective-permute-done | bytes 114720 | tf_op jit(solution)/shard_map/ppermute | solution.py:136
  21.4 1.2 %shard_map.133 = (bf16[64,896]{1,0:T(8,128)(2,1)S(1)}, bf16[64,896]{1,0:T(8,128)(2,1)S(1)}, f32[3,64,640]{2,1,0:T(8,128)S(1)}) custom-call(s32[1]{0:T(128)} %bitcast.5.refs_0_, bf16[2,32,896]{2,1,0:T(8,128)(2,1)S(1)} %collective-permute-done.8.refs_1_, bf16[2,32,896]{2,1,0:T(8,128)(2,1)S(1)} %collective-permute-done.9.refs_2_, ...), custom_call_target="tpu_custom_call" | custom-call | flops 220200960 | bytes 3440640 | tf_op jit(solution)/shard_map/pallas_call | solution.py:398
  22.6 1.2 %shard_map.134 = (bf16[64,896]{1,0:T(8,128)(2,1)S(1)}, bf16[64,896]{1,0:T(8,128)(2,1)S(1)}, f32[3,64,640]{2,1,0:T(8,128)S(1)}) custom-call(s32[1]{0:T(128)} %bitcast.5.refs_0_, bf16[2,32,896]{2,1,0:T(8,128)(2,1)S(1)} %collective-permute-done.5.refs_1_, bf16[2,32,896]{2,1,0:T(8,128)(2,1)S(1)} %collective-permute-done.6.refs_2_, ...), custom_call_target="tpu_custom_call" | custom-call | flops 220200960 | bytes 3440640 | tf_op jit(solution)/shard_map/pallas_call | solution.py:398
  23.8 1.2 %shard_map.135 = (bf16[64,896]{1,0:T(8,128)(2,1)S(1)}, bf16[64,896]{1,0:T(8,128)(2,1)S(1)}, f32[3,64,640]{2,1,0:T(8,128)S(1)}) custom-call(s32[1]{0:T(128)} %bitcast.5.refs_0_, bf16[2,32,896]{2,1,0:T(8,128)(2,1)S(1)} %collective-permute-done.3.refs_1_, bf16[2,32,896]{2,1,0:T(8,128)(2,1)S(1)} %collective-permute-done.4.refs_2_, ...), custom_call_target="tpu_custom_call" | custom-call | flops 220200960 | bytes 3440640 | tf_op jit(solution)/shard_map/pallas_call | solution.py:398
  25.0 0.7 %shard_map.136 = (bf16[1,32,896]{2,1,0:T(8,128)(2,1)S(1)}, bf16[1,32,896]{2,1,0:T(8,128)(2,1)S(1)}, bf16[64,640]{1,0:T(8,128)(2,1)S(1)}, bf16[64,640]{1,0:T(8,12...) custom-call(s32[1]{0:T(128)} %bitcast.5.refs_0_, ...), custom_call_target="tpu_custom_call" | custom-call | flops 293601280 | bytes 4587520 | tf_op jit(solution)/shard_map/pallas_call | solution.py:418
  25.9 1.2 %shard_map.137 = (bf16[3,32,896]{2,1,0:T(8,128)(2,1)S(1)}, bf16[3,32,896]{2,1,0:T(8,128)(2,1)S(1)}) custom-call(s32[1]{0:T(128)} %bitcast.5.refs_0_, bf16[64,640]{1,0:T(8,128)(2,1)S(1)} %get-tuple-element.76.refs_1_, bf16[64,640]{1,0:T(8,128)(2,1)S(1)} %get-tuple-element.77.refs_2_, bf16[640,3584]{1,0:T(8,128)(2,1)S(1)} %shard_map.129.refs_4_.refs_3_, ...), custom_call_target="tpu_custom_call" | custom-call | flops 293601280 | bytes 4587520 | tf_op jit(solution)/shard_map/pallas_call | solution.py:424
  27.6 2.1 %collective-permute-start.12 = (bf16[32,896]{1,0:T(8,128)(2,1)S(1)}, bf16[32,896]{1,0:T(8,128)(2,1)S(1)}, u32[]{:S(2)}, u32[]{:S(2)}) collective-permute-start(bf16[32,896]{1,0:T(8,128)(2,1)S(1)} %fusion.7), channel_id=1, source_target_pairs={{0,3},{1,2},{2,1},{3,0},{4,7},{5,6},{6,5},{7,4},{8,11},{9,10},{10,... | collective-permute-start | bytes 172040 | tf_op jit(solution)/shard_map/ppermute | solution.py:136
  29.8 1.1 %collective-permute-start.13 = (bf16[32,896]{1,0:T(8,128)(2,1)S(1)}, bf16[32,896]{1,0:T(8,128)(2,1)S(1)}, u32[]{:S(2)}, u32[]{:S(2)}) collective-permute-start(bf16[32,896]{1,0:T(8,128)(2,1)S(1)} %get-tuple-element.84), channel_id=1, source_target_pairs={{0,2},{1,3},{2,0},{3,1},{4,6},{5,7},{6,4},{7,5},{8,10},{9,11},{10,... | collective-permute-start | bytes 172040 | tf_op jit(solution)/shard_map/ppermute | solution.py:136
  30.9 0.8 %collective-permute-start.14 = (bf16[32,896]{1,0:T(8,128)(2,1)S(1)}, bf16[32,896]{1,0:T(8,128)(2,1)S(1)}, u32[]{:S(2)}, u32[]{:S(2)}) collective-permute-start(bf16[32,896]{1,0:T(8,128)(2,1)S(1)} %get-tuple-element.85), channel_id=1, source_target_pairs={{0,1},{1,0},{2,3},{3,2},{4,5},{5,4},{6,7},{7,6},{8,9},{9,8},{10,11... | collective-permute-start | bytes 172040 | tf_op jit(solution)/shard_map/ppermute | solution.py:136
  31.7 3.3 %shard_map.138 = (bf16[640,3584]{1,0:T(8,128)(2,1)}, bf16[640,3584]{1,0:T(8,128)(2,1)}) custom-call(s32[1]{0:T(128)} %bitcast.5.refs_0_, bf16[640,64]{1,0:T(8,128)(2,1)S(1)} %get-tuple-element.88.refs_1_, bf16[64,896]{1,0:T(8,128)(2,1)S(1)} %get-tuple-element.89.refs_2_, bf16[64,896]{1,0:T(8,128)(2,1)S(1)} %get-tuple-element.90.refs_3_, ...), custom_call_target="tpu_custom_call" | custom-call | flops 440401920 | bytes 6881280 | tf_op jit(solution)/shard_map/pallas_call | solution.py:330
  35.1 2.5 %collective-permute-start.15 = (bf16[2,8,896]{2,1,0:T(8,128)(2,1)S(1)}, bf16[2,8,896]{2,1,0:T(8,128)(2,1)S(1)}, u32[]{:S(2)}, u32[]{:S(2)}) collective-permute-start(bf16[2,8,896]{2,1,0:T(8,128)(2,1)S(1)} %slice.35), channel_id=1, source_target_pairs={{0,16},{1,17},{2,18},{3,19},{4,20},{5,21},{6,22},{7,23},{8,24},{9,... | collective-permute-start | bytes 86024 | tf_op jit(solution)/shard_map/ppermute | solution.py:136
  37.6 1.8 %shard_map.139 = bf16[640,3584]{1,0:T(8,128)(2,1)} custom-call(s32[1]{0:T(128)} %bitcast.5.refs_0_, bf16[640,64]{1,0:T(8,128)(2,1)S(1)} %get-tuple-element.101.refs_6_.refs_1_, bf16[64,896]{1,0:T(8,128)(2,1)S(1)} %get-tuple-element.102.refs_2_.refs_4_, bf16[64,896]{1,0:T(8,128)(2,1)S(1)} %get-tuple-element.103.refs_3_.refs_5_, ...), custom_call_target="tpu_custom_call", output_to_operand_aliasing={{}: (4, {})} | custom-call | flops 146800640 | bytes 2293760 | tf_op jit(solution)/shard_map/pallas_call | solution.py:330
  40.0 1.5 %collective-permute-start.16 = (bf16[1,8,896]{2,1,0:T(8,128)(2,1)S(1)}, bf16[1,8,896]{2,1,0:T(8,128)(2,1)S(1)}, u32[]{:S(2)}, u32[]{:S(2)}) collective-permute-start(bf16[1,8,896]{2,1,0:T(8,128)(2,1)S(1)} %slice.44), channel_id=1, source_target_pairs={{0,8},{1,9},{2,10},{3,11},{4,12},{5,13},{6,14},{7,15},{8,0},{9,1},... | collective-permute-start | bytes 43016 | tf_op jit(solution)/shard_map/ppermute | solution.py:136
  41.5 2.6 %shard_map.140 = bf16[640,3584]{1,0:T(8,128)(2,1)} custom-call(s32[1]{0:T(128)} %bitcast.5.refs_0_, bf16[640,64]{1,0:T(8,128)(2,1)S(1)} %get-tuple-element.107.refs_1_, bf16[64,896]{1,0:T(8,128)(2,1)S(1)} %get-tuple-element.94.refs_7_.refs_2_, bf16[64,896]{1,0:T(8,128)(2,1)S(1)} %get-tuple-element.95.refs_8_.refs_3_, ...), custom_call_target="tpu_custom_call" | custom-call | flops 293601280 | bytes 4587520 | tf_op jit(solution)/shard_map/pallas_call | solution.py:330
  44.0 0.6 %fusion.9 = bf16[8,896]{1,0:T(8,128)(2,1)} fusion(bf16[1,8,896]{2,1,0:T(8,128)(2,1)S(1)} %collective-permute-done.16, bf16[2,8,896]{2,1,0:T(8,128)(2,1)S(1)} %add_convert_fusion.2), kind=kLoop, calls=%fused_computation.20 | loop fusion | flops 28672 | bytes 43008 | tf_op jit(solution)/shard_map/squeeze | solution.py:464
  (41 shorter events, 2.5 us)
Async XLA Ops:
  1.5 6.5 %collective-permute-start = (bf16[2,8,1024]{2,1,0:T(8,128)(2,1)S(1)}, bf16[2,8,1024]{2,1,0:T(8,128)(2,1)S(1)}, u32[]{:S(2)}, u32[]{:S(2)}) collective-permute-start(bf16[2,8,1024]{2,1,0:T(8,128)(2,1)S(1)} %fusion.6.refs_1_), channel_id=1, source_target_pairs={{0,16},{1,17},{2,18},{3,19},{4,20},{5,21},{6,22},{7,23},{8,24},{9,... | collective-permute-start | bytes 98312 | tf_op jit(solution)/shard_map/ppermute | solution.py:136
  5.6 4.2 %slice-start = ((s8[4587520]{0:T(1024)(128)(4,1)}), s8[4194304]{0:T(1024)(128)(4,1)S(1)}, s32[]{:S(2)}) async-start(s8[4587520]{0:T(1024)(128)(4,1)} %bitcast.29), calls=%async_computation | async-start | bytes 8388608
  5.6 4.2 %slice-start.1 = ((s8[4587520]{0:T(1024)(128)(4,1)}), s8[393216]{0:T(1024)(128)(4,1)S(1)}, s32[]{:S(2)}) async-start(s8[4587520]{0:T(1024)(128)(4,1)} %bitcast.29), calls=%async_computation.1 | async-start | bytes 786432
  8.1 4.4 %collective-permute-start.1 = (bf16[2,16,1024]{2,1,0:T(8,128)(2,1)S(1)}, bf16[2,16,1024]{2,1,0:T(8,128)(2,1)S(1)}, u32[]{:S(2)}, u32[]{:S(2)}) collective-permute-start(bf16[2,16,1024]{2,1,0:T(8,128)(2,1)S(1)} %get-tuple-element.114.refs_2_), channel_id=1, source_target_pairs={{0,8},{1,9},{2,10},{3,11},{4,12},{5,13},{6,14},{7,15},{8,0},{9,1},... | collective-permute-start | bytes 196616 | tf_op jit(solution)/shard_map/ppermute | solution.py:136
  12.6 6.3 %collective-permute-start.8 = (bf16[2,32,896]{2,1,0:T(8,128)(2,1)S(1)}, bf16[2,32,896]{2,1,0:T(8,128)(2,1)S(1)}, u32[]{:S(2)}, u32[]{:S(2)}) collective-permute-start(bf16[2,32,896]{2,1,0:T(8,128)(2,1)S(1)} %slice.39.refs_1_), channel_id=1, source_target_pairs={{0,3},{1,2},{2,1},{3,0},{4,7},{5,6},{6,5},{7,4},{8,11},{9,10},{10,... | collective-permute-start | bytes 344072 | tf_op jit(solution)/shard_map/ppermute | solution.py:136
  15.1 2.5 %collective-permute-start.7 = (bf16[2,32,896]{2,1,0:T(8,128)(2,1)S(1)}, bf16[2,32,896]{2,1,0:T(8,128)(2,1)S(1)}, u32[]{:S(2)}, u32[]{:S(2)}) collective-permute-start(bf16[2,32,896]{2,1,0:T(8,128)(2,1)S(1)} %slice.39.refs_1_), channel_id=1, source_target_pairs={{0,4},{1,5},{2,6},{3,7},{4,0},{5,1},{6,2},{7,3},{8,12},{9,13},{10,... | collective-permute-start | bytes 344072 | tf_op jit(solution)/shard_map/ppermute | solution.py:136
  15.1 5.8 %collective-permute-start.5 = (bf16[2,32,896]{2,1,0:T(8,128)(2,1)S(1)}, bf16[2,32,896]{2,1,0:T(8,128)(2,1)S(1)}, u32[]{:S(2)}, u32[]{:S(2)}) collective-permute-start(bf16[2,32,896]{2,1,0:T(8,128)(2,1)S(1)} %slice.39.refs_1_), channel_id=1, source_target_pairs={{0,1},{1,0},{2,3},{3,2},{4,5},{5,4},{6,7},{7,6},{8,9},{9,8},{10,11... | collective-permute-start | bytes 344072 | tf_op jit(solution)/shard_map/ppermute | solution.py:136
  15.6 5.3 %collective-permute-start.3 = (bf16[2,32,896]{2,1,0:T(8,128)(2,1)S(1)}, bf16[2,32,896]{2,1,0:T(8,128)(2,1)S(1)}, u32[]{:S(2)}, u32[]{:S(2)}) collective-permute-start(bf16[2,32,896]{2,1,0:T(8,128)(2,1)S(1)} %slice.39.refs_1_), channel_id=1, source_target_pairs={{0,2},{1,3},{2,0},{3,1},{4,6},{5,7},{6,4},{7,5},{8,10},{9,11},{10,... | collective-permute-start | bytes 344072 | tf_op jit(solution)/shard_map/ppermute | solution.py:136
  16.1 1.3 %collective-permute-start.2 = (bf16[32,128]{1,0:T(8,128)(2,1)S(1)}, bf16[32,128]{1,0:T(8,128)(2,1)S(1)}, u32[]{:S(2)}, u32[]{:S(2)}) collective-permute-start(bf16[32,128]{1,0:T(8,128)(2,1)S(1)} %slice_bitcast_fusion.3.refs_3_), channel_id=1, source_target_pairs={{0,4},{1,5},{2,6},{3,7},{4,0},{5,1},{6,2},{7,3},{8,12},{9,13},{10,... | collective-permute-start | bytes 24584 | tf_op jit(solution)/shard_map/ppermute | solution.py:136
  18.9 2.5 %collective-permute-start.9 = (bf16[2,32,896]{2,1,0:T(8,128)(2,1)S(1)}, bf16[2,32,896]{2,1,0:T(8,128)(2,1)S(1)}, u32[]{:S(2)}, u32[]{:S(2)}) collective-permute-start(bf16[2,32,896]{2,1,0:T(8,128)(2,1)S(1)} %collective-permute-done.8.refs_1_), channel_id=1, source_target_pairs={{0,4},{1,5},{2,6},{3,7},{4,0},{5,1},{6,2},{7,3},{8,12},{9,13},{10,... | collective-permute-start | bytes 344072 | tf_op jit(solution)/shard_map/ppermute | solution.py:136
  20.9 1.7 %collective-permute-start.6 = (bf16[2,32,896]{2,1,0:T(8,128)(2,1)S(1)}, bf16[2,32,896]{2,1,0:T(8,128)(2,1)S(1)}, u32[]{:S(2)}, u32[]{:S(2)}) collective-permute-start(bf16[2,32,896]{2,1,0:T(8,128)(2,1)S(1)} %collective-permute-done.5.refs_1_), channel_id=1, source_target_pairs={{0,4},{1,5},{2,6},{3,7},{4,0},{5,1},{6,2},{7,3},{8,12},{9,13},{10,... | collective-permute-start | bytes 344072 | tf_op jit(solution)/shard_map/ppermute | solution.py:136
  20.9 2.9 %collective-permute-start.4 = (bf16[2,32,896]{2,1,0:T(8,128)(2,1)S(1)}, bf16[2,32,896]{2,1,0:T(8,128)(2,1)S(1)}, u32[]{:S(2)}, u32[]{:S(2)}) collective-permute-start(bf16[2,32,896]{2,1,0:T(8,128)(2,1)S(1)} %collective-permute-done.3.refs_1_), channel_id=1, source_target_pairs={{0,4},{1,5},{2,6},{3,7},{4,0},{5,1},{6,2},{7,3},{8,12},{9,13},{10,... | collective-permute-start | bytes 344072 | tf_op jit(solution)/shard_map/ppermute | solution.py:136
  25.7 1.4 %collective-permute-start.10 = (bf16[1,32,896]{2,1,0:T(8,128)(2,1)S(1)}, bf16[1,32,896]{2,1,0:T(8,128)(2,1)S(1)}, u32[]{:S(2)}, u32[]{:S(2)}) collective-permute-start(bf16[1,32,896]{2,1,0:T(8,128)(2,1)S(1)} %get-tuple-element.75), channel_id=1, source_target_pairs={{0,4},{1,5},{2,6},{3,7},{4,0},{5,1},{6,2},{7,3},{8,12},{9,13},{10,... | collective-permute-start | bytes 172040 | tf_op jit(solution)/shard_map/ppermute | solution.py:136
  27.1 2.6 %collective-permute-start.11 = (bf16[3,32,896]{2,1,0:T(8,128)(2,1)S(1)}, bf16[3,32,896]{2,1,0:T(8,128)(2,1)S(1)}, u32[]{:S(2)}, u32[]{:S(2)}) collective-permute-start(bf16[3,32,896]{2,1,0:T(8,128)(2,1)S(1)} %get-tuple-element.81), channel_id=1, source_target_pairs={{0,4},{1,5},{2,6},{3,7},{4,0},{5,1},{6,2},{7,3},{8,12},{9,13},{10,... | collective-permute-start | bytes 516104 | tf_op jit(solution)/shard_map/ppermute | solution.py:136
  27.6 7.4 %collective-permute-start.12 = (bf16[32,896]{1,0:T(8,128)(2,1)S(1)}, bf16[32,896]{1,0:T(8,128)(2,1)S(1)}, u32[]{:S(2)}, u32[]{:S(2)}) collective-permute-start(bf16[32,896]{1,0:T(8,128)(2,1)S(1)} %fusion.7), channel_id=1, source_target_pairs={{0,3},{1,2},{2,1},{3,0},{4,7},{5,6},{6,5},{7,4},{8,11},{9,10},{10,... | collective-permute-start | bytes 172040 | tf_op jit(solution)/shard_map/ppermute | solution.py:136
  29.8 5.2 %collective-permute-start.13 = (bf16[32,896]{1,0:T(8,128)(2,1)S(1)}, bf16[32,896]{1,0:T(8,128)(2,1)S(1)}, u32[]{:S(2)}, u32[]{:S(2)}) collective-permute-start(bf16[32,896]{1,0:T(8,128)(2,1)S(1)} %get-tuple-element.84), channel_id=1, source_target_pairs={{0,2},{1,3},{2,0},{3,1},{4,6},{5,7},{6,4},{7,5},{8,10},{9,11},{10,... | collective-permute-start | bytes 172040 | tf_op jit(solution)/shard_map/ppermute | solution.py:136
  30.9 4.2 %collective-permute-start.14 = (bf16[32,896]{1,0:T(8,128)(2,1)S(1)}, bf16[32,896]{1,0:T(8,128)(2,1)S(1)}, u32[]{:S(2)}, u32[]{:S(2)}) collective-permute-start(bf16[32,896]{1,0:T(8,128)(2,1)S(1)} %get-tuple-element.85), channel_id=1, source_target_pairs={{0,1},{1,0},{2,3},{3,2},{4,5},{5,4},{6,7},{7,6},{8,9},{9,8},{10,11... | collective-permute-start | bytes 172040 | tf_op jit(solution)/shard_map/ppermute | solution.py:136
  35.1 4.8 %collective-permute-start.15 = (bf16[2,8,896]{2,1,0:T(8,128)(2,1)S(1)}, bf16[2,8,896]{2,1,0:T(8,128)(2,1)S(1)}, u32[]{:S(2)}, u32[]{:S(2)}) collective-permute-start(bf16[2,8,896]{2,1,0:T(8,128)(2,1)S(1)} %slice.35), channel_id=1, source_target_pairs={{0,16},{1,17},{2,18},{3,19},{4,20},{5,21},{6,22},{7,23},{8,24},{9,... | collective-permute-start | bytes 86024 | tf_op jit(solution)/shard_map/ppermute | solution.py:136
  40.0 4.1 %collective-permute-start.16 = (bf16[1,8,896]{2,1,0:T(8,128)(2,1)S(1)}, bf16[1,8,896]{2,1,0:T(8,128)(2,1)S(1)}, u32[]{:S(2)}, u32[]{:S(2)}) collective-permute-start(bf16[1,8,896]{2,1,0:T(8,128)(2,1)S(1)} %slice.44), channel_id=1, source_target_pairs={{0,8},{1,9},{2,10},{3,11},{4,12},{5,13},{6,14},{7,15},{8,0},{9,1},... | collective-permute-start | bytes 43016 | tf_op jit(solution)/shard_map/ppermute | solution.py:136

commit v4 on v3

--- a/solution.py
+++ b/solution.py
@@ -195,8 +195,9 @@
     )(*weights, after)
 
 
-def plan_kernel(bits, parts, top, place_ref, seed_ref, layer_ref, own_ref, other_ref, *refs):
-    gate_ref, base_ref = refs[-2:]
+def plan_kernel(
+    bits, parts, top, place_ref, seed_ref, layer_ref, own_ref, other_ref, gate_ref, keep_ref
+):
     notes = jnp.concatenate([own_ref[...], other_ref[...]], axis=0).astype(F32)
     rows = notes.shape[0]
     group = rows >> bits
@@ -220,7 +221,17 @@
     for b in range(bits):
         offset = offset + (((position >> b) & 1) << (bits - 1 - b))
     row_ids = (expert << bits) * CAP_SRC + (offset ^ expert) * CAP_SRC + slot
-    base_ref[...] = row_ids * FF * -1640531535 + seed_ref[0] * 40503 + layer_ref[0] * 97
+    base = row_ids * FF * -1640531535 + seed_ref[0] * 40503 + layer_ref[0] * 97
+    units = keep_ref.shape[1]
+    unit_ids = (place_ref[0] % parts) * units + lax.broadcasted_iota(I32, (rows, units), 1)
+    mixed = base + unit_ids * -1640531535
+    mixed = mixed ^ logical(mixed, 15)
+    mixed = mixed * -2048144789
+    mixed = mixed ^ logical(mixed, 13)
+    mixed = mixed * -1028477387
+    mixed = mixed ^ logical(mixed, 16)
+    levels = logical(mixed, 8) & 1023
+    keep_ref[...] = jnp.where(levels >= 102, KEEP_FACTOR, 0.0).astype(F32)
 
 
 def pre_kernel(part, first, *refs):
@@ -251,40 +262,33 @@
 
 
 def hidden_kernel(
-    part_ids, place_ref, base_ref, acc_ref, wg, wu,
-    keep_ref, send_ref, g_ref, u_ref, hid_t_ref, g_t_ref, u_t_ref,
+    part_ids, place_ref, mul_ref, acc_ref, wg, wu, keep_ref, send_ref, h_ref, g_ref, u_ref
 ):
-    me = place_ref[0]
-    _, rows, units = acc_ref.shape
-    width = keep_ref.shape[2]
-    unit_ids = (me % (wg.shape[1] // width)) * units + lax.broadcasted_iota(I32, (rows, units), 1)
-    mixed = base_ref[...] + unit_ids * -1640531535
-    mixed = mixed ^ logical(mixed, 15)
-    mixed = mixed * -2048144789
-    mixed = mixed ^ logical(mixed, 13)
-    mixed = mixed * -1028477387
-    mixed = mixed ^ logical(mixed, 16)
-    levels = logical(mixed, 8) & 1023
-    keep_mul = jnp.where(levels >= 102, KEEP_FACTOR, 0.0).astype(F32)
+    keep_mul = mul_ref[...]
     gate_pre = acc_ref[0]
     up_pre = acc_ref[1]
     grad_hidden = acc_ref[2] * keep_mul
     logistic = jax.nn.sigmoid(gate_pre)
     swish = gate_pre * logistic
-    upre = grad_hidden * swish
-    gpre = grad_hidden * up_pre * logistic * (1.0 + gate_pre * (1.0 - logistic))
-    g = gpre.astype(BF16)
-    u = upre.astype(BF16)
+    u = (grad_hidden * swish).astype(BF16)
+    g = grad_hidden * up_pre * logistic * (1.0 + gate_pre * (1.0 - logistic))
+    g = g.astype(BF16)
+    h_ref[...] = (swish * up_pre * keep_mul).astype(BF16)
     g_ref[...] = g
     u_ref[...] = u
-    pieces(me, part_ids, g, u, wg, wu, keep_ref, send_ref)
-    hid_t_ref[...] = (swish * up_pre * keep_mul).T.astype(BF16)
-    g_t_ref[...] = gpre.T.astype(BF16)
-    u_t_ref[...] = upre.T.astype(BF16)
+    pieces(place_ref[0], part_ids, g, u, wg, wu, keep_ref, send_ref)
 
 
 def piece_kernel(part_ids, place_ref, g_ref, u_ref, wg, wu, keep_ref, send_ref):
     pieces(place_ref[0], part_ids, g_ref[...], u_ref[...], wg, wu, keep_ref, send_ref)
+
+
+def turning_kernel(
+    part_ids, place_ref, h_ref, g_ref, u_ref, wg, wu, keep_ref, send_ref, *turned_refs
+):
+    piece_kernel(part_ids, place_ref, g_ref, u_ref, wg, wu, keep_ref, send_ref)
+    for ref, turned_ref in zip((h_ref, g_ref, u_ref), turned_refs):
+        turned_ref[...] = ref[...].astype(F32).T.astype(BF16)
 
 
 def weight_kernel(jobs, parts, cuts, place_ref, *refs):
@@ -383,10 +387,10 @@
     own = [data[:, :, :width]]
     own += [swap(own[0], j, size) for j in range(1, parts)]
     other_notes = swap(notes, parts, size)
-    gate, base = call(
+    gate, keep_mul = call(
         lambda *refs: plan_kernel(bits, parts, top, *refs),
         [SMEM] * 3 + [VMEM] * 2, [VMEM] * 2,
-        [shape((rows, 1), F32), shape((rows, 1), I32)],
+        [shape((rows, 1), F32), shape((rows, units), F32)],
     )(place, drop_seed, layer_id, notes, other_notes)
     xs, dys, acc = [None] * parts, [None] * parts, None
     order = [0] + list(range(1, parts))[::-1]
@@ -409,25 +413,30 @@
             i, k = order[n + 1], order[n + 2]
             others[k] = swap(own[k], parts, size)
             others[i], others[k] = others[i], others[k]
-    high = [parts - 1]
-    low = list(range(parts - 1))
+    high, low, mine = [parts - 1], list(range(1, parts - 1)), [0]
     block, blocks = (shape((len(ids), half, width)) for ids in (high, low))
     turned = shape((units, rows))
     straight = shape((rows, units))
     flops = 4 * rows * units * width * (parts // 2)
-    keep, send, g, u, hid_t, g_t, u_t = call(
-        lambda *refs: hidden_kernel(high, *refs), [SMEM] + [VMEM] * 4, [VMEM] * 7,
-        [block, block, straight, straight, turned, turned, turned],
+    keep, send, h, g, u = call(
+        lambda *refs: hidden_kernel(high, *refs), [SMEM] + [VMEM] * 4, [VMEM] * 5,
+        [block, block, straight, straight, straight],
         flops=flops, moved=2 * units * width * parts,
-    )(place, base, acc, wg, wu)
+    )(place, keep_mul, acc, wg, wu)
     upper_keep, upper_came = keep, swap(send, parts, size)
-    keep, send = call(
-        lambda *refs: piece_kernel(low, *refs), [SMEM] + [VMEM] * 4, [VMEM] * 2,
-        [blocks, blocks], flops=flops, moved=2 * units * width * parts,
-    )(place, g, u, wg, wu)
+    keep, send, hid_t, g_t, u_t = call(
+        lambda *refs: turning_kernel(low, *refs), [SMEM] + [VMEM] * 5, [VMEM] * 5,
+        [blocks, blocks, turned, turned, turned], flops=flops, moved=2 * units * width * parts,
+    )(place, h, g, u, wg, wu)
     upper_came, keep, send = lax.optimization_barrier((upper_came, keep, send))
     upper = add(upper_keep, upper_came)
     lower = add(keep, swap(send, parts, size))
+    later_g = lax.optimization_barrier((g, lower))[0]
+    keep, send = call(
+        lambda *refs: piece_kernel(mine, *refs), [SMEM] + [VMEM] * 4, [VMEM] * 2,
+        [block, block], flops=flops, moved=2 * units * width * parts,
+    )(place, later_g, u, wg, wu)
+    own = add(keep, swap(send, parts, size))
     every, front, back = list(range(parts)), list(range(parts // 2)), list(range(parts // 2, parts))
 
     def rounds(kept, sends, after, jobs):
@@ -439,28 +448,32 @@
             *came, made = lax.optimization_barrier((*came, made))
         return add(kept, *came), made
 
-    sends = [(upper[i], part) for i, part in enumerate(high)][::-1]
-    sends += [(lower[i], part) for i, part in enumerate(low)][:0:-1]
+    sends = [(upper[0], high[0])] + [(lower[i], low[i]) for i in range(len(low))][::-1]
     waiting, _ = lax.optimization_barrier((tuple(block for block, _ in sends[1:]), lower))
     sends[1:] = [(block, send[1]) for block, send in zip(waiting, sends[1:])]
     part, (grad_down, grad_gate) = rounds(
-        lower[0], sends, lower, [(hid_t, dys, every, None), (g_t, xs, front, None)]
+        own[0], sends, lower, [(hid_t, dys, every, None), (g_t, xs, front, None)]
     )
     part = part.reshape(experts // 2, group, width)
     distance, grad_up = experts // 2, None
-    jobs = [(g_t, xs, back, grad_gate)]
     while distance > 1:
         kept, away = part[0::2], part[1::2]
+        jobs = []
+        if distance == experts // 2:
+            jobs = [(g_t, xs, back, grad_gate), (u_t, xs, every[:1], None)]
+        elif distance == experts // 4:
+            jobs = [(u_t, xs, every[1:], grad_up)]
         part, made = rounds(kept, [(away, distance * parts)], away, jobs)
         if distance == experts // 2:
-            (grad_gate,), jobs = made, [(u_t, xs, every, None)]
+            grad_gate, grad_up = made
         elif jobs:
-            (grad_up,), jobs = made, []
+            (grad_up,) = made
         distance //= 2
     if experts == 2:
-        (grad_gate,) = weight_grads(place, jobs)
-    if grad_up is None:
+        (grad_gate,) = weight_grads(place, [(g_t, xs, back, grad_gate)])
         (grad_up,) = weight_grads(place, [(u_t, xs, every, None)])
+    elif experts == 4:
+        (grad_up,) = weight_grads(place, [(u_t, xs, every[1:], grad_up)])
     return (part[0], grad_gate[None], grad_up[None], grad_down[None])
 
 

time: 44.9 us -> 44.6 us (level)
    ppermute x17 -> x18, starting transfers between devices: 19 us -> 18.6 us  [swap(): return lax.ppermute(value, AXES, [(i, i ^ distance) for i in range(size)])]
    ppermute x17 -> x18, waiting for transfers between devices: 2.06 us -> 1.92 us  [swap(): return lax.ppermute(value, AXES, [(i, i ^ distance) for i in range(size)])]
    pallas_call x1 -> x2, Pallas kernels: 1.22 us -> 1.3 us  [the longest x1 0.83 us: token_device(): call(lambda *refs: turning_kernel(low, *refs), [SMEM] + [VMEM] * 5, [VMEM...]
  transfers between devices with their start and end apart: 17 -> 18, of which waited for: 3 -> 5; matrix products, arithmetic and copies ran while one was open for 0% -> 0% of each run, Pallas kernels for 40% -> 41%
where the time goes in v4:
time: 44.6 us; the launch traced here: 44.3 us
  Pallas kernels  19.9 us (45%)
  starting transfers between devices  18.6 us (42%)
  between operations  2.21 us (5%)
  waiting for transfers between devices  1.92 us (4%)
  other arithmetic  1.6 us (4%)
    ppermute x18, starting transfers between devices, swap(): return lax.ppermute(value, AXES, [(i, i ^ distance) for i in range(size)])  18.6 us
    pallas_call x3, Pallas kernels, weight_grads(): pl.pallas_call(lambda *refs: weight_kernel(ids, parts, cuts, *refs), in_s...  7.73 us
    pallas_call x2, Pallas kernels, load(): call(lambda *refs: load_kernel(count, *refs), [HBM] * count + [VMEM], [VM...  5.25 us
    pallas_call x4, Pallas kernels, token_device(): call(lambda *refs, j=j, n=n: pre_kernel(j, n == 0, *refs), [SMEM] + [VMEM...  4.83 us
    ppermute x18, waiting for transfers between devices, swap(): return lax.ppermute(value, AXES, [(i, i ^ distance) for i in range(size)])  1.92 us
    convert_element_type x1, other arithmetic, pack(): return (put(tokens, 0, 0).astype(F32) + put(cotangent, 1, 0).astype(F32)...  0.89 us
  transfers between devices with their start and end apart: 18, of which 5 were waited for; matrix products, arithmetic and copies ran while one was open for 0% of the time, Pallas kernels for 41%

profile of v4, /device:TPU:0, one launch (start us, length us, event | category | flops | bytes accessed | tf_op | source)
XLA Modules:
  0.0 44.3 jit_solution(3522284127089086488)
XLA Ops:
  0.6 0.9 %fusion.6.refs_1_ = bf16[2,8,1024]{2,1,0:T(8,128)(2,1)S(1)} fusion(f32[1,8,8]{2,1,0:T(8,128)} %bitcast.40, s32[1,8,8]{2,1,0:T(8,128)} %bitcast.41, s32[1,8,8]{2,1,0:T(8,128)} %bitcast.42, bf16[1,8,896]{2,1,0:T(8,128)(2,1)} %bitcast.38, bf16[1,8,896]{2,1,0:T(8,128)(2,1)} %bitcast.39), kind=kLoop, calls=%fused_computation.13 | loop fusion | flops 311296 | bytes 62208 | tf_op jit(solution)/shard_map/convert_element_type | solution.py:175
  1.5 4.0 %collective-permute-start = (bf16[2,8,1024]{2,1,0:T(8,128)(2,1)S(1)}, bf16[2,8,1024]{2,1,0:T(8,128)(2,1)S(1)}, u32[]{:S(2)}, u32[]{:S(2)}) collective-permute-start(bf16[2,8,1024]{2,1,0:T(8,128)(2,1)S(1)} %fusion.6.refs_1_), channel_id=1, source_target_pairs={{0,16},{1,17},{2,18},{3,19},{4,20},{5,21},{6,22},{7,23},{8,24},{9,... | collective-permute-start | bytes 98312 | tf_op jit(solution)/shard_map/ppermute | solution.py:136
  5.6 2.5 %shard_map.129.refs_4_.refs_3_ = bf16[640,3584]{1,0:T(8,128)(2,1)S(1)} custom-call(bf16[640,3584]{1,0:T(8,128)(2,1)} %bitcast.35, bf16[2,8,1024]{2,1,0:T(8,128)(2,1)S(1)} %fusion.6.refs_1_), custom_call_target="tpu_custom_call" | custom-call | bytes 4587520 | tf_op jit(solution)/shard_map/pallas_call | solution.py:191
  8.1 1.6 %collective-permute-start.1 = (bf16[2,16,1024]{2,1,0:T(8,128)(2,1)S(1)}, bf16[2,16,1024]{2,1,0:T(8,128)(2,1)S(1)}, u32[]{:S(2)}, u32[]{:S(2)}) collective-permute-start(bf16[2,16,1024]{2,1,0:T(8,128)(2,1)S(1)} %get-tuple-element.130.refs_2_), channel_id=1, source_target_pairs={{0,8},{1,9},{2,10},{3,11},{4,12},{5,13},{6,14},{7,15},{8,0},{9,1},... | collective-permute-start | bytes 196616 | tf_op jit(solution)/shard_map/ppermute | solution.py:136
  9.7 2.8 %shard_map.130 = (bf16[640,3584]{1,0:T(8,128)(2,1)S(1)}, bf16[640,3584]{1,0:T(8,128)(2,1)S(1)}) custom-call(bf16[640,3584]{1,0:T(8,128)(2,1)S(1)} %bitcast.33, bf16[640,3584]{1,0:T(8,128)(2,1)} %bitcast.36, bf16[2,16,1024]{2,1,0:T(8,128)(2,1)S(1)} %get-tuple-element.130.refs_2_), custom_call_target="tpu_custom_call" | custom-call | bytes 9175040 | tf_op jit(solution)/shard_map/pallas_call | solution.py:191
  12.6 2.5 %collective-permute-start.8 = (bf16[2,32,896]{2,1,0:T(8,128)(2,1)S(1)}, bf16[2,32,896]{2,1,0:T(8,128)(2,1)S(1)}, u32[]{:S(2)}, u32[]{:S(2)}) collective-permute-start(bf16[2,32,896]{2,1,0:T(8,128)(2,1)S(1)} %slice.35.refs_1_), channel_id=1, source_target_pairs={{0,3},{1,2},{2,1},{3,0},{4,7},{5,6},{6,5},{7,4},{8,11},{9,10},{10,... | collective-permute-start | bytes 344072 | tf_op jit(solution)/shard_map/ppermute | solution.py:136
  15.1 0.5 %collective-permute-start.5 = (bf16[2,32,896]{2,1,0:T(8,128)(2,1)S(1)}, bf16[2,32,896]{2,1,0:T(8,128)(2,1)S(1)}, u32[]{:S(2)}, u32[]{:S(2)}) collective-permute-start(bf16[2,32,896]{2,1,0:T(8,128)(2,1)S(1)} %slice.35.refs_1_), channel_id=1, source_target_pairs={{0,1},{1,0},{2,3},{3,2},{4,5},{5,4},{6,7},{7,6},{8,9},{9,8},{10,11... | collective-permute-start | bytes 344072 | tf_op jit(solution)/shard_map/ppermute | solution.py:136
  15.6 0.5 %collective-permute-start.3 = (bf16[2,32,896]{2,1,0:T(8,128)(2,1)S(1)}, bf16[2,32,896]{2,1,0:T(8,128)(2,1)S(1)}, u32[]{:S(2)}, u32[]{:S(2)}) collective-permute-start(bf16[2,32,896]{2,1,0:T(8,128)(2,1)S(1)} %slice.35.refs_1_), channel_id=1, source_target_pairs={{0,2},{1,3},{2,0},{3,1},{4,6},{5,7},{6,4},{7,5},{8,10},{9,11},{10,... | collective-permute-start | bytes 344072 | tf_op jit(solution)/shard_map/ppermute | solution.py:136
  17.7 1.2 %shard_map.132 = (bf16[64,896]{1,0:T(8,128)(2,1)S(1)}, bf16[64,896]{1,0:T(8,128)(2,1)S(1)}, f32[3,64,640]{2,1,0:T(8,128)S(1)}) custom-call(s32[1]{0:T(128)} %bitcast.5.refs_0_, bf16[2,32,896]{2,1,0:T(8,128)(2,1)S(1)} %slice.35.refs_1_, bf16[2,32,896]{2,1,0:T(8,128)(2,1)S(1)} %collective-permute-done.7.refs_2_, f32[64,1]{1,0:T(8,128)S(1)} %get-tuple-element.73.refs_3_, ...), custom_call_target="tpu_custom_call" | custom-call | flops 220200960 | bytes 3440640 | tf_op jit(solution)/shard_map/pallas_call | solution.py:402
  18.9 0.6 %collective-permute-start.9 = (bf16[2,32,896]{2,1,0:T(8,128)(2,1)S(1)}, bf16[2,32,896]{2,1,0:T(8,128)(2,1)S(1)}, u32[]{:S(2)}, u32[]{:S(2)}) collective-permute-start(bf16[2,32,896]{2,1,0:T(8,128)(2,1)S(1)} %collective-permute-done.8.refs_1_), channel_id=1, source_target_pairs={{0,4},{1,5},{2,6},{3,7},{4,0},{5,1},{6,2},{7,3},{8,12},{9,13},{10,... | collective-permute-start | bytes 344072 | tf_op jit(solution)/shard_map/ppermute | solution.py:136
  19.5 1.3 %collective-permute-done.5.refs_1_ = bf16[2,32,896]{2,1,0:T(8,128)(2,1)S(1)} collective-permute-done((bf16[2,32,896]{2,1,0:T(8,128)(2,1)S(1)}, bf16[2,32,896]{2,1,0:T(8,128)(2,1)S(1)}, u32[]{:S(2)}, u32[]{:S(2)}) %collective-permute-start.5) | collective-permute-done | bytes 114720 | tf_op jit(solution)/shard_map/ppermute | solution.py:136
  21.4 1.2 %shard_map.133 = (bf16[64,896]{1,0:T(8,128)(2,1)S(1)}, bf16[64,896]{1,0:T(8,128)(2,1)S(1)}, f32[3,64,640]{2,1,0:T(8,128)S(1)}) custom-call(s32[1]{0:T(128)} %bitcast.5.refs_0_, bf16[2,32,896]{2,1,0:T(8,128)(2,1)S(1)} %collective-permute-done.8.refs_1_, bf16[2,32,896]{2,1,0:T(8,128)(2,1)S(1)} %collective-permute-done.9.refs_2_, ...), custom_call_target="tpu_custom_call" | custom-call | flops 220200960 | bytes 3440640 | tf_op jit(solution)/shard_map/pallas_call | solution.py:402
  22.6 1.2 %shard_map.134 = (bf16[64,896]{1,0:T(8,128)(2,1)S(1)}, bf16[64,896]{1,0:T(8,128)(2,1)S(1)}, f32[3,64,640]{2,1,0:T(8,128)S(1)}) custom-call(s32[1]{0:T(128)} %bitcast.5.refs_0_, bf16[2,32,896]{2,1,0:T(8,128)(2,1)S(1)} %collective-permute-done.5.refs_1_, bf16[2,32,896]{2,1,0:T(8,128)(2,1)S(1)} %collective-permute-done.6.refs_2_, ...), custom_call_target="tpu_custom_call" | custom-call | flops 220200960 | bytes 3440640 | tf_op jit(solution)/shard_map/pallas_call | solution.py:402
  23.8 1.2 %shard_map.135 = (bf16[64,896]{1,0:T(8,128)(2,1)S(1)}, bf16[64,896]{1,0:T(8,128)(2,1)S(1)}, f32[3,64,640]{2,1,0:T(8,128)S(1)}) custom-call(s32[1]{0:T(128)} %bitcast.5.refs_0_, bf16[2,32,896]{2,1,0:T(8,128)(2,1)S(1)} %collective-permute-done.3.refs_1_, bf16[2,32,896]{2,1,0:T(8,128)(2,1)S(1)} %collective-permute-done.4.refs_2_, ...), custom_call_target="tpu_custom_call" | custom-call | flops 220200960 | bytes 3440640 | tf_op jit(solution)/shard_map/pallas_call | solution.py:402
  25.0 0.5 %shard_map.136 = (bf16[1,32,896]{2,1,0:T(8,128)(2,1)S(1)}, bf16[1,32,896]{2,1,0:T(8,128)(2,1)S(1)}, bf16[64,640]{1,0:T(8,128)(2,1)S(1)}, bf16[64,640]{1,0:T(8,128)(2,1)S(1)}, bf16[64,640]{1,0:T(8,128)(2,1)S(1)}) custom-call(s32[1]{0:T(128)} %bitcast.5.refs_0_, f32[64,640]{1,0:T(8,128)S(1)} %get-tuple-element.72.refs_1_, ...), custom_call_target="tpu_custom_call" | custom-call | flops 293601280 | bytes 4587520 | tf_op jit(solution)/shard_map/pallas_call | solution.py:421
  25.7 0.8 %shard_map.137 = (bf16[2,32,896]{2,1,0:T(8,128)(2,1)S(1)}, bf16[2,32,896]{2,1,0:T(8,128)(2,1)S(1)}, bf16[640,64]{1,0:T(8,128)(2,1)S(1)}, bf16[640,64]{1,0:T(8,128)(2,1)S(1)}, bf16[640,64]{1,0:T(8,128)(2,1)S(1)}) custom-call(s32[1]{0:T(128)} %bitcast.5.refs_0_, bf16[64,640]{1,0:T(8,128)(2,1)S(1)} %get-tuple-element.85.refs_1_, ...), custom_call_target="tpu_custom_call" | custom-call | flops 293601280 | bytes 4587520 | tf_op jit(solution)/shard_map/pallas_call | solution.py:427
  27.1 2.4 %collective-permute-start.13 = (bf16[32,896]{1,0:T(8,128)(2,1)S(1)}, bf16[32,896]{1,0:T(8,128)(2,1)S(1)}, u32[]{:S(2)}, u32[]{:S(2)}) collective-permute-start(bf16[32,896]{1,0:T(8,128)(2,1)S(1)} %fusion.8), channel_id=1, source_target_pairs={{0,3},{1,2},{2,1},{3,0},{4,7},{5,6},{6,5},{7,4},{8,11},{9,10},{10,... | collective-permute-start | bytes 172040 | tf_op jit(solution)/shard_map/ppermute | solution.py:136
  29.6 1.1 %collective-permute-start.14 = (bf16[32,896]{1,0:T(8,128)(2,1)S(1)}, bf16[32,896]{1,0:T(8,128)(2,1)S(1)}, u32[]{:S(2)}, u32[]{:S(2)}) collective-permute-start(bf16[32,896]{1,0:T(8,128)(2,1)S(1)} %get-tuple-element.96), channel_id=1, source_target_pairs={{0,2},{1,3},{2,0},{3,1},{4,6},{5,7},{6,4},{7,5},{8,10},{9,11},{10,... | collective-permute-start | bytes 172040 | tf_op jit(solution)/shard_map/ppermute | solution.py:136
  31.6 3.3 %shard_map.139 = (bf16[640,3584]{1,0:T(8,128)(2,1)}, bf16[640,3584]{1,0:T(8,128)(2,1)}) custom-call(s32[1]{0:T(128)} %bitcast.5.refs_0_, bf16[640,64]{1,0:T(8,128)(2,1)S(1)} %get-tuple-element.100.refs_1_, bf16[64,896]{1,0:T(8,128)(2,1)S(1)} %get-tuple-element.101.refs_2_, bf16[64,896]{1,0:T(8,128)(2,1)S(1)} %get-tuple-element.102.refs_3_, ...), custom_call_target="tpu_custom_call" | custom-call | flops 440401920 | bytes 6881280 | tf_op jit(solution)/shard_map/pallas_call | solution.py:334
  35.1 2.5 %collective-permute-start.16 = (bf16[2,8,896]{2,1,0:T(8,128)(2,1)S(1)}, bf16[2,8,896]{2,1,0:T(8,128)(2,1)S(1)}, u32[]{:S(2)}, u32[]{:S(2)}) collective-permute-start(bf16[2,8,896]{2,1,0:T(8,128)(2,1)S(1)} %slice.31), channel_id=1, source_target_pairs={{0,16},{1,17},{2,18},{3,19},{4,20},{5,21},{6,22},{7,23},{8,24},{9,... | collective-permute-start | bytes 86024 | tf_op jit(solution)/shard_map/ppermute | solution.py:136
  37.6 2.2 %shard_map.140 = (bf16[640,3584]{1,0:T(8,128)(2,1)}, bf16[640,3584]{1,0:T(8,128)(2,1)}) custom-call(s32[1]{0:T(128)} %bitcast.5.refs_0_, bf16[640,64]{1,0:T(8,128)(2,1)S(1)} %get-tuple-element.114.refs_6_.refs_1_, bf16[64,896]{1,0:T(8,128)(2,1)S(1)} %get-tuple-element.115.refs_2_.refs_3_, ...), custom_call_target="tpu_custom_call", output_to_operand_aliasing={{0}: (6, {})} | custom-call | flops 220200960 | bytes 3440640 | tf_op jit(solution)/shard_map/pallas_call | solution.py:334
  39.9 1.5 %collective-permute-start.17 = (bf16[1,8,896]{2,1,0:T(8,128)(2,1)S(1)}, bf16[1,8,896]{2,1,0:T(8,128)(2,1)S(1)}, u32[]{:S(2)}, u32[]{:S(2)}) collective-permute-start(bf16[1,8,896]{2,1,0:T(8,128)(2,1)S(1)} %slice.39), channel_id=1, source_target_pairs={{0,8},{1,9},{2,10},{3,11},{4,12},{5,13},{6,14},{7,15},{8,0},{9,1},... | collective-permute-start | bytes 43016 | tf_op jit(solution)/shard_map/ppermute | solution.py:136
  41.4 2.2 %shard_map.141 = bf16[640,3584]{1,0:T(8,128)(2,1)} custom-call(s32[1]{0:T(128)} %bitcast.5.refs_0_, bf16[640,64]{1,0:T(8,128)(2,1)S(1)} %get-tuple-element.122.refs_4_.refs_1_, bf16[64,896]{1,0:T(8,128)(2,1)S(1)} %get-tuple-element.107.refs_8_.refs_2_, bf16[64,896]{1,0:T(8,128)(2,1)S(1)} %get-tuple-element.115.refs_2_.refs_3_, ...), custom_call_target="tpu_custom_call", output_to_operand_aliasing={{}: (5, {})} | custom-call | flops 220200960 | bytes 3440640 | tf_op jit(solution)/shard_map/pallas_call | solution.py:334
  43.7 0.6 %fusion.10 = bf16[8,896]{1,0:T(8,128)(2,1)} fusion(bf16[1,8,896]{2,1,0:T(8,128)(2,1)S(1)} %collective-permute-done.17, bf16[2,8,896]{2,1,0:T(8,128)(2,1)S(1)} %add_convert_fusion.3), kind=kLoop, calls=%fused_computation.21 | loop fusion | flops 28672 | bytes 43008 | tf_op jit(solution)/shard_map/squeeze | solution.py:477
  (44 shorter events, 2.8 us)
Async XLA Ops:
  1.5 6.5 %collective-permute-start = (bf16[2,8,1024]{2,1,0:T(8,128)(2,1)S(1)}, bf16[2,8,1024]{2,1,0:T(8,128)(2,1)S(1)}, u32[]{:S(2)}, u32[]{:S(2)}) collective-permute-start(bf16[2,8,1024]{2,1,0:T(8,128)(2,1)S(1)} %fusion.6.refs_1_), channel_id=1, source_target_pairs={{0,16},{1,17},{2,18},{3,19},{4,20},{5,21},{6,22},{7,23},{8,24},{9,... | collective-permute-start | bytes 98312 | tf_op jit(solution)/shard_map/ppermute | solution.py:136
  5.6 4.2 %slice-start = ((s8[4587520]{0:T(1024)(128)(4,1)}), s8[4194304]{0:T(1024)(128)(4,1)S(1)}, s32[]{:S(2)}) async-start(s8[4587520]{0:T(1024)(128)(4,1)} %bitcast.31), calls=%async_computation | async-start | bytes 8388608
  5.6 4.2 %slice-start.1 = ((s8[4587520]{0:T(1024)(128)(4,1)}), s8[393216]{0:T(1024)(128)(4,1)S(1)}, s32[]{:S(2)}) async-start(s8[4587520]{0:T(1024)(128)(4,1)} %bitcast.31), calls=%async_computation.1 | async-start | bytes 786432
  8.1 4.4 %collective-permute-start.1 = (bf16[2,16,1024]{2,1,0:T(8,128)(2,1)S(1)}, bf16[2,16,1024]{2,1,0:T(8,128)(2,1)S(1)}, u32[]{:S(2)}, u32[]{:S(2)}) collective-permute-start(bf16[2,16,1024]{2,1,0:T(8,128)(2,1)S(1)} %get-tuple-element.130.refs_2_), channel_id=1, source_target_pairs={{0,8},{1,9},{2,10},{3,11},{4,12},{5,13},{6,14},{7,15},{8,0},{9,1},... | collective-permute-start | bytes 196616 | tf_op jit(solution)/shard_map/ppermute | solution.py:136
  12.6 6.3 %collective-permute-start.8 = (bf16[2,32,896]{2,1,0:T(8,128)(2,1)S(1)}, bf16[2,32,896]{2,1,0:T(8,128)(2,1)S(1)}, u32[]{:S(2)}, u32[]{:S(2)}) collective-permute-start(bf16[2,32,896]{2,1,0:T(8,128)(2,1)S(1)} %slice.35.refs_1_), channel_id=1, source_target_pairs={{0,3},{1,2},{2,1},{3,0},{4,7},{5,6},{6,5},{7,4},{8,11},{9,10},{10,... | collective-permute-start | bytes 344072 | tf_op jit(solution)/shard_map/ppermute | solution.py:136
  15.1 2.6 %collective-permute-start.7 = (bf16[2,32,896]{2,1,0:T(8,128)(2,1)S(1)}, bf16[2,32,896]{2,1,0:T(8,128)(2,1)S(1)}, u32[]{:S(2)}, u32[]{:S(2)}) collective-permute-start(bf16[2,32,896]{2,1,0:T(8,128)(2,1)S(1)} %slice.35.refs_1_), channel_id=1, source_target_pairs={{0,4},{1,5},{2,6},{3,7},{4,0},{5,1},{6,2},{7,3},{8,12},{9,13},{10,... | collective-permute-start | bytes 344072 | tf_op jit(solution)/shard_map/ppermute | solution.py:136
  15.1 5.8 %collective-permute-start.5 = (bf16[2,32,896]{2,1,0:T(8,128)(2,1)S(1)}, bf16[2,32,896]{2,1,0:T(8,128)(2,1)S(1)}, u32[]{:S(2)}, u32[]{:S(2)}) collective-permute-start(bf16[2,32,896]{2,1,0:T(8,128)(2,1)S(1)} %slice.35.refs_1_), channel_id=1, source_target_pairs={{0,1},{1,0},{2,3},{3,2},{4,5},{5,4},{6,7},{7,6},{8,9},{9,8},{10,11... | collective-permute-start | bytes 344072 | tf_op jit(solution)/shard_map/ppermute | solution.py:136
  15.6 5.3 %collective-permute-start.3 = (bf16[2,32,896]{2,1,0:T(8,128)(2,1)S(1)}, bf16[2,32,896]{2,1,0:T(8,128)(2,1)S(1)}, u32[]{:S(2)}, u32[]{:S(2)}) collective-permute-start(bf16[2,32,896]{2,1,0:T(8,128)(2,1)S(1)} %slice.35.refs_1_), channel_id=1, source_target_pairs={{0,2},{1,3},{2,0},{3,1},{4,6},{5,7},{6,4},{7,5},{8,10},{9,11},{10,... | collective-permute-start | bytes 344072 | tf_op jit(solution)/shard_map/ppermute | solution.py:136
  16.1 1.3 %collective-permute-start.2 = (bf16[32,128]{1,0:T(8,128)(2,1)S(1)}, bf16[32,128]{1,0:T(8,128)(2,1)S(1)}, u32[]{:S(2)}, u32[]{:S(2)}) collective-permute-start(bf16[32,128]{1,0:T(8,128)(2,1)S(1)} %slice_bitcast_fusion.2.refs_3_), channel_id=1, source_target_pairs={{0,4},{1,5},{2,6},{3,7},{4,0},{5,1},{6,2},{7,3},{8,12},{9,13},{10,... | collective-permute-start | bytes 24584 | tf_op jit(solution)/shard_map/ppermute | solution.py:136
  18.9 2.4 %collective-permute-start.9 = (bf16[2,32,896]{2,1,0:T(8,128)(2,1)S(1)}, bf16[2,32,896]{2,1,0:T(8,128)(2,1)S(1)}, u32[]{:S(2)}, u32[]{:S(2)}) collective-permute-start(bf16[2,32,896]{2,1,0:T(8,128)(2,1)S(1)} %collective-permute-done.8.refs_1_), channel_id=1, source_target_pairs={{0,4},{1,5},{2,6},{3,7},{4,0},{5,1},{6,2},{7,3},{8,12},{9,13},{10,... | collective-permute-start | bytes 344072 | tf_op jit(solution)/shard_map/ppermute | solution.py:136
  20.9 1.7 %collective-permute-start.6 = (bf16[2,32,896]{2,1,0:T(8,128)(2,1)S(1)}, bf16[2,32,896]{2,1,0:T(8,128)(2,1)S(1)}, u32[]{:S(2)}, u32[]{:S(2)}) collective-permute-start(bf16[2,32,896]{2,1,0:T(8,128)(2,1)S(1)} %collective-permute-done.5.refs_1_), channel_id=1, source_target_pairs={{0,4},{1,5},{2,6},{3,7},{4,0},{5,1},{6,2},{7,3},{8,12},{9,13},{10,... | collective-permute-start | bytes 344072 | tf_op jit(solution)/shard_map/ppermute | solution.py:136
  20.9 2.9 %collective-permute-start.4 = (bf16[2,32,896]{2,1,0:T(8,128)(2,1)S(1)}, bf16[2,32,896]{2,1,0:T(8,128)(2,1)S(1)}, u32[]{:S(2)}, u32[]{:S(2)}) collective-permute-start(bf16[2,32,896]{2,1,0:T(8,128)(2,1)S(1)} %collective-permute-done.3.refs_1_), channel_id=1, source_target_pairs={{0,4},{1,5},{2,6},{3,7},{4,0},{5,1},{6,2},{7,3},{8,12},{9,13},{10,... | collective-permute-start | bytes 344072 | tf_op jit(solution)/shard_map/ppermute | solution.py:136
  25.6 1.3 %collective-permute-start.10 = (bf16[1,32,896]{2,1,0:T(8,128)(2,1)S(1)}, bf16[1,32,896]{2,1,0:T(8,128)(2,1)S(1)}, u32[]{:S(2)}, u32[]{:S(2)}) collective-permute-start(bf16[1,32,896]{2,1,0:T(8,128)(2,1)S(1)} %get-tuple-element.84), channel_id=1, source_target_pairs={{0,4},{1,5},{2,6},{3,7},{4,0},{5,1},{6,2},{7,3},{8,12},{9,13},{10,... | collective-permute-start | bytes 172040 | tf_op jit(solution)/shard_map/ppermute | solution.py:136
  26.9 2.6 %collective-permute-start.11 = (bf16[2,32,896]{2,1,0:T(8,128)(2,1)S(1)}, bf16[2,32,896]{2,1,0:T(8,128)(2,1)S(1)}, u32[]{:S(2)}, u32[]{:S(2)}) collective-permute-start(bf16[2,32,896]{2,1,0:T(8,128)(2,1)S(1)} %get-tuple-element.90), channel_id=1, source_target_pairs={{0,4},{1,5},{2,6},{3,7},{4,0},{5,1},{6,2},{7,3},{8,12},{9,13},{10,... | collective-permute-start | bytes 344072 | tf_op jit(solution)/shard_map/ppermute | solution.py:136
  27.1 7.9 %collective-permute-start.13 = (bf16[32,896]{1,0:T(8,128)(2,1)S(1)}, bf16[32,896]{1,0:T(8,128)(2,1)S(1)}, u32[]{:S(2)}, u32[]{:S(2)}) collective-permute-start(bf16[32,896]{1,0:T(8,128)(2,1)S(1)} %fusion.8), channel_id=1, source_target_pairs={{0,3},{1,2},{2,1},{3,0},{4,7},{5,6},{6,5},{7,4},{8,11},{9,10},{10,... | collective-permute-start | bytes 172040 | tf_op jit(solution)/shard_map/ppermute | solution.py:136
  29.6 5.4 %collective-permute-start.14 = (bf16[32,896]{1,0:T(8,128)(2,1)S(1)}, bf16[32,896]{1,0:T(8,128)(2,1)S(1)}, u32[]{:S(2)}, u32[]{:S(2)}) collective-permute-start(bf16[32,896]{1,0:T(8,128)(2,1)S(1)} %get-tuple-element.96), channel_id=1, source_target_pairs={{0,2},{1,3},{2,0},{3,1},{4,6},{5,7},{6,4},{7,5},{8,10},{9,11},{10,... | collective-permute-start | bytes 172040 | tf_op jit(solution)/shard_map/ppermute | solution.py:136
  30.6 4.4 %collective-permute-start.15 = (bf16[32,896]{1,0:T(8,128)(2,1)S(1)}, bf16[32,896]{1,0:T(8,128)(2,1)S(1)}, u32[]{:S(2)}, u32[]{:S(2)}) collective-permute-start(bf16[32,896]{1,0:T(8,128)(2,1)S(1)} %get-tuple-element.97), channel_id=1, source_target_pairs={{0,1},{1,0},{2,3},{3,2},{4,5},{5,4},{6,7},{7,6},{8,9},{9,8},{10,11... | collective-permute-start | bytes 172040 | tf_op jit(solution)/shard_map/ppermute | solution.py:136
  31.6 3.4 %collective-permute-start.12 = (bf16[1,32,896]{2,1,0:T(8,128)(2,1)S(1)}, bf16[1,32,896]{2,1,0:T(8,128)(2,1)S(1)}, u32[]{:S(2)}, u32[]{:S(2)}) collective-permute-start(bf16[1,32,896]{2,1,0:T(8,128)(2,1)S(1)} %get-tuple-element.93), channel_id=1, source_target_pairs={{0,4},{1,5},{2,6},{3,7},{4,0},{5,1},{6,2},{7,3},{8,12},{9,13},{10,... | collective-permute-start | bytes 172040 | tf_op jit(solution)/shard_map/ppermute | solution.py:136
  35.1 4.8 %collective-permute-start.16 = (bf16[2,8,896]{2,1,0:T(8,128)(2,1)S(1)}, bf16[2,8,896]{2,1,0:T(8,128)(2,1)S(1)}, u32[]{:S(2)}, u32[]{:S(2)}) collective-permute-start(bf16[2,8,896]{2,1,0:T(8,128)(2,1)S(1)} %slice.31), channel_id=1, source_target_pairs={{0,16},{1,17},{2,18},{3,19},{4,20},{5,21},{6,22},{7,23},{8,24},{9,... | collective-permute-start | bytes 86024 | tf_op jit(solution)/shard_map/ppermute | solution.py:136
  39.9 3.8 %collective-permute-start.17 = (bf16[1,8,896]{2,1,0:T(8,128)(2,1)S(1)}, bf16[1,8,896]{2,1,0:T(8,128)(2,1)S(1)}, u32[]{:S(2)}, u32[]{:S(2)}) collective-permute-start(bf16[1,8,896]{2,1,0:T(8,128)(2,1)S(1)} %slice.39), channel_id=1, source_target_pairs={{0,8},{1,9},{2,10},{3,11},{4,12},{5,13},{6,14},{7,15},{8,0},{9,1},... | collective-permute-start | bytes 43016 | tf_op jit(solution)/shard_map/ppermute | solution.py:136

commit v5 on v4

--- a/solution.py
+++ b/solution.py
@@ -234,9 +234,7 @@
     keep_ref[...] = jnp.where(levels >= 102, KEEP_FACTOR, 0.0).astype(F32)
 
 
-def pre_kernel(part, first, *refs):
-    place_ref, own_ref, other_ref, gate_ref, wg, wu, wd = refs[:7]
-    x_ref, dy_ref, acc_ref = refs[-3:]
+def products(part, place_ref, own_ref, other_ref, gate_ref, wg, wu, wd, x_ref, dy_ref, acc_ref):
     width = own_ref.shape[2]
     cols = columns(place_ref[0], part, wg.shape[1] // width, width)
     x = jnp.concatenate([own_ref[0], other_ref[0]], axis=0)
@@ -244,9 +242,15 @@
     dy = (gate_ref[...] * c.astype(F32)).astype(BF16)
     x_ref[...] = x
     dy_ref[...] = dy
-    for i, (left, weight) in enumerate(((x, wg), (x, wu), (dy, wd))):
-        term = contract_last(left, weight[:, cols])
-        acc_ref[i] = term if first else refs[7][i] + term
+    terms = [contract_last(left, w[:, cols]) for left, w in ((x, wg), (x, wu), (dy, wd))]
+    return terms if acc_ref is None else [acc_ref[i] + term for i, term in enumerate(terms)]
+
+
+def pre_kernel(part, first, *refs):
+    x_ref, dy_ref, acc_ref = refs[-3:]
+    before = None if first else refs[7]
+    for i, term in enumerate(products(part, *refs[:7], x_ref, dy_ref, before)):
+        acc_ref[i] = term
 
 
 def pieces(me, part_ids, g, u, wg, wu, keep_ref, send_ref):
@@ -262,12 +266,14 @@
 
 
 def hidden_kernel(
-    part_ids, place_ref, mul_ref, acc_ref, wg, wu, keep_ref, send_ref, h_ref, g_ref, u_ref
+    part, part_ids, place_ref, own_ref, other_ref, gate_ref, wg, wu, wd, acc_ref, mul_ref,
+    x_ref, dy_ref, keep_ref, send_ref, h_ref, g_ref, u_ref,
 ):
     keep_mul = mul_ref[...]
-    gate_pre = acc_ref[0]
-    up_pre = acc_ref[1]
-    grad_hidden = acc_ref[2] * keep_mul
+    gate_pre, up_pre, grad_hidden = products(
+        part, place_ref, own_ref, other_ref, gate_ref, wg, wu, wd, x_ref, dy_ref, acc_ref
+    )
+    grad_hidden = grad_hidden * keep_mul
     logistic = jax.nn.sigmoid(gate_pre)
     swish = gate_pre * logistic
     u = (grad_hidden * swish).astype(BF16)
@@ -399,6 +405,8 @@
     for n, j in enumerate(order):
         held = [] if acc is None else [acc]
         other = others[j]
+        if n == parts - 1:
+            break
         xs[j], dys[j], acc = call(
             lambda *refs, j=j, n=n: pre_kernel(j, n == 0, *refs),
             [SMEM] + [VMEM] * (6 + len(held)), [VMEM] * 3,
@@ -418,11 +426,12 @@
     turned = shape((units, rows))
     straight = shape((rows, units))
     flops = 4 * rows * units * width * (parts // 2)
-    keep, send, h, g, u = call(
-        lambda *refs: hidden_kernel(high, *refs), [SMEM] + [VMEM] * 4, [VMEM] * 5,
-        [block, block, straight, straight, straight],
+    last = order[-1]
+    xs[last], dys[last], keep, send, h, g, u = call(
+        lambda *refs: hidden_kernel(last, high, *refs), [SMEM] + [VMEM] * 8, [VMEM] * 7,
+        [shape((rows, width)), shape((rows, width)), block, block, straight, straight, straight],
         flops=flops, moved=2 * units * width * parts,
-    )(place, keep_mul, acc, wg, wu)
+    )(place, own[last], others[last], gate, wg, wu, wd, acc, keep_mul)
     upper_keep, upper_came = keep, swap(send, parts, size)
     keep, send, hid_t, g_t, u_t = call(
         lambda *refs: turning_kernel(low, *refs), [SMEM] + [VMEM] * 5, [VMEM] * 5,

time: 44.6 us -> 44.6 us (level)
    pallas_call x1, Pallas kernels: 0.53 us -> 1.74 us  [token_device(): call(lambda *refs: hidden_kernel(last, high, *refs), [SMEM] + [VMEM] * 8,...]
    pallas_call x4 -> x3, Pallas kernels: 4.83 us -> 3.62 us  [token_device(): call(lambda *refs, j=j, n=n: pre_kernel(j, n == 0, *refs), [SMEM] + [VMEM...]
where the time goes in v5:
time: 44.6 us; the launch traced here: 44.3 us
  Pallas kernels  19.9 us (45%)
  starting transfers between devices  18.6 us (42%)
  between operations  2.21 us (5%)
  waiting for transfers between devices  1.91 us (4%)
  other arithmetic  1.6 us (4%)
    ppermute x18, starting transfers between devices, swap(): return lax.ppermute(value, AXES, [(i, i ^ distance) for i in range(size)])  18.6 us
    pallas_call x3, Pallas kernels, weight_grads(): pl.pallas_call(lambda *refs: weight_kernel(ids, parts, cuts, *refs), in_s...  7.72 us
    pallas_call x2, Pallas kernels, load(): call(lambda *refs: load_kernel(count, *refs), [HBM] * count + [VMEM], [VM...  5.25 us
    pallas_call x3, Pallas kernels, token_device(): call(lambda *refs, j=j, n=n: pre_kernel(j, n == 0, *refs), [SMEM] + [VMEM...  3.62 us
    ppermute x18, waiting for transfers between devices, swap(): return lax.ppermute(value, AXES, [(i, i ^ distance) for i in range(size)])  1.91 us
    pallas_call x1, Pallas kernels, token_device(): call(lambda *refs: hidden_kernel(last, high, *refs), [SMEM] + [VMEM] * 8,...  1.74 us
    convert_element_type x1, other arithmetic, pack(): return (put(tokens, 0, 0).astype(F32) + put(cotangent, 1, 0).astype(F32)...  0.89 us
  transfers between devices with their start and end apart: 18, of which 5 were waited for; matrix products, arithmetic and copies ran while one was open for 0% of the time, Pallas kernels for 41%

profile of v5, /device:TPU:0, one launch (start us, length us, event | category | flops | bytes accessed | tf_op | source)
XLA Modules:
  0.0 44.3 jit_solution(11017437496121174584)
XLA Ops:
  0.6 0.9 %fusion.6.refs_1_ = bf16[2,8,1024]{2,1,0:T(8,128)(2,1)S(1)} fusion(f32[1,8,8]{2,1,0:T(8,128)} %bitcast.40, s32[1,8,8]{2,1,0:T(8,128)} %bitcast.41, s32[1,8,8]{2,1,0:T(8,128)} %bitcast.42, bf16[1,8,896]{2,1,0:T(8,128)(2,1)} %bitcast.38, bf16[1,8,896]{2,1,0:T(8,128)(2,1)} %bitcast.39), kind=kLoop, calls=%fused_computation.13 | loop fusion | flops 311296 | bytes 62208 | tf_op jit(solution)/shard_map/convert_element_type | solution.py:175
  1.5 4.0 %collective-permute-start = (bf16[2,8,1024]{2,1,0:T(8,128)(2,1)S(1)}, bf16[2,8,1024]{2,1,0:T(8,128)(2,1)S(1)}, u32[]{:S(2)}, u32[]{:S(2)}) collective-permute-start(bf16[2,8,1024]{2,1,0:T(8,128)(2,1)S(1)} %fusion.6.refs_1_), channel_id=1, source_target_pairs={{0,16},{1,17},{2,18},{3,19},{4,20},{5,21},{6,22},{7,23},{8,24},{9,... | collective-permute-start | bytes 98312 | tf_op jit(solution)/shard_map/ppermute | solution.py:136
  5.6 2.5 %shard_map.129.refs_4_.refs_3_ = bf16[640,3584]{1,0:T(8,128)(2,1)S(1)} custom-call(bf16[640,3584]{1,0:T(8,128)(2,1)} %bitcast.35, bf16[2,8,1024]{2,1,0:T(8,128)(2,1)S(1)} %fusion.6.refs_1_), custom_call_target="tpu_custom_call" | custom-call | bytes 4587520 | tf_op jit(solution)/shard_map/pallas_call | solution.py:191
  8.1 1.6 %collective-permute-start.1 = (bf16[2,16,1024]{2,1,0:T(8,128)(2,1)S(1)}, bf16[2,16,1024]{2,1,0:T(8,128)(2,1)S(1)}, u32[]{:S(2)}, u32[]{:S(2)}) collective-permute-start(bf16[2,16,1024]{2,1,0:T(8,128)(2,1)S(1)} %get-tuple-element.128.refs_2_), channel_id=1, source_target_pairs={{0,8},{1,9},{2,10},{3,11},{4,12},{5,13},{6,14},{7,15},{8,0},{9,1},... | collective-permute-start | bytes 196616 | tf_op jit(solution)/shard_map/ppermute | solution.py:136
  9.7 2.8 %shard_map.130 = (bf16[640,3584]{1,0:T(8,128)(2,1)S(1)}, bf16[640,3584]{1,0:T(8,128)(2,1)S(1)}) custom-call(bf16[640,3584]{1,0:T(8,128)(2,1)S(1)} %bitcast.33, bf16[640,3584]{1,0:T(8,128)(2,1)} %bitcast.36, bf16[2,16,1024]{2,1,0:T(8,128)(2,1)S(1)} %get-tuple-element.128.refs_2_), custom_call_target="tpu_custom_call" | custom-call | bytes 9175040 | tf_op jit(solution)/shard_map/pallas_call | solution.py:191
  12.6 2.5 %collective-permute-start.8 = (bf16[2,32,896]{2,1,0:T(8,128)(2,1)S(1)}, bf16[2,32,896]{2,1,0:T(8,128)(2,1)S(1)}, u32[]{:S(2)}, u32[]{:S(2)}) collective-permute-start(bf16[2,32,896]{2,1,0:T(8,128)(2,1)S(1)} %slice.34.refs_1_), channel_id=1, source_target_pairs={{0,3},{1,2},{2,1},{3,0},{4,7},{5,6},{6,5},{7,4},{8,11},{9,10},{10,... | collective-permute-start | bytes 344072 | tf_op jit(solution)/shard_map/ppermute | solution.py:136
  15.1 0.5 %collective-permute-start.5 = (bf16[2,32,896]{2,1,0:T(8,128)(2,1)S(1)}, bf16[2,32,896]{2,1,0:T(8,128)(2,1)S(1)}, u32[]{:S(2)}, u32[]{:S(2)}) collective-permute-start(bf16[2,32,896]{2,1,0:T(8,128)(2,1)S(1)} %slice.34.refs_1_), channel_id=1, source_target_pairs={{0,1},{1,0},{2,3},{3,2},{4,5},{5,4},{6,7},{7,6},{8,9},{9,8},{10,11... | collective-permute-start | bytes 344072 | tf_op jit(solution)/shard_map/ppermute | solution.py:136
  15.6 0.5 %collective-permute-start.2 = (bf16[2,32,896]{2,1,0:T(8,128)(2,1)S(1)}, bf16[2,32,896]{2,1,0:T(8,128)(2,1)S(1)}, u32[]{:S(2)}, u32[]{:S(2)}) collective-permute-start(bf16[2,32,896]{2,1,0:T(8,128)(2,1)S(1)} %slice.34.refs_1_), channel_id=1, source_target_pairs={{0,2},{1,3},{2,0},{3,1},{4,6},{5,7},{6,4},{7,5},{8,10},{9,11},{10,... | collective-permute-start | bytes 344072 | tf_op jit(solution)/shard_map/ppermute | solution.py:136
  17.7 1.2 %shard_map.132 = (bf16[64,896]{1,0:T(8,128)(2,1)S(1)}, bf16[64,896]{1,0:T(8,128)(2,1)S(1)}, f32[3,64,640]{2,1,0:T(8,128)S(1)}) custom-call(s32[1]{0:T(128)} %bitcast.5.refs_0_, bf16[2,32,896]{2,1,0:T(8,128)(2,1)S(1)} %slice.34.refs_1_, bf16[2,32,896]{2,1,0:T(8,128)(2,1)S(1)} %collective-permute-done.7.refs_2_, f32[64,1]{1,0:T(8,128)S(1)} %get-tuple-element.71.refs_3_, ...), custom_call_target="tpu_custom_call" | custom-call | flops 220200960 | bytes 3440640 | tf_op jit(solution)/shard_map/pallas_call | solution.py:410
  18.9 0.6 %collective-permute-start.9 = (bf16[2,32,896]{2,1,0:T(8,128)(2,1)S(1)}, bf16[2,32,896]{2,1,0:T(8,128)(2,1)S(1)}, u32[]{:S(2)}, u32[]{:S(2)}) collective-permute-start(bf16[2,32,896]{2,1,0:T(8,128)(2,1)S(1)} %collective-permute-done.8.refs_1_), channel_id=1, source_target_pairs={{0,4},{1,5},{2,6},{3,7},{4,0},{5,1},{6,2},{7,3},{8,12},{9,13},{10,... | collective-permute-start | bytes 344072 | tf_op jit(solution)/shard_map/ppermute | solution.py:136
  19.5 1.3 %collective-permute-done.5.refs_1_ = bf16[2,32,896]{2,1,0:T(8,128)(2,1)S(1)} collective-permute-done((bf16[2,32,896]{2,1,0:T(8,128)(2,1)S(1)}, bf16[2,32,896]{2,1,0:T(8,128)(2,1)S(1)}, u32[]{:S(2)}, u32[]{:S(2)}) %collective-permute-start.5) | collective-permute-done | bytes 114720 | tf_op jit(solution)/shard_map/ppermute | solution.py:136
  21.4 1.2 %shard_map.133 = (bf16[64,896]{1,0:T(8,128)(2,1)S(1)}, bf16[64,896]{1,0:T(8,128)(2,1)S(1)}, f32[3,64,640]{2,1,0:T(8,128)S(1)}) custom-call(s32[1]{0:T(128)} %bitcast.5.refs_0_, bf16[2,32,896]{2,1,0:T(8,128)(2,1)S(1)} %collective-permute-done.8.refs_1_, bf16[2,32,896]{2,1,0:T(8,128)(2,1)S(1)} %collective-permute-done.9.refs_2_, ...), custom_call_target="tpu_custom_call" | custom-call | flops 220200960 | bytes 3440640 | tf_op jit(solution)/shard_map/pallas_call | solution.py:410
  22.6 1.2 %shard_map.134 = (bf16[64,896]{1,0:T(8,128)(2,1)S(1)}, bf16[64,896]{1,0:T(8,128)(2,1)S(1)}, f32[3,64,640]{2,1,0:T(8,128)S(1)}) custom-call(s32[1]{0:T(128)} %bitcast.5.refs_0_, bf16[2,32,896]{2,1,0:T(8,128)(2,1)S(1)} %collective-permute-done.5.refs_1_, bf16[2,32,896]{2,1,0:T(8,128)(2,1)S(1)} %collective-permute-done.6.refs_2_, ...), custom_call_target="tpu_custom_call" | custom-call | flops 220200960 | bytes 3440640 | tf_op jit(solution)/shard_map/pallas_call | solution.py:410
  23.8 1.7 %shard_map.135 = (bf16[64,896]{1,0:T(8,128)(2,1)S(1)}, bf16[64,896]{1,0:T(8,128)(2,1)S(1)}, bf16[1,32,896]{2,1,0:T(8,128)(2,1)S(1)}, bf16[1,32,896]{2,1,0:T(8,12...) custom-call(s32[1]{0:T(128)} %bitcast.5.refs_0_, ...), custom_call_target="tpu_custom_call" | custom-call | flops 293601280 | bytes 4587520 | tf_op jit(solution)/shard_map/pallas_call | solution.py:430
  25.7 0.8 %shard_map.136 = (bf16[2,32,896]{2,1,0:T(8,128)(2,1)S(1)}, bf16[2,32,896]{2,1,0:T(8,128)(2,1)S(1)}, bf16[640,64]{1,0:T(8,128)(2,1)S(1)}, bf16[640,64]{1,0:T(8,128)(2,1)S(1)}, bf16[640,64]{1,0:T(8,128)(2,1)S(1)}) custom-call(s32[1]{0:T(128)} %bitcast.5.refs_0_, bf16[64,640]{1,0:T(8,128)(2,1)S(1)} %get-tuple-element.83.refs_1_, ...), custom_call_target="tpu_custom_call" | custom-call | flops 293601280 | bytes 4587520 | tf_op jit(solution)/shard_map/pallas_call | solution.py:436
  27.1 2.4 %collective-permute-start.13 = (bf16[32,896]{1,0:T(8,128)(2,1)S(1)}, bf16[32,896]{1,0:T(8,128)(2,1)S(1)}, u32[]{:S(2)}, u32[]{:S(2)}) collective-permute-start(bf16[32,896]{1,0:T(8,128)(2,1)S(1)} %fusion.8), channel_id=1, source_target_pairs={{0,3},{1,2},{2,1},{3,0},{4,7},{5,6},{6,5},{7,4},{8,11},{9,10},{10,... | collective-permute-start | bytes 172040 | tf_op jit(solution)/shard_map/ppermute | solution.py:136
  29.5 1.1 %collective-permute-start.14 = (bf16[32,896]{1,0:T(8,128)(2,1)S(1)}, bf16[32,896]{1,0:T(8,128)(2,1)S(1)}, u32[]{:S(2)}, u32[]{:S(2)}) collective-permute-start(bf16[32,896]{1,0:T(8,128)(2,1)S(1)} %get-tuple-element.94), channel_id=1, source_target_pairs={{0,2},{1,3},{2,0},{3,1},{4,6},{5,7},{6,4},{7,5},{8,10},{9,11},{10,... | collective-permute-start | bytes 172040 | tf_op jit(solution)/shard_map/ppermute | solution.py:136
  31.1 0.5 %shard_map.137 = (bf16[1,32,896]{2,1,0:T(8,128)(2,1)S(1)}, bf16[1,32,896]{2,1,0:T(8,128)(2,1)S(1)}) custom-call(s32[1]{0:T(128)} %bitcast.5.refs_0_, bf16[64,640]{1,0:T(8,128)(2,1)S(1)} %get-tuple-element.89.refs_2_.refs_1_, bf16[64,640]{1,0:T(8,128)(2,1)S(1)} %get-tuple-element.84.refs_3_.refs_2_, bf16[640,3584]{1,0:T(8,128)(2,1)S(1)} %shard_map.129.refs_4_.refs_3_, ...), custom_call_target="tpu_custom_call" | custom-call | flops 293601280 | bytes 4587520 | tf_op jit(solution)/shard_map/pallas_call | solution.py:444
  31.6 3.3 %shard_map.138 = (bf16[640,3584]{1,0:T(8,128)(2,1)}, bf16[640,3584]{1,0:T(8,128)(2,1)}) custom-call(s32[1]{0:T(128)} %bitcast.5.refs_0_, bf16[640,64]{1,0:T(8,128)(2,1)S(1)} %get-tuple-element.98.refs_1_, bf16[64,896]{1,0:T(8,128)(2,1)S(1)} %get-tuple-element.99.refs_2_, bf16[64,896]{1,0:T(8,128)(2,1)S(1)} %get-tuple-element.100.refs_3_, ...), custom_call_target="tpu_custom_call" | custom-call | flops 440401920 | bytes 6881280 | tf_op jit(solution)/shard_map/pallas_call | solution.py:340
  35.0 2.5 %collective-permute-start.16 = (bf16[2,8,896]{2,1,0:T(8,128)(2,1)S(1)}, bf16[2,8,896]{2,1,0:T(8,128)(2,1)S(1)}, u32[]{:S(2)}, u32[]{:S(2)}) collective-permute-start(bf16[2,8,896]{2,1,0:T(8,128)(2,1)S(1)} %slice.31), channel_id=1, source_target_pairs={{0,16},{1,17},{2,18},{3,19},{4,20},{5,21},{6,22},{7,23},{8,24},{9,... | collective-permute-start | bytes 86024 | tf_op jit(solution)/shard_map/ppermute | solution.py:136
  37.6 2.2 %shard_map.139 = (bf16[640,3584]{1,0:T(8,128)(2,1)}, bf16[640,3584]{1,0:T(8,128)(2,1)}) custom-call(s32[1]{0:T(128)} %bitcast.5.refs_0_, bf16[640,64]{1,0:T(8,128)(2,1)S(1)} %get-tuple-element.112.refs_6_.refs_1_, bf16[64,896]{1,0:T(8,128)(2,1)S(1)} %get-tuple-element.113.refs_2_.refs_3_, ...), custom_call_target="tpu_custom_call", output_to_operand_aliasing={{0}: (6, {})} | custom-call | flops 220200960 | bytes 3440640 | tf_op jit(solution)/shard_map/pallas_call | solution.py:340
  39.9 1.5 %collective-permute-start.17 = (bf16[1,8,896]{2,1,0:T(8,128)(2,1)S(1)}, bf16[1,8,896]{2,1,0:T(8,128)(2,1)S(1)}, u32[]{:S(2)}, u32[]{:S(2)}) collective-permute-start(bf16[1,8,896]{2,1,0:T(8,128)(2,1)S(1)} %slice.39), channel_id=1, source_target_pairs={{0,8},{1,9},{2,10},{3,11},{4,12},{5,13},{6,14},{7,15},{8,0},{9,1},... | collective-permute-start | bytes 43016 | tf_op jit(solution)/shard_map/ppermute | solution.py:136
  41.4 2.2 %shard_map.140 = bf16[640,3584]{1,0:T(8,128)(2,1)} custom-call(s32[1]{0:T(128)} %bitcast.5.refs_0_, bf16[640,64]{1,0:T(8,128)(2,1)S(1)} %get-tuple-element.120.refs_4_.refs_1_, bf16[64,896]{1,0:T(8,128)(2,1)S(1)} %get-tuple-element.105.refs_8_.refs_2_, bf16[64,896]{1,0:T(8,128)(2,1)S(1)} %get-tuple-element.113.refs_2_.refs_3_, ...), custom_call_target="tpu_custom_call", output_to_operand_aliasing={{}: (5, {})} | custom-call | flops 220200960 | bytes 3440640 | tf_op jit(solution)/shard_map/pallas_call | solution.py:340
  43.7 0.6 %fusion.10 = bf16[8,896]{1,0:T(8,128)(2,1)} fusion(bf16[1,8,896]{2,1,0:T(8,128)(2,1)S(1)} %collective-permute-done.17, bf16[2,8,896]{2,1,0:T(8,128)(2,1)S(1)} %add_convert_fusion.3), kind=kLoop, calls=%fused_computation.21 | loop fusion | flops 28672 | bytes 43008 | tf_op jit(solution)/shard_map/squeeze | solution.py:486
  (43 shorter events, 2.2 us)
Async XLA Ops:
  1.5 6.5 %collective-permute-start = (bf16[2,8,1024]{2,1,0:T(8,128)(2,1)S(1)}, bf16[2,8,1024]{2,1,0:T(8,128)(2,1)S(1)}, u32[]{:S(2)}, u32[]{:S(2)}) collective-permute-start(bf16[2,8,1024]{2,1,0:T(8,128)(2,1)S(1)} %fusion.6.refs_1_), channel_id=1, source_target_pairs={{0,16},{1,17},{2,18},{3,19},{4,20},{5,21},{6,22},{7,23},{8,24},{9,... | collective-permute-start | bytes 98312 | tf_op jit(solution)/shard_map/ppermute | solution.py:136
  5.6 4.2 %slice-start = ((s8[4587520]{0:T(1024)(128)(4,1)}), s8[4194304]{0:T(1024)(128)(4,1)S(1)}, s32[]{:S(2)}) async-start(s8[4587520]{0:T(1024)(128)(4,1)} %bitcast.31), calls=%async_computation | async-start | bytes 8388608
  5.6 4.2 %slice-start.1 = ((s8[4587520]{0:T(1024)(128)(4,1)}), s8[393216]{0:T(1024)(128)(4,1)S(1)}, s32[]{:S(2)}) async-start(s8[4587520]{0:T(1024)(128)(4,1)} %bitcast.31), calls=%async_computation.1 | async-start | bytes 786432
  8.1 4.4 %collective-permute-start.1 = (bf16[2,16,1024]{2,1,0:T(8,128)(2,1)S(1)}, bf16[2,16,1024]{2,1,0:T(8,128)(2,1)S(1)}, u32[]{:S(2)}, u32[]{:S(2)}) collective-permute-start(bf16[2,16,1024]{2,1,0:T(8,128)(2,1)S(1)} %get-tuple-element.128.refs_2_), channel_id=1, source_target_pairs={{0,8},{1,9},{2,10},{3,11},{4,12},{5,13},{6,14},{7,15},{8,0},{9,1},... | collective-permute-start | bytes 196616 | tf_op jit(solution)/shard_map/ppermute | solution.py:136
  12.6 6.3 %collective-permute-start.8 = (bf16[2,32,896]{2,1,0:T(8,128)(2,1)S(1)}, bf16[2,32,896]{2,1,0:T(8,128)(2,1)S(1)}, u32[]{:S(2)}, u32[]{:S(2)}) collective-permute-start(bf16[2,32,896]{2,1,0:T(8,128)(2,1)S(1)} %slice.34.refs_1_), channel_id=1, source_target_pairs={{0,3},{1,2},{2,1},{3,0},{4,7},{5,6},{6,5},{7,4},{8,11},{9,10},{10,... | collective-permute-start | bytes 344072 | tf_op jit(solution)/shard_map/ppermute | solution.py:136
  15.1 2.6 %collective-permute-start.7 = (bf16[2,32,896]{2,1,0:T(8,128)(2,1)S(1)}, bf16[2,32,896]{2,1,0:T(8,128)(2,1)S(1)}, u32[]{:S(2)}, u32[]{:S(2)}) collective-permute-start(bf16[2,32,896]{2,1,0:T(8,128)(2,1)S(1)} %slice.34.refs_1_), channel_id=1, source_target_pairs={{0,4},{1,5},{2,6},{3,7},{4,0},{5,1},{6,2},{7,3},{8,12},{9,13},{10,... | collective-permute-start | bytes 344072 | tf_op jit(solution)/shard_map/ppermute | solution.py:136
  15.1 5.8 %collective-permute-start.5 = (bf16[2,32,896]{2,1,0:T(8,128)(2,1)S(1)}, bf16[2,32,896]{2,1,0:T(8,128)(2,1)S(1)}, u32[]{:S(2)}, u32[]{:S(2)}) collective-permute-start(bf16[2,32,896]{2,1,0:T(8,128)(2,1)S(1)} %slice.34.refs_1_), channel_id=1, source_target_pairs={{0,1},{1,0},{2,3},{3,2},{4,5},{5,4},{6,7},{7,6},{8,9},{9,8},{10,11... | collective-permute-start | bytes 344072 | tf_op jit(solution)/shard_map/ppermute | solution.py:136
  15.6 5.3 %collective-permute-start.2 = (bf16[2,32,896]{2,1,0:T(8,128)(2,1)S(1)}, bf16[2,32,896]{2,1,0:T(8,128)(2,1)S(1)}, u32[]{:S(2)}, u32[]{:S(2)}) collective-permute-start(bf16[2,32,896]{2,1,0:T(8,128)(2,1)S(1)} %slice.34.refs_1_), channel_id=1, source_target_pairs={{0,2},{1,3},{2,0},{3,1},{4,6},{5,7},{6,4},{7,5},{8,10},{9,11},{10,... | collective-permute-start | bytes 344072 | tf_op jit(solution)/shard_map/ppermute | solution.py:136
  16.1 1.3 %collective-permute-start.4 = (bf16[32,128]{1,0:T(8,128)(2,1)S(1)}, bf16[32,128]{1,0:T(8,128)(2,1)S(1)}, u32[]{:S(2)}, u32[]{:S(2)}) collective-permute-start(bf16[32,128]{1,0:T(8,128)(2,1)S(1)} %slice_bitcast_fusion.2.refs_3_), channel_id=1, source_target_pairs={{0,4},{1,5},{2,6},{3,7},{4,0},{5,1},{6,2},{7,3},{8,12},{9,13},{10,... | collective-permute-start | bytes 24584 | tf_op jit(solution)/shard_map/ppermute | solution.py:136
  18.9 2.4 %collective-permute-start.9 = (bf16[2,32,896]{2,1,0:T(8,128)(2,1)S(1)}, bf16[2,32,896]{2,1,0:T(8,128)(2,1)S(1)}, u32[]{:S(2)}, u32[]{:S(2)}) collective-permute-start(bf16[2,32,896]{2,1,0:T(8,128)(2,1)S(1)} %collective-permute-done.8.refs_1_), channel_id=1, source_target_pairs={{0,4},{1,5},{2,6},{3,7},{4,0},{5,1},{6,2},{7,3},{8,12},{9,13},{10,... | collective-permute-start | bytes 344072 | tf_op jit(solution)/shard_map/ppermute | solution.py:136
  20.9 1.7 %collective-permute-start.6 = (bf16[2,32,896]{2,1,0:T(8,128)(2,1)S(1)}, bf16[2,32,896]{2,1,0:T(8,128)(2,1)S(1)}, u32[]{:S(2)}, u32[]{:S(2)}) collective-permute-start(bf16[2,32,896]{2,1,0:T(8,128)(2,1)S(1)} %collective-permute-done.5.refs_1_), channel_id=1, source_target_pairs={{0,4},{1,5},{2,6},{3,7},{4,0},{5,1},{6,2},{7,3},{8,12},{9,13},{10,... | collective-permute-start | bytes 344072 | tf_op jit(solution)/shard_map/ppermute | solution.py:136
  20.9 2.9 %collective-permute-start.3 = (bf16[2,32,896]{2,1,0:T(8,128)(2,1)S(1)}, bf16[2,32,896]{2,1,0:T(8,128)(2,1)S(1)}, u32[]{:S(2)}, u32[]{:S(2)}) collective-permute-start(bf16[2,32,896]{2,1,0:T(8,128)(2,1)S(1)} %collective-permute-done.2.refs_1_), channel_id=1, source_target_pairs={{0,4},{1,5},{2,6},{3,7},{4,0},{5,1},{6,2},{7,3},{8,12},{9,13},{10,... | collective-permute-start | bytes 344072 | tf_op jit(solution)/shard_map/ppermute | solution.py:136
  25.6 1.3 %collective-permute-start.10 = (bf16[1,32,896]{2,1,0:T(8,128)(2,1)S(1)}, bf16[1,32,896]{2,1,0:T(8,128)(2,1)S(1)}, u32[]{:S(2)}, u32[]{:S(2)}) collective-permute-start(bf16[1,32,896]{2,1,0:T(8,128)(2,1)S(1)} %get-tuple-element.82), channel_id=1, source_target_pairs={{0,4},{1,5},{2,6},{3,7},{4,0},{5,1},{6,2},{7,3},{8,12},{9,13},{10,... | collective-permute-start | bytes 172040 | tf_op jit(solution)/shard_map/ppermute | solution.py:136
  26.9 2.6 %collective-permute-start.11 = (bf16[2,32,896]{2,1,0:T(8,128)(2,1)S(1)}, bf16[2,32,896]{2,1,0:T(8,128)(2,1)S(1)}, u32[]{:S(2)}, u32[]{:S(2)}) collective-permute-start(bf16[2,32,896]{2,1,0:T(8,128)(2,1)S(1)} %get-tuple-element.88), channel_id=1, source_target_pairs={{0,4},{1,5},{2,6},{3,7},{4,0},{5,1},{6,2},{7,3},{8,12},{9,13},{10,... | collective-permute-start | bytes 344072 | tf_op jit(solution)/shard_map/ppermute | solution.py:136
  27.1 7.9 %collective-permute-start.13 = (bf16[32,896]{1,0:T(8,128)(2,1)S(1)}, bf16[32,896]{1,0:T(8,128)(2,1)S(1)}, u32[]{:S(2)}, u32[]{:S(2)}) collective-permute-start(bf16[32,896]{1,0:T(8,128)(2,1)S(1)} %fusion.8), channel_id=1, source_target_pairs={{0,3},{1,2},{2,1},{3,0},{4,7},{5,6},{6,5},{7,4},{8,11},{9,10},{10,... | collective-permute-start | bytes 172040 | tf_op jit(solution)/shard_map/ppermute | solution.py:136
  29.5 5.4 %collective-permute-start.14 = (bf16[32,896]{1,0:T(8,128)(2,1)S(1)}, bf16[32,896]{1,0:T(8,128)(2,1)S(1)}, u32[]{:S(2)}, u32[]{:S(2)}) collective-permute-start(bf16[32,896]{1,0:T(8,128)(2,1)S(1)} %get-tuple-element.94), channel_id=1, source_target_pairs={{0,2},{1,3},{2,0},{3,1},{4,6},{5,7},{6,4},{7,5},{8,10},{9,11},{10,... | collective-permute-start | bytes 172040 | tf_op jit(solution)/shard_map/ppermute | solution.py:136
  30.6 4.3 %collective-permute-start.15 = (bf16[32,896]{1,0:T(8,128)(2,1)S(1)}, bf16[32,896]{1,0:T(8,128)(2,1)S(1)}, u32[]{:S(2)}, u32[]{:S(2)}) collective-permute-start(bf16[32,896]{1,0:T(8,128)(2,1)S(1)} %get-tuple-element.95), channel_id=1, source_target_pairs={{0,1},{1,0},{2,3},{3,2},{4,5},{5,4},{6,7},{7,6},{8,9},{9,8},{10,11... | collective-permute-start | bytes 172040 | tf_op jit(solution)/shard_map/ppermute | solution.py:136
  31.5 3.4 %collective-permute-start.12 = (bf16[1,32,896]{2,1,0:T(8,128)(2,1)S(1)}, bf16[1,32,896]{2,1,0:T(8,128)(2,1)S(1)}, u32[]{:S(2)}, u32[]{:S(2)}) collective-permute-start(bf16[1,32,896]{2,1,0:T(8,128)(2,1)S(1)} %get-tuple-element.91), channel_id=1, source_target_pairs={{0,4},{1,5},{2,6},{3,7},{4,0},{5,1},{6,2},{7,3},{8,12},{9,13},{10,... | collective-permute-start | bytes 172040 | tf_op jit(solution)/shard_map/ppermute | solution.py:136
  35.0 4.8 %collective-permute-start.16 = (bf16[2,8,896]{2,1,0:T(8,128)(2,1)S(1)}, bf16[2,8,896]{2,1,0:T(8,128)(2,1)S(1)}, u32[]{:S(2)}, u32[]{:S(2)}) collective-permute-start(bf16[2,8,896]{2,1,0:T(8,128)(2,1)S(1)} %slice.31), channel_id=1, source_target_pairs={{0,16},{1,17},{2,18},{3,19},{4,20},{5,21},{6,22},{7,23},{8,24},{9,... | collective-permute-start | bytes 86024 | tf_op jit(solution)/shard_map/ppermute | solution.py:136
  39.9 3.8 %collective-permute-start.17 = (bf16[1,8,896]{2,1,0:T(8,128)(2,1)S(1)}, bf16[1,8,896]{2,1,0:T(8,128)(2,1)S(1)}, u32[]{:S(2)}, u32[]{:S(2)}) collective-permute-start(bf16[1,8,896]{2,1,0:T(8,128)(2,1)S(1)} %slice.39), channel_id=1, source_target_pairs={{0,8},{1,9},{2,10},{3,11},{4,12},{5,13},{6,14},{7,15},{8,0},{9,1},... | collective-permute-start | bytes 43016 | tf_op jit(solution)/shard_map/ppermute | solution.py:136
